TPU v7x, 256 devices: a whole 4x4x8 slice. The times are simulated.
256 devices in a mesh: sp: 64 (over y, z, core), dp: 4 (over x).
Axes of the slice: x: 4, y: 4, z: 8, core: 2. Of those that a mesh axis runs over, the one named last changes fastest.
Arguments:
- volume: bfloat16 [4, 96, 256, 8, 128], P('dp', None, 'sp'), may hold values from -6 to 6
- cotangent: bfloat16 [4, 96, 256, 8, 128], P('dp', None, 'sp'), may hold values from -6 to 6
- kernels_xy: bfloat16 [2, 96, 3, 3], replicated, may hold values from -2 to 2
- kernels_z: bfloat16 [2, 96, 3], replicated, may hold values from -3.5 to 3.5
- mixing: bfloat16 [2, 96, 96], replicated, may hold values from -0.625 to 0.625
Outputs:
- volume_grad: bfloat16 [4, 96, 256, 8, 128], P('dp', None, 'sp')
- mixing_grad: float32 [2, 96, 96], replicated
- xy_grad: float32 [2, 96, 3, 3], replicated
- z_grad: float32 [2, 96, 3], replicated
All inputs are finite; a program needn't handle non-finite values.
Results may differ from a plain program's by a relative error of at most 0.018.
Values may be sent and summed in bfloat16 or wider, within the bound.
A program may use at most 64 MiB of HBM per device.

v0:
```python
import math

import jax
import jax.numpy as jnp
from jax import lax
from jax.sharding import PartitionSpec as P


def padded_2(x, sides, width):
    for axis, dim in sides:
        count, length = (lax.axis_size(axis), x.shape[dim])
        up = [(i, (i + 1) % count) for i in range(count - 1)]
        down = [(j, i) for i, j in up]
        last = lax.slice_in_dim(x, length - width, length, axis=dim)
        first = lax.slice_in_dim(x, 0, width, axis=dim)
        before = lax.ppermute(last, axis, up)
        after = lax.ppermute(first, axis, down)
        x = jnp.concatenate([before, x, after], axis=dim)
    return x


def conv_plane(inputs, kernel):
    extent = inputs.shape[1] - 2
    across = inputs.shape[3]
    padded = jnp.pad(inputs, ((0, 0), (0, 0), (0, 0), (1, 1)))
    summed = jnp.zeros((inputs.shape[0], extent, inputs.shape[2], across), jnp.float32)
    for row_tap in range(3):
        for col_tap in range(3):
            summed = summed + kernel[:, row_tap, col_tap][:, None, None, None] * padded[
                :, row_tap : row_tap + extent, :, col_tap : col_tap + across
            ].astype(jnp.float32)
    return summed


def conv_depth(inputs, kernel):
    depth_len = inputs.shape[2]
    padded = jnp.pad(inputs, ((0, 0), (0, 0), (1, 1), (0, 0)))
    summed = jnp.zeros(inputs.shape, jnp.float32)
    for depth_tap in range(3):
        summed = (
            summed
            + kernel[:, depth_tap][:, None, None, None]
            * padded[:, :, depth_tap : depth_tap + depth_len, :]
        )
    return summed


def mix_channels(weights, inputs):
    channels = inputs.shape[0]
    flat = inputs.reshape(channels, -1)
    return jnp.dot(weights, flat, preferred_element_type=jnp.float32).reshape(inputs.shape)


def forward_block(inputs, kernel_xy, kernel_z, weights):
    planar = conv_plane(inputs, kernel_xy)
    axial = conv_depth(planar, kernel_z).astype(jnp.bfloat16)
    preact = mix_channels(weights, axial)
    return (planar, axial, preact)


def silu_slope(preact):
    sigma = jax.nn.sigmoid(preact)
    return sigma * (1.0 + preact * (1.0 - sigma))


def backward_block(grad_out, planar, axial, preact, around, kernel_z, weights, trim):
    grad_pre = (grad_out.astype(jnp.float32) * silu_slope(preact)).astype(jnp.bfloat16)
    channels = grad_pre.shape[0]
    grad_axial = jnp.dot(
        weights.T, grad_pre.reshape(channels, -1), preferred_element_type=jnp.float32
    ).reshape(grad_pre.shape)
    grad_planar = conv_depth(grad_axial, kernel_z[:, ::-1]).astype(jnp.bfloat16)
    extent = grad_pre.shape[1]
    own_extent = extent - 2 * trim
    own_pre = grad_pre.reshape(channels, -1)
    own_axial = axial.reshape(channels, -1)
    grad_weights = lax.dot_general(
        own_pre, own_axial, (((1,), (1,)), ((), ())), preferred_element_type=jnp.float32
    )
    depth_len = planar.shape[2]
    planar_pad = jnp.pad(planar, ((0, 0), (0, 0), (1, 1), (0, 0)))
    grad_kz = jnp.stack(
        [
            jnp.sum(
                grad_axial * planar_pad[:, :, depth_tap : depth_tap + depth_len, :], axis=(1, 2, 3)
            )
            for depth_tap in range(3)
        ],
        axis=1,
    )
    own_grad_planar = grad_planar.astype(jnp.float32)
    across = around.shape[3]
    around_pad = jnp.pad(around, ((0, 0), (0, 0), (0, 0), (1, 1)))
    rows_list = []
    for row_tap in range(3):
        cols_list = []
        for col_tap in range(3):
            cols_list.append(
                jnp.sum(
                    own_grad_planar
                    * around_pad[
                        :, row_tap : row_tap + own_extent, :, col_tap : col_tap + across
                    ].astype(jnp.float32),
                    axis=(1, 2, 3),
                )
            )
        rows_list.append(jnp.stack(cols_list, axis=1))
    grad_kxy = jnp.stack(rows_list, axis=1)
    return (grad_planar, (grad_weights, grad_kxy, grad_kz))


def edge_grads(grad_planar):
    return padded_2(grad_planar, (("sp", 1),), 1)


def settle_all(lower, upper):
    summed = lax.psum((lower[0], lower[1], lower[2], upper[0], upper[1], upper[2]), ("sp", "dp"))
    return ((summed[0], summed[1], summed[2]), (summed[3], summed[4], summed[5]))


def on_device(volume, cotangent, kernels_xy, kernels_z, mixing):
    inputs = volume[0]
    grad_top = cotangent[0]
    kernel_xy = kernels_xy.astype(jnp.float32)
    kernel_z = kernels_z.astype(jnp.float32)
    slab_len = inputs.shape[1]
    ranks = lax.axis_size("sp")
    place = lax.axis_index("sp")
    wide = padded_2(inputs, (("sp", 1),), 2)
    planar1, axial1, preact1 = forward_block(wide, kernel_xy[0], kernel_z[0], mixing[0])
    hidden = jax.nn.silu(preact1).astype(jnp.bfloat16)
    spots = place * slab_len - 1 + jnp.arange(slab_len + 2, dtype=jnp.int32)
    hidden = jnp.where(
        ((spots >= 0) & (spots < slab_len * ranks))[None, :, None, None],
        hidden,
        jnp.zeros_like(hidden),
    )
    planar2, axial2, preact2 = forward_block(hidden, kernel_xy[1], kernel_z[1], mixing[1])
    grad_planar2, upper = backward_block(
        grad_top, planar2, axial2, preact2, hidden, kernel_z[1], mixing[1], 0
    )
    grad_hidden = conv_plane(edge_grads(grad_planar2), kernel_xy[1][:, ::-1, ::-1]).astype(
        jnp.bfloat16
    )
    grad_planar1, lower = backward_block(
        grad_hidden,
        planar1[:, 1:-1],
        axial1[:, 1:-1],
        preact1[:, 1:-1],
        wide[:, 1:-1],
        kernel_z[0],
        mixing[0],
        0,
    )
    grad_inputs = conv_plane(edge_grads(grad_planar1), kernel_xy[0][:, ::-1, ::-1]).astype(
        jnp.bfloat16
    )
    lower, upper = settle_all(lower, upper)
    factor = 1.0 / math.sqrt(
        lax.axis_size("dp") * slab_len * ranks * inputs.shape[2] * inputs.shape[3]
    )
    mixing_grad = jnp.stack([lower[0], upper[0]]) * factor
    xy_grad = jnp.stack([lower[1], upper[1]]) * factor
    z_grad = jnp.stack([lower[2], upper[2]]) * factor
    return (grad_inputs[None], mixing_grad, xy_grad, z_grad)


def solution(mesh):
    return jax.shard_map(
        on_device,
        mesh=mesh,
        in_specs=(P("dp", None, "sp", None, None), P("dp", None, "sp", None, None), P(), P(), P()),
        out_specs=(P("dp", None, "sp", None, None), P(), P(), P()),
        check_vma=False,
    )
```

profile of v0, /device:TPU:1, one launch (start us, length us, event | category | flops | bytes accessed | tf_op | source)
XLA Modules:
  0.0 328.5 jit_solution(12075035630448840751)
XLA Ops:
  7.2 1.5 copy.76
  8.8 4.9 %collective-permute-start = (bf16[96,2,8,128]{3,0,2,1:T(8,128)(2,1)S(1)}, bf16[96,2,8,128]{3,0,2,1:T(8,128)(2,1)S(1)}, u32[]{:S(2)}, u32[]{:S(2)}) collective-permute-start(bf16[96,2,8,128]{3,0,2,1:T(8,128)(2,1)S(1)} %get-tuple-element.61), channel_id=1, source_target_pairs={{0,4},{4,8},{8,12},{12,16},{16,20},{20,24},{24,28},{28,32},{32,36}... | collective-permute-start | bytes 1179656 | tf_op jit(solution)/shard_map/ppermute | solution.py:16
  13.8 1.9 collective-permute-start.1
  15.8 1.5 reshape.101
  18.5 4.4 %collective-permute-done.1 = bf16[96,2,8,128]{3,0,2,1:T(8,128)(2,1)S(1)} collective-permute-done((bf16[96,2,8,128]{3,0,2,1:T(8,128)(2,1)S(1)}, bf16[96,2,8,128]{3,0,2,1:T(8,128)(2,1)S(1)}, u32[]{:S(2)}, u32[]{:S(2)}) %collective-permute-start.1) | collective-permute-done | bytes 393248 | tf_op jit(solution)/shard_map/ppermute | solution.py:17
  23.0 3.1 multiply_add_fusion
  26.1 1.4 copy-done
  30.4 3.0 fusion.24
  36.5 6.6 %multiply_reduce_fusion.2 = (f32[96]{0:T(128)S(1)}, f32[96]{0:T(128)S(1)}, f32[96]{0:T(128)S(1)}, f32[96]{0:T(128)S(1)}, f32[96]{0:T(128)S(1)}, /*index=5*/f32[9...) fusion(f32[96,4,8,128]{3,2,1,0:T(8,128)S(1)} %bitcast.196, ...), kind=kLoop, calls=%fused_computation.147 | loop fusion | flops 15727488 | bytes 7477248 | tf_op jit(solution)/shard_map/reduce_sum | solution.py:84
  43.1 1.9 collective-permute-start.2
  45.1 2.6 collective-permute-start.3
  49.8 1.2 convolution_bitcast_fusion.3
  51.0 1.4 collective-permute-done.3
  52.3 1.5 fusion.9
  53.9 3.5 %multiply_convert_fusion.1 = bf16[96,4,8,128]{3,2,1,0:T(8,128)(2,1)S(1)} fusion(f32[96,6,8,128]{3,2,1,0:T(8,128)S(1)} %bitcast.193, bf16[96,6,8,130]{3,2,1,0:T(8,128)(2,1)S(1)} %fusion.9, f32[96]{0:T(128)S(1)} %get-tuple-element.71, bf16[96,1,8,128]{3,2,1,0:T(8,128)(2,1)S(1)} %collective-permute-done.3, bf16[96,4,8,128]{3,2,1,0:T(8,128)(2,1)S(1)} %get-tuple-element.56, ...), kind=kLoop, calls=%fused_computation.149 | loop fusion | flops 15335424 | bytes 8260992 | tf_op jit(solution)/shard_map/convert_element_type | solution.py:67
  60.7 1.4 fusion.31
  62.7 2.8 fusion.60
  66.2 2.1 collective-permute-start.4
  68.3 2.3 collective-permute-start.5
  70.6 242.2 %all-reduce.13.cloned.1.call-done = (f32[1,96,96]{2,1,0:T(8,128)}, f32[1,96,96]{2,1,0:T(8,128)}, f32[1,96,3,3]{1,3,2,0:T(4,128)}, f32[1,96,3,3]{1,3,2,0:T(4,128)...) async-done(((f32[1,96,96]{2,1,0:T(8,128)}, f32[1,96,96]{2,1,0:T(8,128)}, f32[1,96,3,3]{1,3,2,0:T(4,128)}, f32[1,96,3,3]{1,3,2,0:T(4,128)}, f32[1,96,3]{1,2,0:T(4,128)}, ...) | async-done | bytes 82960 | tf_op jit(solution)/shard_map/psum | solution.py:117
  315.4 1.5 maximum_multiply_fusion
  316.9 1.6 fusion.11
  318.4 2.0 fusion.92
  320.4 1.2 copy.31
  (68 shorter events, 16.6 us)
Async XLA Ops:
  7.2 8.5 %copy-start.7 = (bf16[2,96,3,3]{1,0,3,2:T(2,128)(2,1)S(1)}, bf16[2,96,3,3]{1,0,3,2:T(2,128)(2,1)}, u32[]{:S(2)}) copy-start(bf16[2,96,3,3]{1,0,3,2:T(2,128)(2,1)} %param.7) | copy-start | bytes 10372
  7.2 8.6 %copy-start.8 = (bf16[2,96,3]{1,0,2:T(2,128)(2,1)S(1)}, bf16[2,96,3]{1,0,2:T(2,128)(2,1)}, u32[]{:S(2)}) copy-start(bf16[2,96,3]{1,0,2:T(2,128)(2,1)} %param.8) | copy-start | bytes 3460
  7.2 8.6 %copy-start.4 = (bf16[1,96,4,8,128]{4,3,2,1,0:T(8,128)(2,1)S(1)}, bf16[1,96,4,8,128]{4,3,2,1,0:T(8,128)(2,1)}, u32[]{:S(2)}) copy-start(bf16[1,96,4,8,128]{4,3,2,1,0:T(8,128)(2,1)} %param.6) | copy-start | bytes 2359300
  7.2 305.6 %all-reduce.13.cloned.1.call-start = ((), (), s32[]{:S(2)}) async-start(), calls=%async_computation | async-start | bytes 229376 | tf_op jit(solution)/shard_map/psum | solution.py:117
  8.8 9.6 %collective-permute-start = (bf16[96,2,8,128]{3,0,2,1:T(8,128)(2,1)S(1)}, bf16[96,2,8,128]{3,0,2,1:T(8,128)(2,1)S(1)}, u32[]{:S(2)}, u32[]{:S(2)}) collective-permute-start(bf16[96,2,8,128]{3,0,2,1:T(8,128)(2,1)S(1)} %get-tuple-element.61), channel_id=1, source_target_pairs={{0,4},{4,8},{8,12},{12,16},{16,20},{20,24},{24,28},{28,32},{32,36}... | collective-permute-start | bytes 1179656 | tf_op jit(solution)/shard_map/ppermute | solution.py:16
  13.8 9.1 %collective-permute-start.1 = (bf16[96,2,8,128]{3,0,2,1:T(8,128)(2,1)S(1)}, bf16[96,2,8,128]{3,0,2,1:T(8,128)(2,1)S(1)}, u32[]{:S(2)}, u32[]{:S(2)}) collective-permute-start(bf16[96,2,8,128]{3,0,2,1:T(8,128)(2,1)S(1)} %get-tuple-element.62), channel_id=1, source_target_pairs={{4,0},{8,4},{12,8},{16,12},{20,16},{24,20},{28,24},{32,28},{36,32}... | collective-permute-start | bytes 1179656 | tf_op jit(solution)/shard_map/ppermute | solution.py:17
  23.0 3.1 copy-start.2
  26.1 1.4 copy-start
  28.1 0.8 copy-start.6
  34.0 1.4 copy-start.5
  43.1 7.8 %collective-permute-start.2 = (bf16[96,1,8,128]{3,2,1,0:T(8,128)(2,1)S(1)}, bf16[96,1,8,128]{3,2,1,0:T(8,128)(2,1)S(1)}, u32[]{:S(2)}, u32[]{:S(2)}) collective-permute-start(bf16[96,1,8,128]{3,2,1,0:T(8,128)(2,1)S(1)} %get-tuple-element.59), channel_id=1, source_target_pairs={{0,4},{4,8},{8,12},{12,16},{16,20},{20,24},{24,28},{28,32},{32,36}... | collective-permute-start | bytes 589832 | tf_op jit(solution)/shard_map/ppermute | solution.py:16
  45.1 7.3 %collective-permute-start.3 = (bf16[96,1,8,128]{3,2,1,0:T(8,128)(2,1)S(1)}, bf16[96,1,8,128]{3,2,1,0:T(8,128)(2,1)S(1)}, u32[]{:S(2)}, u32[]{:S(2)}) collective-permute-start(bf16[96,1,8,128]{3,2,1,0:T(8,128)(2,1)S(1)} %get-tuple-element.60), channel_id=1, source_target_pairs={{4,0},{8,4},{12,8},{16,12},{20,16},{24,20},{28,24},{32,28},{36,32}... | collective-permute-start | bytes 589832 | tf_op jit(solution)/shard_map/ppermute | solution.py:17
  58.5 1.7 copy-start.1
  58.9 1.8 slice-start
  60.7 2.0 slice-start.1
  60.7 2.0 copy-start.3
  66.2 250.6 %collective-permute-start.4 = (bf16[96,1,8,128]{3,0,2,1:T(8,128)(2,1)S(1)}, bf16[96,1,8,128]{3,0,2,1:T(8,128)(2,1)S(1)}, u32[]{:S(2)}, u32[]{:S(2)}) collective-permute-start(bf16[96,1,8,128]{3,0,2,1:T(8,128)(2,1)S(1)} %get-tuple-element.57), channel_id=1, source_target_pairs={{0,4},{4,8},{8,12},{12,16},{16,20},{20,24},{24,28},{28,32},{32,36}... | collective-permute-start | bytes 589832 | tf_op jit(solution)/shard_map/ppermute | solution.py:16
  68.3 248.6 %collective-permute-start.5 = (bf16[96,1,8,128]{3,0,2,1:T(8,128)(2,1)S(1)}, bf16[96,1,8,128]{3,0,2,1:T(8,128)(2,1)S(1)}, u32[]{:S(2)}, u32[]{:S(2)}) collective-permute-start(bf16[96,1,8,128]{3,0,2,1:T(8,128)(2,1)S(1)} %get-tuple-element.58), channel_id=1, source_target_pairs={{4,0},{8,4},{12,8},{16,12},{20,16},{24,20},{28,24},{32,28},{36,32}... | collective-permute-start | bytes 589832 | tf_op jit(solution)/shard_map/ppermute | solution.py:17
Sparse Core Ops, SparseCore 0:
  66.3 246.4 all-reduce.12
where the time goes:
time: 329 us; the launch traced here: 328 us
  waiting for transfers between devices  249 us (76%)
  other arithmetic  33.4 us (10%)
  starting transfers between devices  15.7 us (5%)
  between operations  14.4 us (4%)
  local copies, waits for them, and re-layouts  11.5 us (3%)
  matrix products  4.28 us (1%)
    psum x1, waiting for transfers between devices, settle_all(): lax.psum((lower[0], lower[1], lower[2], upper[0], upper[1], upper[2]), ('...  242 us
    ppermute x3, starting transfers between devices, padded_2(): before = lax.ppermute(last, axis, up)  8.92 us
    unnamed x28, local copies, waits for them, and re-layouts  8.82 us
    reduce_sum x2, other arithmetic, backward_block(): jnp.sum(grad_axial * planar_pad[:, :, depth_tap:depth_tap + depth_len, :]...  7.96 us
    ppermute x3, starting transfers between devices, padded_2(): after = lax.ppermute(first, axis, down)  6.79 us
  transfers between devices with their start and end apart: 7, of which 4 were waited for; matrix products, arithmetic and copies ran while one was open for 3% of the time, Pallas kernels for 0%

commit v1 on v0

--- a/solution.py
+++ b/solution.py
@@ -1,9 +1,14 @@
+import functools
 import math
 
 import jax
 import jax.numpy as jnp
 from jax import lax
+from jax.experimental import pallas as pl
+from jax.experimental.pallas import tpu as pltpu
 from jax.sharding import PartitionSpec as P
+
+MESH = pl.DeviceIdType.MESH
 
 
 def padded_2(x, sides, width):
@@ -113,8 +118,73 @@
     return padded_2(grad_planar, (("sp", 1),), 1)
 
 
+def exchange_bits(axes):
+    bits = []
+    for name, size in axes:
+        assert size & (size - 1) == 0
+        for b in range(size.bit_length() - 1):
+            bits.append((name, 1 << b))
+    return bits
+
+
+def allreduce_kernel(axes, x_ref, o_ref, recv, acc, send_sem, recv_sem):
+    bits = exchange_bits(axes)
+    here = {name: lax.axis_index(name) for name, _ in axes}
+    partners = []
+    for name, stride in bits:
+        bit = (here[name] // stride) % 2
+        where = dict(here)
+        where[name] = here[name] + stride * (1 - 2 * bit)
+        partners.append(tuple(where[n] for n, _ in axes))
+    barrier = pltpu.get_barrier_semaphore()
+    for partner in partners:
+        pl.semaphore_signal(barrier, inc=1, device_id=partner, device_id_type=MESH)
+    pl.semaphore_wait(barrier, len(partners))
+    src = x_ref
+    for k, partner in enumerate(partners):
+        copy = pltpu.make_async_remote_copy(
+            src_ref=src,
+            dst_ref=recv.at[k],
+            send_sem=send_sem.at[k],
+            recv_sem=recv_sem.at[k],
+            device_id=partner,
+            device_id_type=MESH,
+        )
+        copy.start()
+        copy.wait()
+        dst = o_ref if k == len(partners) - 1 else acc.at[k]
+        dst[...] = src[...] + recv[k]
+        src = dst
+
+
+def all_sum(flat, axes):
+    steps = len(exchange_bits(axes))
+    return pl.pallas_call(
+        functools.partial(allreduce_kernel, axes),
+        out_shape=jax.ShapeDtypeStruct(flat.shape, flat.dtype),
+        in_specs=[pl.BlockSpec(memory_space=pltpu.VMEM)],
+        out_specs=pl.BlockSpec(memory_space=pltpu.VMEM),
+        scratch_shapes=[
+            pltpu.VMEM((steps,) + flat.shape, flat.dtype),
+            pltpu.VMEM((steps,) + flat.shape, flat.dtype),
+            pltpu.SemaphoreType.DMA((steps,)),
+            pltpu.SemaphoreType.DMA((steps,)),
+        ],
+        compiler_params=pltpu.CompilerParams(collective_id=0, has_side_effects=True),
+    )(flat)
+
+
 def settle_all(lower, upper):
-    summed = lax.psum((lower[0], lower[1], lower[2], upper[0], upper[1], upper[2]), ("sp", "dp"))
+    parts = (lower[0], lower[1], lower[2], upper[0], upper[1], upper[2])
+    flat = jnp.concatenate([p.reshape(-1) for p in parts])
+    rows = -(-flat.shape[0] // 1024) * 8
+    flat = jnp.pad(flat, (0, rows * 128 - flat.shape[0])).reshape(rows, 128)
+    axes = (("sp", lax.axis_size("sp")), ("dp", lax.axis_size("dp")))
+    flat = all_sum(flat, axes).reshape(-1)
+    summed, at = [], 0
+    for p in parts:
+        summed.append(flat[at : at + p.size].reshape(p.shape))
+        at += p.size
     return ((summed[0], summed[1], summed[2]), (summed[3], summed[4], summed[5]))
 
 

time: 329 us -> 144 us (0.44)
  the two profiles are of different devices: /device:TPU:1 before, /device:TPU:8 now
where the time goes in v1:
time: 144 us; the launch traced here: 143 us
  Pallas kernels  40.5 us (28%)
  other arithmetic  39.4 us (27%)
  local copies, waits for them, and re-layouts  29.3 us (20%)
  starting transfers between devices  24.7 us (17%)
  matrix products  4.25 us (3%)
  waiting for transfers between devices  3.2 us (2%)
  between operations  1.62 us (1%)
    pallas_call x1, Pallas kernels, all_sum(): pl.pallas_call(functools.partial(allreduce_kernel, axes), out_shape=jax.S...  40.5 us
    ppermute x3, starting transfers between devices, padded_2(): after = lax.ppermute(first, axis, down)  19 us
    unnamed x120, local copies, waits for them, and re-layouts  11.9 us
    reduce_sum x2, other arithmetic, backward_block(): jnp.sum(grad_axial * planar_pad[:, :, depth_tap:depth_tap + depth_len, :]...  10.1 us
    add x2, other arithmetic, conv_plane(): summed + kernel[:, row_tap, col_tap][:, None, None, None] * padded[:, row...  6.97 us
    ppermute x3, starting transfers between devices, padded_2(): before = lax.ppermute(last, axis, up)  5.75 us
    convert_element_type x2, other arithmetic, backward_block(): (grad_out.astype(jnp.float32) * silu_slope(preact)).astype(jnp.bfloat16)  5.05 us
    reshape x6, local copies, waits for them, and re-layouts, settle_all(): flat = jnp.concatenate([p.reshape(-1) for p in parts])  4.86 us
  transfers between devices with their start and end apart: 6, of which 3 were waited for; matrix products, arithmetic and copies ran while one was open for 7% of the time, Pallas kernels for 0%

profile of v1, /device:TPU:8, one launch (start us, length us, event | category | flops | bytes accessed | tf_op | source)
XLA Modules:
  0.0 142.9 jit_solution(860600397457316954)
XLA Ops:
  0.7 1.5 %copy.97 = bf16[1,96,4,8,128]{4,1,3,2,0:T(8,128)(2,1)S(1)} copy(bf16[1,96,4,8,128]{4,3,2,1,0:T(8,128)(2,1)} %param.5) | data formatting | bytes 1572864 | tf_op args[0]
  2.2 1.9 %collective-permute-start = (bf16[96,2,8,128]{3,0,2,1:T(8,128)(2,1)S(1)}, bf16[96,2,8,128]{3,0,2,1:T(8,128)(2,1)S(1)}, u32[]{:S(2)}, u32[]{:S(2)}) collective-permute-start(bf16[96,2,8,128]{3,0,2,1:T(8,128)(2,1)S(1)} %get-tuple-element.59), channel_id=1, source_target_pairs={{0,4},{4,8},{8,12},{12,16},{16,20},{20,24},{24,28},{28,32},{32,36}... | collective-permute-start | bytes 1179656 | tf_op jit(solution)/shard_map/ppermute | solution.py:21
  4.2 7.1 %collective-permute-start.1 = (bf16[96,2,8,128]{3,0,2,1:T(8,128)(2,1)S(1)}, bf16[96,2,8,128]{3,0,2,1:T(8,128)(2,1)S(1)}, u32[]{:S(2)}, u32[]{:S(2)}) collective-permute-start(bf16[96,2,8,128]{3,0,2,1:T(8,128)(2,1)S(1)} %get-tuple-element.60), channel_id=1, source_target_pairs={{4,0},{8,4},{12,8},{16,12},{20,16},{24,20},{28,24},{32,28},{36,32}... | collective-permute-start | bytes 1179656 | tf_op jit(solution)/shard_map/ppermute | solution.py:22
  13.0 1.5 %reshape.137 = f32[96,4096]{1,0:T(8,128)} reshape(bf16[1,96,4,8,128]{4,3,2,1,0:T(8,128)(2,1)S(1)} %copy-done.9) | data formatting | bytes 2359296 | tf_op jit(solution)/shard_map/convert_element_type | solution.py:72
  14.8 1.8 %collective-permute-done.1 = bf16[96,2,8,128]{3,0,2,1:T(8,128)(2,1)S(1)} collective-permute-done((bf16[96,2,8,128]{3,0,2,1:T(8,128)(2,1)S(1)}, bf16[96,2,8,128]{3,0,2,1:T(8,128)(2,1)S(1)}, u32[]{:S(2)}, u32[]{:S(2)}) %collective-permute-start.1) | collective-permute-done | bytes 393248 | tf_op jit(solution)/shard_map/ppermute | solution.py:22
  18.0 4.0 %multiply_add_fusion = f32[96,6,8,128]{3,0,2,1:T(8,128)S(1)} fusion(bf16[96,2,8,128]{3,0,2,1:T(8,128)(2,1)} %copy-done.7, bf16[96,4,8,128]{3,0,2,1:T(8,128)(2,1)S(1)} %bitcast.181, bf16[96,2,8,128]{3,0,2,1:T(8,128)(2,1)S(1)} %collective-permute-done, bf16[96,8,8,128]{3,0,2,1:T(8,128)(2,1)S(1)} %pad_maximum_fusion, f32[96]{0:T(128)S(1)} %copy-done.32, ...), kind=kLoop, calls=%fused_computation.66 | loop fusion | flops 18874368 | bytes 6689280 | tf_op jit(solution)/shard_map/add | solution.py:34
  22.0 1.4 copy-done
  26.6 3.0 %fusion.24 = f32[96,4,8,128]{3,2,1,0:T(8,128)S(1)} fusion(f32[96]{0:T(128)S(1)} %get-tuple-element.68, f32[96]{0:T(128)S(1)} %get-tuple-element.69, f32[96]{0:T(128)S(1)} %get-tuple-element.70, f32[96]{0:T(128)S(1)} %get-tuple-element.71, f32[96]{0:T(128)S(1)} %get-tuple-element.72, f32[96]{0:T(128)S(1)} %get-tuple-element.73, f32[96]{0:T(128)S(1)} %get-tuple-element.74, ...), kind=kLoop, calls=%fused_computation.88 | loop fusion | flops 10223616 | bytes 5116416 | tf_op jit(solution)/shard_map/add | solution.py:34
  30.7 1.3 copy-done.13
  33.4 7.8 %multiply_reduce_fusion.2 = (f32[96]{0:T(128)S(1)}, f32[96]{0:T(128)S(1)}, f32[96]{0:T(128)S(1)}, f32[96]{0:T(128)}, f32[96]{0:T(128)S(1)}, /*index=5*/f32[96]{0...) fusion(f32[96,4,8,128]{3,2,1,0:T(8,128)S(1)} %bitcast.187, ...), kind=kLoop, calls=%fused_computation.147 | loop fusion | flops 15727488 | bytes 7477248 | tf_op jit(solution)/shard_map/reduce_sum | solution.py:89
  46.9 1.9 %fusion.105 = (bf16[96,1,8,128]{3,2,1,0:T(8,128)(2,1)}, bf16[96,1,8,128]{3,2,1,0:T(8,128)(2,1)}) fusion(bf16[96,4,8,128]{3,2,1,0:T(8,128)(2,1)} %get-tuple-element.53), kind=kLoop, calls=%fused_computation.234 | loop fusion | bytes 786432 | tf_op jit(solution)/shard_map/slice | solution.py:19
  48.7 1.9 %collective-permute-start.2 = (bf16[96,1,8,128]{3,2,1,0:T(8,128)(2,1)}, bf16[96,1,8,128]{3,2,1,0:T(8,128)(2,1)}, u32[]{:S(2)}, u32[]{:S(2)}) collective-permute-start(bf16[96,1,8,128]{3,2,1,0:T(8,128)(2,1)} %get-tuple-element.57), channel_id=1, source_target_pairs={{0,4},{4,8},{8,12},{12,16},{16,20},{20,24},{24,28},{28,32},{32,36}... | collective-permute-start | bytes 589832 | tf_op jit(solution)/shard_map/ppermute | solution.py:21
  50.6 6.1 %collective-permute-start.3 = (bf16[96,1,8,128]{3,2,1,0:T(8,128)(2,1)}, bf16[96,1,8,128]{3,2,1,0:T(8,128)(2,1)}, u32[]{:S(2)}, u32[]{:S(2)}) collective-permute-start(bf16[96,1,8,128]{3,2,1,0:T(8,128)(2,1)} %get-tuple-element.58), channel_id=1, source_target_pairs={{4,0},{8,4},{12,8},{16,12},{20,16},{24,20},{28,24},{32,28},{36,32}... | collective-permute-start | bytes 589832 | tf_op jit(solution)/shard_map/ppermute | solution.py:22
  56.8 1.8 %copy.67 = f32[12,8,32,128]{3,2,1,0:T(8,128)S(1)} copy(f32[12,8,32,128]{3,1,2,0:T(8,128)} %bitcast.185) | data formatting | bytes 3145728
  60.8 1.5 %reshape.132 = f32[9216]{0:T(1024)} reshape(f32[96,96]{1,0:T(8,128)} %convolution_bitcast_fusion.3) | data formatting | bytes 73728 | tf_op jit(solution)/shard_map/reshape | solution.py:179
  62.4 2.7 %fusion.9 = bf16[96,6,8,130]{3,2,1,0:T(8,128)(2,1)S(1)} fusion(bf16[96,1,8,128]{3,2,1,0:T(8,128)(2,1)} %collective-permute-done.3, bf16[96,4,8,128]{3,2,1,0:T(8,128)(2,1)} %get-tuple-element.53, bf16[96,1,8,128]{3,2,1,0:T(8,128)(2,1)} %collective-permute-done.2), kind=kLoop, calls=%fused_computation.57 | loop fusion | flops 7188480 | bytes 2377728 | tf_op jit(solution)/shard_map/concatenate | solution.py:23
  65.2 4.5 %multiply_convert_fusion.1 = bf16[96,4,8,128]{3,2,1,0:T(8,128)(2,1)S(1)} fusion(f32[96,6,8,128]{3,2,1,0:T(8,128)S(1)} %bitcast.184, bf16[96,6,8,130]{3,2,1,0:T(8,128)(2,1)S(1)} %fusion.9, f32[96]{0:T(128)S(1)} %copy-done.54, bf16[96,1,8,128]{3,2,1,0:T(8,128)(2,1)} %collective-permute-done.3, bf16[96,4,8,128]{3,2,1,0:T(8,128)(2,1)S(1)} %copy-done.3, ...), kind=kLoop, calls=%fused_computation.149 | loop fusion | flops 15335424 | bytes 8260992 | tf_op jit(solution)/shard_map/convert_element_type | solution.py:72
  72.9 2.3 %fusion.31 = (f32[96]{0:T(128)S(1)}, f32[96]{0:T(128)S(1)}, f32[96]{0:T(128)S(1)}, f32[96,4,8,128]{3,0,2,1:T(8,128)}) fusion(f32[96,4,8,128]{3,0,2,1:T(8,128)S(1)} %slice-done, f32[96,4,8,128]{3,2,1,0:T(8,128)S(1)} %bitcast.188, f32[96,6,8,128]{3,0,2,1:T(8,128)S(1)} %copy-done.1), kind=kLoop, calls=%fused_computation.95 | loop fusion | flops 2359008 | bytes 6292608 | tf_op jit(solution)/shard_map/reduce_sum | solution.py:89
  75.6 4.6 %fusion.60 = (f32[96]{0:T(128)S(1)}, f32[96]{0:T(128)S(1)}, f32[96]{0:T(128)S(1)}, f32[96]{0:T(128)S(1)}, f32[96]{0:T(128)S(1)}, /*index=5*/f32[96]{0:T(128)S(1)...) fusion(bf16[96,6,8,128]{3,0,2,1:T(8,128)(2,1)S(1)} %slice-done.1, ...), kind=kLoop, calls=%fused_computation.124 | loop fusion | flops 15727776 | bytes 5902848 | tf_op jit(solution)/shard_map/reduce_sum | solution.py:104
  83.0 40.5 %shard_map.84 = f32[168,128]{1,0:T(8,128)} custom-call(f32[168,128]{1,0:T(8,128)} %pad_bitcast_fusion.x_ref), custom_call_target="tpu_custom_call" | custom-call | tf_op jit(solution)/shard_map/pallas_call | solution.py:162
  127.2 1.9 %collective-permute-start.4 = (bf16[96,1,8,128]{3,0,2,1:T(8,128)(2,1)S(1)}, bf16[96,1,8,128]{3,0,2,1:T(8,128)(2,1)S(1)}, u32[]{:S(2)}, u32[]{:S(2)}) collective-permute-start(bf16[96,1,8,128]{3,0,2,1:T(8,128)(2,1)S(1)} %get-tuple-element.55), channel_id=1, source_target_pairs={{0,4},{4,8},{8,12},{12,16},{16,20},{20,24},{24,28},{28,32},{32,36}... | collective-permute-start | bytes 589832 | tf_op jit(solution)/shard_map/ppermute | solution.py:21
  129.1 5.8 %collective-permute-start.5 = (bf16[96,1,8,128]{3,0,2,1:T(8,128)(2,1)S(1)}, bf16[96,1,8,128]{3,0,2,1:T(8,128)(2,1)S(1)}, u32[]{:S(2)}, u32[]{:S(2)}) collective-permute-start(bf16[96,1,8,128]{3,0,2,1:T(8,128)(2,1)S(1)} %get-tuple-element.56), channel_id=1, source_target_pairs={{4,0},{8,4},{12,8},{16,12},{20,16},{24,20},{28,24},{32,28},{36,32}... | collective-permute-start | bytes 589832 | tf_op jit(solution)/shard_map/ppermute | solution.py:22
  138.1 1.6 %fusion.11 = bf16[96,6,8,130]{3,0,2,1:T(8,128)(2,1)S(1)} fusion(bf16[96,1,8,128]{3,0,2,1:T(8,128)(2,1)S(1)} %collective-permute-done.5, bf16[96,4,8,128]{3,0,2,1:T(8,128)(2,1)S(1)} %get-tuple-element.43, bf16[96,1,8,128]{3,0,2,1:T(8,128)(2,1)S(1)} %collective-permute-done.4), kind=kLoop, calls=%fused_computation.59 | loop fusion | flops 7188480 | bytes 2377728 | tf_op jit(solution)/shard_map/concatenate | solution.py:23
  139.7 2.0 %fusion.92 = bf16[1,96,4,8,128]{4,1,3,2,0:T(8,128)(2,1)S(1)} fusion(bf16[96,6,8,130]{3,0,2,1:T(8,128)(2,1)S(1)} %fusion.11, f32[96]{0:T(128)S(1)} %get-tuple-element.76, bf16[96,1,8,128]{3,0,2,1:T(8,128)(2,1)S(1)} %collective-permute-done.5, bf16[96,4,8,128]{3,0,2,1:T(8,128)(2,1)S(1)} %get-tuple-element.43, f32[96]{0:T(128)S(1)} %copy-done.31, ...), kind=kLoop, calls=%fused_computation.180 | loop fusion | flops 11403264 | bytes 6688128 | tf_op jit(solution)/shard_map/broadcast_in_dim | solution.py:235
  (183 shorter events, 31.3 us)
Async XLA Ops:
  0.6 10.6 %copy-start.16 = (bf16[2,96,3,3]{1,0,3,2:T(2,128)(2,1)S(1)}, bf16[2,96,3,3]{1,0,3,2:T(2,128)(2,1)}, u32[]{:S(2)}) copy-start(bf16[2,96,3,3]{1,0,3,2:T(2,128)(2,1)} %param.7) | copy-start | bytes 10372
  0.6 11.3 %copy-start.17 = (bf16[2,96,3]{1,0,2:T(2,128)(2,1)S(1)}, bf16[2,96,3]{1,0,2:T(2,128)(2,1)}, u32[]{:S(2)}) copy-start(bf16[2,96,3]{1,0,2:T(2,128)(2,1)} %param.8) | copy-start | bytes 3460
  0.7 12.4 %copy-start.9 = (bf16[1,96,4,8,128]{4,3,2,1,0:T(8,128)(2,1)S(1)}, bf16[1,96,4,8,128]{4,3,2,1,0:T(8,128)(2,1)}, u32[]{:S(2)}) copy-start(bf16[1,96,4,8,128]{4,3,2,1,0:T(8,128)(2,1)} %param.6) | copy-start | bytes 2359300
  2.2 12.5 %collective-permute-start = (bf16[96,2,8,128]{3,0,2,1:T(8,128)(2,1)S(1)}, bf16[96,2,8,128]{3,0,2,1:T(8,128)(2,1)S(1)}, u32[]{:S(2)}, u32[]{:S(2)}) collective-permute-start(bf16[96,2,8,128]{3,0,2,1:T(8,128)(2,1)S(1)} %get-tuple-element.59), channel_id=1, source_target_pairs={{0,4},{4,8},{8,12},{12,16},{16,20},{20,24},{24,28},{28,32},{32,36}... | collective-permute-start | bytes 1179656 | tf_op jit(solution)/shard_map/ppermute | solution.py:21
  4.2 12.4 %collective-permute-start.1 = (bf16[96,2,8,128]{3,0,2,1:T(8,128)(2,1)S(1)}, bf16[96,2,8,128]{3,0,2,1:T(8,128)(2,1)S(1)}, u32[]{:S(2)}, u32[]{:S(2)}) collective-permute-start(bf16[96,2,8,128]{3,0,2,1:T(8,128)(2,1)S(1)} %get-tuple-element.60), channel_id=1, source_target_pairs={{4,0},{8,4},{12,8},{16,12},{20,16},{24,20},{28,24},{32,28},{36,32}... | collective-permute-start | bytes 1179656 | tf_op jit(solution)/shard_map/ppermute | solution.py:22
  11.9 5.4 %copy-start.18 = (f32[96]{0:T(128)}, f32[96]{0:T(128)S(1)}, u32[]{:S(2)}) copy-start(f32[96]{0:T(128)S(1)} %get-tuple-element.77) | copy-start | bytes 1156
  11.9 5.4 %copy-start.20 = (f32[96]{0:T(128)}, f32[96]{0:T(128)S(1)}, u32[]{:S(2)}) copy-start(f32[96]{0:T(128)S(1)} %get-tuple-element.78) | copy-start | bytes 1156
  11.9 5.4 %copy-start.22 = (f32[96]{0:T(128)}, f32[96]{0:T(128)S(1)}, u32[]{:S(2)}) copy-start(f32[96]{0:T(128)S(1)} %get-tuple-element.79) | copy-start | bytes 1156
  14.5 12.0 %copy-start.37 = (f32[96]{0:T(128)}, f32[96]{0:T(128)S(1)}, u32[]{:S(2)}) copy-start(f32[96]{0:T(128)S(1)} %get-tuple-element.67) | copy-start | bytes 1156
  14.5 12.0 %copy-start.39 = (f32[96]{0:T(128)}, f32[96]{0:T(128)S(1)}, u32[]{:S(2)}) copy-start(f32[96]{0:T(128)S(1)} %get-tuple-element.68) | copy-start | bytes 1156
  14.5 12.0 %copy-start.41 = (f32[96]{0:T(128)}, f32[96]{0:T(128)S(1)}, u32[]{:S(2)}) copy-start(f32[96]{0:T(128)S(1)} %get-tuple-element.69) | copy-start | bytes 1156
  14.5 12.0 %copy-start.43 = (f32[96]{0:T(128)}, f32[96]{0:T(128)S(1)}, u32[]{:S(2)}) copy-start(f32[96]{0:T(128)S(1)} %get-tuple-element.70) | copy-start | bytes 1156
  14.6 12.0 %copy-start.45 = (f32[96]{0:T(128)}, f32[96]{0:T(128)S(1)}, u32[]{:S(2)}) copy-start(f32[96]{0:T(128)S(1)} %get-tuple-element.71) | copy-start | bytes 1156
  14.6 12.0 %copy-start.47 = (f32[96]{0:T(128)}, f32[96]{0:T(128)S(1)}, u32[]{:S(2)}) copy-start(f32[96]{0:T(128)S(1)} %get-tuple-element.72) | copy-start | bytes 1156
  14.6 12.0 %copy-start.49 = (f32[96]{0:T(128)}, f32[96]{0:T(128)S(1)}, u32[]{:S(2)}) copy-start(f32[96]{0:T(128)S(1)} %get-tuple-element.73) | copy-start | bytes 1156
  14.6 12.0 %copy-start.51 = (f32[96]{0:T(128)}, f32[96]{0:T(128)S(1)}, u32[]{:S(2)}) copy-start(f32[96]{0:T(128)S(1)} %get-tuple-element.74) | copy-start | bytes 1156
  14.6 12.0 %copy-start.53 = (f32[96]{0:T(128)}, f32[96]{0:T(128)S(1)}, u32[]{:S(2)}) copy-start(f32[96]{0:T(128)S(1)} %get-tuple-element.75) | copy-start | bytes 1156
  17.3 4.7 %copy-start.2 = (bf16[96,8,8,128]{3,0,2,1:T(8,128)(2,1)}, bf16[96,8,8,128]{3,0,2,1:T(8,128)(2,1)S(1)}, u32[]{:S(2)}) copy-start(bf16[96,8,8,128]{3,0,2,1:T(8,128)(2,1)S(1)} %pad_maximum_fusion) | copy-start | bytes 4718596
  48.7 13.7 %collective-permute-start.2 = (bf16[96,1,8,128]{3,2,1,0:T(8,128)(2,1)}, bf16[96,1,8,128]{3,2,1,0:T(8,128)(2,1)}, u32[]{:S(2)}, u32[]{:S(2)}) collective-permute-start(bf16[96,1,8,128]{3,2,1,0:T(8,128)(2,1)} %get-tuple-element.57), channel_id=1, source_target_pairs={{0,4},{4,8},{8,12},{12,16},{16,20},{20,24},{24,28},{28,32},{32,36}... | collective-permute-start | bytes 589832 | tf_op jit(solution)/shard_map/ppermute | solution.py:21
  50.6 11.8 %collective-permute-start.3 = (bf16[96,1,8,128]{3,2,1,0:T(8,128)(2,1)}, bf16[96,1,8,128]{3,2,1,0:T(8,128)(2,1)}, u32[]{:S(2)}, u32[]{:S(2)}) collective-permute-start(bf16[96,1,8,128]{3,2,1,0:T(8,128)(2,1)} %get-tuple-element.58), channel_id=1, source_target_pairs={{4,0},{8,4},{12,8},{16,12},{20,16},{24,20},{28,24},{32,28},{36,32}... | collective-permute-start | bytes 589832 | tf_op jit(solution)/shard_map/ppermute | solution.py:22
  65.2 4.5 %copy-start.6 = (bf16[96,6,8,128]{3,0,2,1:T(8,128)(2,1)S(1)}, bf16[96,6,8,128]{3,0,2,1:T(8,128)(2,1)}, u32[]{:S(2)}) copy-start(bf16[96,6,8,128]{3,0,2,1:T(8,128)(2,1)} %copy-done.5) | copy-start | bytes 3538948
  127.2 9.6 %collective-permute-start.4 = (bf16[96,1,8,128]{3,0,2,1:T(8,128)(2,1)S(1)}, bf16[96,1,8,128]{3,0,2,1:T(8,128)(2,1)S(1)}, u32[]{:S(2)}, u32[]{:S(2)}) collective-permute-start(bf16[96,1,8,128]{3,0,2,1:T(8,128)(2,1)S(1)} %get-tuple-element.55), channel_id=1, source_target_pairs={{0,4},{4,8},{8,12},{12,16},{16,20},{20,24},{24,28},{28,32},{32,36}... | collective-permute-start | bytes 589832 | tf_op jit(solution)/shard_map/ppermute | solution.py:21
  129.1 8.9 %collective-permute-start.5 = (bf16[96,1,8,128]{3,0,2,1:T(8,128)(2,1)S(1)}, bf16[96,1,8,128]{3,0,2,1:T(8,128)(2,1)S(1)}, u32[]{:S(2)}, u32[]{:S(2)}) collective-permute-start(bf16[96,1,8,128]{3,0,2,1:T(8,128)(2,1)S(1)} %get-tuple-element.56), channel_id=1, source_target_pairs={{4,0},{8,4},{12,8},{16,12},{20,16},{24,20},{28,24},{32,28},{36,32}... | collective-permute-start | bytes 589832 | tf_op jit(solution)/shard_map/ppermute | solution.py:22
  136.8 2.9 %copy-start.27 = (f32[96]{0:T(128)S(1)}, f32[96]{0:T(128)}, u32[]{:S(2)}) copy-start(f32[96]{0:T(128)} %get-tuple-element.81) | copy-start | bytes 1156
  (40 other events, 78.8 us)

commit v2 on v1

v2 whole, which is shorter than its diff:
```python
import functools
import math

import jax
import jax.numpy as jnp
from jax import lax
from jax.experimental import pallas as pl
from jax.experimental.pallas import tpu as pltpu
from jax.sharding import PartitionSpec as P

MESH = pl.DeviceIdType.MESH


def exchange_bits(axes):
    bits = []
    for name, size in axes:
        assert size & (size - 1) == 0
        for b in range(size.bit_length() - 1):
            bits.append((name, 1 << b))
    return bits


def allreduce_kernel(axes, x_ref, o_ref, recv, acc, send_sem, recv_sem):
    bits = exchange_bits(axes)
    here = {name: lax.axis_index(name) for name, _ in axes}
    partners = []
    for name, stride in bits:
        bit = (here[name] // stride) % 2
        where = dict(here)
        where[name] = here[name] + stride * (1 - 2 * bit)
        partners.append(tuple(where[n] for n, _ in axes))
    barrier = pltpu.get_barrier_semaphore()
    for partner in partners:
        pl.semaphore_signal(barrier, inc=1, device_id=partner, device_id_type=MESH)
    pl.semaphore_wait(barrier, len(partners))
    src = x_ref
    for k, partner in enumerate(partners):
        copy = pltpu.make_async_remote_copy(
            src_ref=src,
            dst_ref=recv.at[k],
            send_sem=send_sem.at[k],
            recv_sem=recv_sem.at[k],
            device_id=partner,
            device_id_type=MESH,
        )
        copy.start()
        copy.wait()
        dst = o_ref if k == len(partners) - 1 else acc.at[k]
        dst[...] = src[...] + recv[k]
        src = dst


def all_sum(flat, axes):
    steps = len(exchange_bits(axes))
    return pl.pallas_call(
        functools.partial(allreduce_kernel, axes),
        out_shape=jax.ShapeDtypeStruct(flat.shape, flat.dtype),
        in_specs=[pl.BlockSpec(memory_space=pltpu.VMEM)],
        out_specs=pl.BlockSpec(memory_space=pltpu.VMEM),
        scratch_shapes=[
            pltpu.VMEM((steps,) + flat.shape, flat.dtype),
            pltpu.VMEM((steps,) + flat.shape, flat.dtype),
            pltpu.SemaphoreType.DMA((steps,)),
            pltpu.SemaphoreType.DMA((steps,)),
        ],
        compiler_params=pltpu.CompilerParams(collective_id=0, has_side_effects=True),
    )(flat)


def settle_all(*parts):
    flat = jnp.concatenate([p.reshape(-1) for p in parts])
    rows = -(-flat.shape[0] // 1024) * 8
    flat = jnp.pad(flat, (0, rows * 128 - flat.shape[0])).reshape(rows, 128)
    axes = (("sp", lax.axis_size("sp")), ("dp", lax.axis_size("dp")))
    flat = all_sum(flat, axes).reshape(-1)
    summed, at = [], 0
    for p in parts:
        summed.append(flat[at : at + p.size].reshape(p.shape))
        at += p.size
    return summed


VMEM_LIMIT = 56 * 1024 * 1024


def halo(x, width):
    count = lax.axis_size("sp")
    up = [(i, i + 1) for i in range(count - 1)]
    down = [(j, i) for i, j in up]
    before = lax.ppermute(x[x.shape[0] - width :], "sp", up)
    after = lax.ppermute(x[:width], "sp", down)
    return jnp.concatenate([before, x, after], axis=0)


def coords(shape):
    lane = lax.broadcasted_iota(jnp.int32, shape, 1)
    return jnp.bitwise_and(lane, 127), jnp.right_shift(lane, 7)


def at_y(a, d, y):
    if d == 0:
        return a
    rolled = pltpu.roll(a, (-d) % a.shape[1], 1)
    return jnp.where((y + d >= 0) & (y + d < 128), rolled, 0.0)


def at_z(a, d, z):
    if d == 0:
        return a
    rolled = pltpu.roll(a, (-128 * d) % a.shape[1], 1)
    return jnp.where((z + d >= 0) & (z + d < a.shape[1] // 128), rolled, 0.0)


def widen(k, lanes):
    return jnp.concatenate([k] * (lanes // k.shape[1]), axis=1)


def fold(a):
    total = a[:, :128]
    for g in range(1, a.shape[1] // 128):
        total = total + a[:, g * 128 : (g + 1) * 128]
    return total


def sigmoid(u):
    return 1.0 / (1.0 + jnp.exp(-u))


def plane_conv(planes, k_ref, b, flip, y):
    lanes = planes[0].shape[1]
    total = None
    for i in range(3):
        src = planes[i].astype(jnp.float32)
        for j in range(3):
            tap = (2 - i) * 3 + (2 - j) if flip else i * 3 + j
            term = widen(k_ref[b, tap], lanes) * at_y(src, j - 1, y)
            total = term if total is None else total + term
    return total


def depth_conv(a, kz_ref, b, flip, z):
    lanes = a.shape[1]
    total = None
    for t in range(3):
        tap = 2 - t if flip else t
        term = widen(kz_ref[b, tap], lanes) * at_z(a, t - 1, z)
        total = term if total is None else total + term
    return total


def silu_grad(g, pre):
    s = sigmoid(pre)
    return (g * (s * (1.0 + pre * (1.0 - s)))).astype(jnp.bfloat16)


def weight_grads(b, gpre, ax, gax, pl, gpl, around, mix_ref, kzg_ref, kxyg_ref, y, z):
    mix_ref[b] += lax.dot_general(
        gpre, ax, (((1,), (1,)), ((), ())), preferred_element_type=jnp.float32
    )
    for t in range(3):
        kzg_ref[b, t] += fold(gax * at_z(pl, t - 1, z))
    gplf = gpl.astype(jnp.float32)
    for i in range(3):
        src = around[i].astype(jnp.float32)
        for j in range(3):
            kxyg_ref[b, i * 3 + j] += fold(gplf * at_y(src, j - 1, y))


def upper_kernel(mask_ref, wide_ref, cot_ref, kxy_ref, kz_ref, w_ref, wt_ref,
                 gp2_ref, pre1_ref, ax1_ref, pl1_ref, mix_ref, kzg_ref, kxyg_ref, h2_ref):
    own = cot_ref.shape[0]
    y, z = coords(cot_ref.shape[1:])
    mix_ref[...] = jnp.zeros_like(mix_ref)
    kzg_ref[...] = jnp.zeros_like(kzg_ref)
    kxyg_ref[...] = jnp.zeros_like(kxyg_ref)

    def forward1(p, carry):
        planar = plane_conv([wide_ref[p + i] for i in range(3)], kxy_ref, 0, False, y)
        axial = depth_conv(planar, kz_ref, 0, False, z).astype(jnp.bfloat16)
        pre = jnp.dot(w_ref[0], axial, preferred_element_type=jnp.float32)
        pl1_ref[p] = planar
        ax1_ref[p] = axial
        pre1_ref[p] = pre
        h2_ref[p] = (pre * sigmoid(pre) * mask_ref[p]).astype(jnp.bfloat16)
        return carry

    lax.fori_loop(0, own + 2, forward1, 0)

    def block2(q, carry):
        around = [h2_ref[q + i] for i in range(3)]
        planar = plane_conv(around, kxy_ref, 1, False, y)
        axial = depth_conv(planar, kz_ref, 1, False, z).astype(jnp.bfloat16)
        pre = jnp.dot(w_ref[1], axial, preferred_element_type=jnp.float32)
        gpre = silu_grad(cot_ref[q].astype(jnp.float32), pre)
        gax = jnp.dot(wt_ref[1], gpre, preferred_element_type=jnp.float32)
        gpl = depth_conv(gax, kz_ref, 1, True, z).astype(jnp.bfloat16)
        gp2_ref[q] = gpl
        weight_grads(1, gpre, axial, gax, planar, gpl, around, mix_ref, kzg_ref, kxyg_ref, y, z)
        return carry

    lax.fori_loop(0, own, block2, 0)


def lower_kernel(gp2_ref, wide_ref, pre1_ref, ax1_ref, pl1_ref, kxy_ref, kz_ref, w_ref, wt_ref, mix_in, kzg_in, kxyg_in,
                 gp1_ref, mix_ref, kzg_ref, kxyg_ref):
    own = gp1_ref.shape[0]
    y, z = coords(gp1_ref.shape[1:])
    mix_ref[...] = mix_in[...]
    kzg_ref[...] = kzg_in[...]
    kxyg_ref[...] = kxyg_in[...]

    def block1(q, carry):
        g1 = plane_conv([gp2_ref[q + i] for i in range(3)], kxy_ref, 1, True, y).astype(jnp.bfloat16)
        gpre = silu_grad(g1.astype(jnp.float32), pre1_ref[q + 1])
        gax = jnp.dot(wt_ref[0], gpre, preferred_element_type=jnp.float32)
        gpl = depth_conv(gax, kz_ref, 0, True, z).astype(jnp.bfloat16)
        gp1_ref[q] = gpl
        around = [wide_ref[q + 1 + i] for i in range(3)]
        weight_grads(0, gpre, ax1_ref[q + 1], gax, pl1_ref[q + 1], gpl, around, mix_ref, kzg_ref, kxyg_ref, y, z)
        return carry

    lax.fori_loop(0, own, block1, 0)


def input_kernel(gp1_ref, kxy_ref, out_ref):
    y, _ = coords(out_ref.shape[1:])

    def plane(q, carry):
        out_ref[q] = plane_conv([gp1_ref[q + i] for i in range(3)], kxy_ref, 0, True, y).astype(out_ref.dtype)
        return carry

    lax.fori_loop(0, out_ref.shape[0], plane, 0)


def vmem_call(kernel, args, outs, scratch=(), smem=0, aliases=None):
    specs = [pl.BlockSpec(memory_space=pltpu.SMEM)] * smem + [pl.BlockSpec(memory_space=pltpu.VMEM)] * (len(args) - smem)
    return pl.pallas_call(
        kernel,
        out_shape=outs,
        in_specs=specs,
        out_specs=[pl.BlockSpec(memory_space=pltpu.VMEM)] * len(outs),
        scratch_shapes=list(scratch),
        input_output_aliases=aliases or {},
        compiler_params=pltpu.CompilerParams(vmem_limit_bytes=VMEM_LIMIT),
    )(*args)


def on_device(volume, cotangent, kernels_xy, kernels_z, mixing):
    _, chans, own, depth, across = volume.shape
    lanes = depth * across
    f32, bf16 = jnp.float32, jnp.bfloat16
    vol = volume[0].reshape(chans, own, lanes).transpose(1, 0, 2)
    cot = cotangent[0].reshape(chans, own, lanes).transpose(1, 0, 2)
    kxy = jnp.broadcast_to(
        kernels_xy.astype(f32).reshape(2, chans, 9).transpose(0, 2, 1)[..., None], (2, 9, chans, 128)
    )
    kz = jnp.broadcast_to(kernels_z.astype(f32).transpose(0, 2, 1)[..., None], (2, 3, chans, 128))
    wt = mixing.transpose(0, 2, 1)
    ranks = lax.axis_size("sp")
    place = lax.axis_index("sp")
    spots = place * own - 1 + jnp.arange(own + 2, dtype=jnp.int32)
    mask = ((spots >= 0) & (spots < own * ranks)).astype(f32)
    wide = halo(vol, 2)
    plane = lambda n, t: jax.ShapeDtypeStruct((n, chans, lanes), t)
    gp2, pre1, ax1, pl1, mix, kzg, kxyg = vmem_call(
        upper_kernel,
        (mask, wide, cot, kxy, kz, mixing, wt),
        (
            plane(own, bf16), plane(own + 2, f32), plane(own + 2, bf16), plane(own + 2, f32),
            jax.ShapeDtypeStruct((2, chans, chans), f32),
            jax.ShapeDtypeStruct((2, 3, chans, 128), f32),
            jax.ShapeDtypeStruct((2, 9, chans, 128), f32),
        ),
        scratch=[pltpu.VMEM((own + 2, chans, lanes), bf16)],
        smem=1,
    )
    gp1, mix, kzg, kxyg = vmem_call(
        lower_kernel,
        (halo(gp2, 1), wide, pre1, ax1, pl1, kxy, kz, mixing, wt, mix, kzg, kxyg),
        (plane(own, bf16), jax.ShapeDtypeStruct((2, chans, chans), f32),
         jax.ShapeDtypeStruct((2, 3, chans, 128), f32), jax.ShapeDtypeStruct((2, 9, chans, 128), f32)),
    )
    grad_in = vmem_call(input_kernel, (halo(gp1, 1), kxy), (plane(own, bf16),))[0]
    grad_in = grad_in.transpose(1, 0, 2).reshape(1, chans, own, depth, across)
    kz_sum = kzg.sum(axis=3).transpose(0, 2, 1)
    kxy_sum = kxyg.sum(axis=3).transpose(0, 2, 1).reshape(2, chans, 3, 3)
    summed = settle_all(mix, kxy_sum, kz_sum)
    factor = 1.0 / math.sqrt(lax.axis_size("dp") * own * ranks * depth * across)
    return (grad_in, summed[0] * factor, summed[1] * factor, summed[2] * factor)


def solution(mesh):
    return jax.shard_map(
        on_device,
        mesh=mesh,
        in_specs=(P("dp", None, "sp", None, None), P("dp", None, "sp", None, None), P(), P(), P()),
        out_specs=(P("dp", None, "sp", None, None), P(), P(), P()),
        check_vma=False,
    )
```

time: 144 us -> 134 us (0.931)
  the two profiles are of different devices: /device:TPU:8 before, /device:TPU:1 now
where the time goes in v2:
time: 134 us; the launch traced here: 132 us
  Pallas kernels  76.1 us (57%)
  starting transfers between devices  18.4 us (14%)
  local copies, waits for them, and re-layouts  15.6 us (12%)
  waiting for transfers between devices  11.8 us (9%)
  other arithmetic  9.42 us (7%)
    pallas_call x1, Pallas kernels, all_sum(): pl.pallas_call(functools.partial(allreduce_kernel, axes), out_shape=jax.S...  42.6 us
    pallas_call x3, Pallas kernels, vmem_call(): pl.pallas_call(kernel, out_shape=outs, in_specs=specs, out_specs=[pl.Bloc...  33.5 us
    ppermute x3, waiting for transfers between devices, halo(): after = lax.ppermute(x[:width], 'sp', down)  11.2 us
    ppermute x3, starting transfers between devices, halo(): before = lax.ppermute(x[x.shape[0] - width:], 'sp', up)  11.1 us
    ppermute x3, starting transfers between devices, halo(): after = lax.ppermute(x[:width], 'sp', down)  7.37 us
    unnamed x17, local copies, waits for them, and re-layouts  4.48 us
    concatenate x3, other arithmetic, halo(): return jnp.concatenate([before, x, after], axis=0)  3.77 us
  transfers between devices with their start and end apart: 6, of which 5 were waited for; matrix products, arithmetic and copies ran while one was open for 3% of the time, Pallas kernels for 0%

profile of v2, /device:TPU:1, one launch (start us, length us, event | category | flops | bytes accessed | tf_op | source)
XLA Modules:
  0.0 132.2 jit_solution(9831069528757601107)
XLA Ops:
  0.6 1.8 %reshape.47 = bf16[96,4,1024]{2,1,0:T(4,128)(2,1)S(1)} reshape(bf16[1,96,4,8,128]{4,3,2,1,0:T(8,128)(2,1)} %param.5) | data formatting | bytes 1572864 | tf_op jit(solution)/shard_map/reshape;squeeze | solution.py:252
  3.6 4.9 %collective-permute-start = (bf16[2,96,1024]{2,1,0:T(8,128)(2,1)}, bf16[2,96,1024]{2,1,0:T(8,128)(2,1)S(1)}, u32[]{:S(2)}, u32[]{:S(2)}) collective-permute-start(bf16[2,96,1024]{2,1,0:T(8,128)(2,1)} %get-tuple-element.42), channel_id=1, source_target_pairs={{0,4},{4,8},{8,12},{12,16},{16,20},{20,24},{24,28},{28,32},{32,36}... | collective-permute-start | bytes 1179656 | tf_op jit(solution)/shard_map/ppermute | solution.py:90
  8.6 1.9 %collective-permute-start.1 = (bf16[2,96,1024]{2,1,0:T(8,128)(2,1)}, bf16[2,96,1024]{2,1,0:T(8,128)(2,1)S(1)}, u32[]{:S(2)}, u32[]{:S(2)}) collective-permute-start(bf16[2,96,1024]{2,1,0:T(8,128)(2,1)} %get-tuple-element.43), channel_id=1, source_target_pairs={{4,0},{8,4},{12,8},{16,12},{20,16},{24,20},{28,24},{32,28},{36,32}... | collective-permute-start | bytes 1179656 | tf_op jit(solution)/shard_map/ppermute | solution.py:91
  11.5 1.1 copy.39
  13.6 4.3 %collective-permute-done.1 = bf16[2,96,1024]{2,1,0:T(8,128)(2,1)S(1)} collective-permute-done((bf16[2,96,1024]{2,1,0:T(8,128)(2,1)}, bf16[2,96,1024]{2,1,0:T(8,128)(2,1)S(1)}, u32[]{:S(2)}, u32[]{:S(2)}) %collective-permute-start.1) | collective-permute-done | bytes 393248 | tf_op jit(solution)/shard_map/ppermute | solution.py:91
  17.9 1.3 %pad_maximum_fusion.wide_ref = bf16[8,96,1024]{2,1,0:T(8,128)(2,1)} fusion(bf16[2,96,1024]{2,1,0:T(8,128)(2,1)S(1)} %collective-permute-done.1, bf16[4,96,1024]{2,1,0:T(8,128)(2,1)S(1)} %bitcast.32, bf16[2,96,1024]{2,1,0:T(8,128)(2,1)S(1)} %collective-permute-done), kind=kLoop, calls=%fused_computation | loop fusion | flops 1572864 | bytes 3145728 | tf_op jit(solution)/shard_map/concatenate | solution.py:92
  20.1 1.3 broadcast_in_dim.4.kxy_ref
  21.3 15.8 %shard_map.84 = (bf16[4,96,1024]{2,1,0:T(8,128)(2,1)}, f32[6,96,1024]{2,1,0:T(8,128)}, bf16[6,96,1024]{2,1,0:T(8,128)(2,1)}, f32[6,96,1024]{2,1,0:T(8,128)}, f32...) custom-call(f32[6]{0:T(128)} %and_convert_fusion.mask_ref, ...), custom_call_target="tpu_custom_call" | custom-call | tf_op jit(solution)/shard_map/pallas_call | solution.py:237
  37.1 1.1 fusion.1
  38.3 1.9 %collective-permute-start.2 = (bf16[1,96,1024]{2,1,0:T(8,128)(2,1)S(1)}, bf16[1,96,1024]{2,1,0:T(8,128)(2,1)S(1)}, u32[]{:S(2)}, u32[]{:S(2)}) collective-permute-start(bf16[1,96,1024]{2,1,0:T(8,128)(2,1)S(1)} %get-tuple-element.40), channel_id=1, source_target_pairs={{0,4},{4,8},{8,12},{12,16},{16,20},{20,24},{24,28},{28,32},{32,36}... | collective-permute-start | bytes 589832 | tf_op jit(solution)/shard_map/ppermute | solution.py:90
  40.2 2.4 %collective-permute-start.3 = (bf16[1,96,1024]{2,1,0:T(8,128)(2,1)S(1)}, bf16[1,96,1024]{2,1,0:T(8,128)(2,1)S(1)}, u32[]{:S(2)}, u32[]{:S(2)}) collective-permute-start(bf16[1,96,1024]{2,1,0:T(8,128)(2,1)S(1)} %get-tuple-element.41), channel_id=1, source_target_pairs={{4,0},{8,4},{12,8},{16,12},{20,16},{24,20},{28,24},{32,28},{36,32}... | collective-permute-start | bytes 589832 | tf_op jit(solution)/shard_map/ppermute | solution.py:91
  42.8 4.7 %collective-permute-done.3 = bf16[1,96,1024]{2,1,0:T(8,128)(2,1)S(1)} collective-permute-done((bf16[1,96,1024]{2,1,0:T(8,128)(2,1)S(1)}, bf16[1,96,1024]{2,1,0:T(8,128)(2,1)S(1)}, u32[]{:S(2)}, u32[]{:S(2)}) %collective-permute-start.3) | collective-permute-done | bytes 196640 | tf_op jit(solution)/shard_map/ppermute | solution.py:91
  47.5 1.3 pad_maximum_fusion.1.gp2_ref
  48.7 12.5 %shard_map.85 = (bf16[4,96,1024]{2,1,0:T(8,128)(2,1)}, f32[2,96,96]{2,1,0:T(8,128)}, f32[2,3,96,128]{3,2,1,0:T(8,128)}, f32[2,9,96,128]{3,2,1,0:T(8,128)}) custom-call(bf16[6,96,1024]{2,1,0:T(8,128)(2,1)} %pad_maximum_fusion.1.gp2_ref, bf16[8,96,1024]{2,1,0:T(8,128)(2,1)} %pad_maximum_fusion.wide_ref, f32[6,96,1024]{2,1,0:T(8,128)} %get-tuple-element.16.pre1_ref, ...), custom_call_target="tpu_custom_call" | custom-call | tf_op jit(solution)/shard_map/pallas_call | solution.py:237
  62.2 1.1 reduce_sum.19
  63.4 1.6 %reduce_sum.18 = f32[2,9,96]{2,1,0:T(8,128)S(1)} reduce(f32[2,9,96,128]{3,2,1,0:T(8,128)} %get-tuple-element.24, f32[]{:T(128)} %constant.7.clone.1), dimensions={3}, to_apply=%region_0.0 | reduce | flops 219456 | bytes 891652 | tf_op jit(solution)/shard_map/reduce_sum | solution.py:286
  66.4 42.6 %shard_map.87 = f32[168,128]{1,0:T(8,128)} custom-call(f32[168,128]{1,0:T(8,128)} %pad_bitcast_fusion.x_ref), custom_call_target="tpu_custom_call" | custom-call | tf_op jit(solution)/shard_map/pallas_call | solution.py:55
  112.3 4.2 %collective-permute-start.4 = (bf16[1,96,1024]{2,1,0:T(8,128)(2,1)S(1)}, bf16[1,96,1024]{2,1,0:T(8,128)(2,1)S(1)}, u32[]{:S(2)}, u32[]{:S(2)}) collective-permute-start(bf16[1,96,1024]{2,1,0:T(8,128)(2,1)S(1)} %get-tuple-element.38), channel_id=1, source_target_pairs={{0,4},{4,8},{8,12},{12,16},{16,20},{20,24},{24,28},{28,32},{32,36}... | collective-permute-start | bytes 589832 | tf_op jit(solution)/shard_map/ppermute | solution.py:90
  116.5 3.0 %collective-permute-start.5 = (bf16[1,96,1024]{2,1,0:T(8,128)(2,1)S(1)}, bf16[1,96,1024]{2,1,0:T(8,128)(2,1)S(1)}, u32[]{:S(2)}, u32[]{:S(2)}) collective-permute-start(bf16[1,96,1024]{2,1,0:T(8,128)(2,1)S(1)} %get-tuple-element.39), channel_id=1, source_target_pairs={{4,0},{8,4},{12,8},{16,12},{20,16},{24,20},{28,24},{32,28},{36,32}... | collective-permute-start | bytes 589832 | tf_op jit(solution)/shard_map/ppermute | solution.py:91
  121.3 2.2 %collective-permute-done.5 = bf16[1,96,1024]{2,1,0:T(8,128)(2,1)S(1)} collective-permute-done((bf16[1,96,1024]{2,1,0:T(8,128)(2,1)S(1)}, bf16[1,96,1024]{2,1,0:T(8,128)(2,1)S(1)}, u32[]{:S(2)}, u32[]{:S(2)}) %collective-permute-start.5) | collective-permute-done | bytes 196640 | tf_op jit(solution)/shard_map/ppermute | solution.py:91
  123.5 1.2 pad_maximum_fusion.2.gp1_ref
  124.7 5.2 %shard_map.86 = bf16[4,96,1024]{2,1,0:T(8,128)(2,1)} custom-call(bf16[6,96,1024]{2,1,0:T(8,128)(2,1)} %pad_maximum_fusion.2.gp1_ref, f32[2,9,96,128]{3,2,1,0:T(8,128)} %broadcast_in_dim.4.kxy_ref), custom_call_target="tpu_custom_call" | custom-call | tf_op jit(solution)/shard_map/pallas_call | solution.py:237
  129.9 1.3 copy.35
  131.2 1.0 copy.30
  (41 shorter events, 11.5 us)
Async XLA Ops:
  2.6 7.9 %copy-start.5 = (bf16[2,96,3]{1,0,2:T(2,128)(2,1)S(1)}, bf16[2,96,3]{1,0,2:T(2,128)(2,1)}, u32[]{:S(2)}) copy-start(bf16[2,96,3]{1,0,2:T(2,128)(2,1)} %param.8) | copy-start | bytes 3460
  2.6 7.9 %copy-start.4 = (bf16[2,96,3,3]{1,0,3,2:T(2,128)(2,1)S(1)}, bf16[2,96,3,3]{1,0,3,2:T(2,128)(2,1)}, u32[]{:S(2)}) copy-start(bf16[2,96,3,3]{1,0,3,2:T(2,128)(2,1)} %param.7) | copy-start | bytes 10372
  2.7 7.9 %copy-start.3 = (bf16[2,96,96]{2,1,0:T(8,128)(2,1)S(1)}, bf16[2,96,96]{2,1,0:T(8,128)(2,1)}, u32[]{:S(2)}) copy-start(bf16[2,96,96]{2,1,0:T(8,128)(2,1)} %w_ref.3) | copy-start | bytes 110596
  2.7 8.6 %copy-start.2 = (bf16[1,96,4,8,128]{4,3,2,1,0:T(8,128)(2,1)S(1)}, bf16[1,96,4,8,128]{4,3,2,1,0:T(8,128)(2,1)}, u32[]{:S(2)}) copy-start(bf16[1,96,4,8,128]{4,3,2,1,0:T(8,128)(2,1)} %param.6) | copy-start | bytes 2359300
  3.6 9.9 %collective-permute-start = (bf16[2,96,1024]{2,1,0:T(8,128)(2,1)}, bf16[2,96,1024]{2,1,0:T(8,128)(2,1)S(1)}, u32[]{:S(2)}, u32[]{:S(2)}) collective-permute-start(bf16[2,96,1024]{2,1,0:T(8,128)(2,1)} %get-tuple-element.42), channel_id=1, source_target_pairs={{0,4},{4,8},{8,12},{12,16},{16,20},{20,24},{24,28},{28,32},{32,36}... | collective-permute-start | bytes 1179656 | tf_op jit(solution)/shard_map/ppermute | solution.py:90
  8.6 9.3 %collective-permute-start.1 = (bf16[2,96,1024]{2,1,0:T(8,128)(2,1)}, bf16[2,96,1024]{2,1,0:T(8,128)(2,1)S(1)}, u32[]{:S(2)}, u32[]{:S(2)}) collective-permute-start(bf16[2,96,1024]{2,1,0:T(8,128)(2,1)} %get-tuple-element.43), channel_id=1, source_target_pairs={{4,0},{8,4},{12,8},{16,12},{20,16},{24,20},{28,24},{32,28},{36,32}... | collective-permute-start | bytes 1179656 | tf_op jit(solution)/shard_map/ppermute | solution.py:91
  37.1 10.3 %copy-start.1 = (bf16[4,96,1024]{2,1,0:T(8,128)(2,1)S(1)}, bf16[4,96,1024]{2,1,0:T(8,128)(2,1)}, u32[]{:S(2)}) copy-start(bf16[4,96,1024]{2,1,0:T(8,128)(2,1)} %get-tuple-element.15) | copy-start | bytes 2359300
  38.3 4.5 %collective-permute-start.2 = (bf16[1,96,1024]{2,1,0:T(8,128)(2,1)S(1)}, bf16[1,96,1024]{2,1,0:T(8,128)(2,1)S(1)}, u32[]{:S(2)}, u32[]{:S(2)}) collective-permute-start(bf16[1,96,1024]{2,1,0:T(8,128)(2,1)S(1)} %get-tuple-element.40), channel_id=1, source_target_pairs={{0,4},{4,8},{8,12},{12,16},{16,20},{20,24},{24,28},{28,32},{32,36}... | collective-permute-start | bytes 589832 | tf_op jit(solution)/shard_map/ppermute | solution.py:90
  40.2 7.3 %collective-permute-start.3 = (bf16[1,96,1024]{2,1,0:T(8,128)(2,1)S(1)}, bf16[1,96,1024]{2,1,0:T(8,128)(2,1)S(1)}, u32[]{:S(2)}, u32[]{:S(2)}) collective-permute-start(bf16[1,96,1024]{2,1,0:T(8,128)(2,1)S(1)} %get-tuple-element.41), channel_id=1, source_target_pairs={{4,0},{8,4},{12,8},{16,12},{20,16},{24,20},{28,24},{32,28},{36,32}... | collective-permute-start | bytes 589832 | tf_op jit(solution)/shard_map/ppermute | solution.py:91
  63.3 48.9 %copy-start = (bf16[4,96,1024]{2,1,0:T(8,128)(2,1)S(1)}, bf16[4,96,1024]{2,1,0:T(8,128)(2,1)}, u32[]{:S(2)}) copy-start(bf16[4,96,1024]{2,1,0:T(8,128)(2,1)} %get-tuple-element.22) | copy-start | bytes 2359300
  112.3 9.0 %collective-permute-start.4 = (bf16[1,96,1024]{2,1,0:T(8,128)(2,1)S(1)}, bf16[1,96,1024]{2,1,0:T(8,128)(2,1)S(1)}, u32[]{:S(2)}, u32[]{:S(2)}) collective-permute-start(bf16[1,96,1024]{2,1,0:T(8,128)(2,1)S(1)} %get-tuple-element.38), channel_id=1, source_target_pairs={{0,4},{4,8},{8,12},{12,16},{16,20},{20,24},{24,28},{28,32},{32,36}... | collective-permute-start | bytes 589832 | tf_op jit(solution)/shard_map/ppermute | solution.py:90
  116.5 7.0 %collective-permute-start.5 = (bf16[1,96,1024]{2,1,0:T(8,128)(2,1)S(1)}, bf16[1,96,1024]{2,1,0:T(8,128)(2,1)S(1)}, u32[]{:S(2)}, u32[]{:S(2)}) collective-permute-start(bf16[1,96,1024]{2,1,0:T(8,128)(2,1)S(1)} %get-tuple-element.39), channel_id=1, source_target_pairs={{4,0},{8,4},{12,8},{16,12},{20,16},{24,20},{28,24},{32,28},{36,32}... | collective-permute-start | bytes 589832 | tf_op jit(solution)/shard_map/ppermute | solution.py:91

commit v3 on v2

--- a/solution.py
+++ b/solution.py
@@ -11,57 +11,78 @@
 MESH = pl.DeviceIdType.MESH
 
 
-def exchange_bits(axes):
+def exchange_groups(axes, radix_bits):
     bits = []
     for name, size in axes:
         assert size & (size - 1) == 0
         for b in range(size.bit_length() - 1):
             bits.append((name, 1 << b))
-    return bits
-
-
-def allreduce_kernel(axes, x_ref, o_ref, recv, acc, send_sem, recv_sem):
-    bits = exchange_bits(axes)
+    return [bits[i : i + radix_bits] for i in range(0, len(bits), radix_bits)]
+
+
+def allreduce_kernel(axes, groups, x_ref, o_ref, recv, acc, send_sem, recv_sem):
     here = {name: lax.axis_index(name) for name, _ in axes}
-    partners = []
-    for name, stride in bits:
-        bit = (here[name] // stride) % 2
-        where = dict(here)
-        where[name] = here[name] + stride * (1 - 2 * bit)
-        partners.append(tuple(where[n] for n, _ in axes))
+    steps = []
+    for group in groups:
+        partners = []
+        for offset in range(1, 1 << len(group)):
+            where = dict(here)
+            for k, (name, stride) in enumerate(group):
+                if (offset >> k) & 1:
+                    bit = (where[name] // stride) % 2
+                    where[name] = where[name] + stride * (1 - 2 * bit)
+            partners.append(tuple(where[n] for n, _ in axes))
+        steps.append(partners)
     barrier = pltpu.get_barrier_semaphore()
-    for partner in partners:
-        pl.semaphore_signal(barrier, inc=1, device_id=partner, device_id_type=MESH)
-    pl.semaphore_wait(barrier, len(partners))
+    count = 0
+    for partners in steps:
+        for partner in partners:
+            pl.semaphore_signal(barrier, inc=1, device_id=partner, device_id_type=MESH)
+            count += 1
+    pl.semaphore_wait(barrier, count)
     src = x_ref
-    for k, partner in enumerate(partners):
-        copy = pltpu.make_async_remote_copy(
-            src_ref=src,
-            dst_ref=recv.at[k],
-            send_sem=send_sem.at[k],
-            recv_sem=recv_sem.at[k],
-            device_id=partner,
-            device_id_type=MESH,
-        )
-        copy.start()
-        copy.wait()
-        dst = o_ref if k == len(partners) - 1 else acc.at[k]
-        dst[...] = src[...] + recv[k]
+    copies = []
+    slot = 0
+    for g, partners in enumerate(steps):
+        here_copies = []
+        for k, partner in enumerate(partners):
+            copy = pltpu.make_async_remote_copy(
+                src_ref=src,
+                dst_ref=recv.at[slot + k],
+                send_sem=send_sem.at[slot + k],
+                recv_sem=recv_sem.at[slot + k],
+                device_id=partner,
+                device_id_type=MESH,
+            )
+            copy.start()
+            here_copies.append(copy)
+        for copy in here_copies:
+            copy.wait_recv()
+        copies += here_copies
+        vals = [src[...]] + [recv[slot + k] for k in range(len(partners))]
+        while len(vals) > 1:
+            vals = [vals[i] + vals[i + 1] for i in range(0, len(vals), 2)]
+        dst = o_ref if g == len(steps) - 1 else acc.at[g]
+        dst[...] = vals[0]
         src = dst
-
-
-def all_sum(flat, axes):
-    steps = len(exchange_bits(axes))
+        slot += len(partners)
+    for copy in copies:
+        copy.wait_send()
+
+
+def all_sum(flat, axes, radix_bits=2):
+    groups = exchange_groups(axes, radix_bits)
+    slots = sum((1 << len(g)) - 1 for g in groups)
     return pl.pallas_call(
-        functools.partial(allreduce_kernel, axes),
+        functools.partial(allreduce_kernel, axes, groups),
         out_shape=jax.ShapeDtypeStruct(flat.shape, flat.dtype),
         in_specs=[pl.BlockSpec(memory_space=pltpu.VMEM)],
         out_specs=pl.BlockSpec(memory_space=pltpu.VMEM),
         scratch_shapes=[
-            pltpu.VMEM((steps,) + flat.shape, flat.dtype),
-            pltpu.VMEM((steps,) + flat.shape, flat.dtype),
-            pltpu.SemaphoreType.DMA((steps,)),
-            pltpu.SemaphoreType.DMA((steps,)),
+            pltpu.VMEM((slots,) + flat.shape, flat.dtype),
+            pltpu.VMEM((len(groups),) + flat.shape, flat.dtype),
+            pltpu.SemaphoreType.DMA((slots,)),
+            pltpu.SemaphoreType.DMA((slots,)),
         ],
         compiler_params=pltpu.CompilerParams(collective_id=0, has_side_effects=True),
     )(flat)

time: 134 us -> 128 us (0.955)
  Pallas kernels: 76.1 us -> 65.1 us
  starting transfers between devices: 18.4 us -> 23.2 us
    pallas_call x1, Pallas kernels: 42.6 us -> 31.7 us  [all_sum(): pl.pallas_call(functools.partial(allreduce_kernel, axes, groups), out_sha...]
    ppermute x3, starting transfers between devices: 11.1 us -> 17 us  [halo(): before = lax.ppermute(x[x.shape[0] - width:], 'sp', up)]
where the time goes in v3:
time: 128 us; the launch traced here: 127 us
  Pallas kernels  65.1 us (51%)
  starting transfers between devices  23.2 us (18%)
  local copies, waits for them, and re-layouts  15.6 us (12%)
  waiting for transfers between devices  12.9 us (10%)
  other arithmetic  9.42 us (7%)
    pallas_call x3, Pallas kernels, vmem_call(): pl.pallas_call(kernel, out_shape=outs, in_specs=specs, out_specs=[pl.Bloc...  33.5 us
    pallas_call x1, Pallas kernels, all_sum(): pl.pallas_call(functools.partial(allreduce_kernel, axes, groups), out_sha...  31.7 us
    ppermute x3, starting transfers between devices, halo(): before = lax.ppermute(x[x.shape[0] - width:], 'sp', up)  17 us
    ppermute x3, waiting for transfers between devices, halo(): after = lax.ppermute(x[:width], 'sp', down)  12.3 us
    ppermute x3, starting transfers between devices, halo(): after = lax.ppermute(x[:width], 'sp', down)  6.25 us
    unnamed x17, local copies, waits for them, and re-layouts  4.48 us
    concatenate x3, other arithmetic, halo(): return jnp.concatenate([before, x, after], axis=0)  3.77 us
  transfers between devices with their start and end apart: 6, of which 5 were waited for; matrix products, arithmetic and copies ran while one was open for 3% of the time, Pallas kernels for 0%

profile of v3, /device:TPU:1, one launch (start us, length us, event | category | flops | bytes accessed | tf_op | source)
XLA Modules:
  0.0 127.2 jit_solution(1325400775596711948)
XLA Ops:
  0.6 1.8 %reshape.47 = bf16[96,4,1024]{2,1,0:T(4,128)(2,1)S(1)} reshape(bf16[1,96,4,8,128]{4,3,2,1,0:T(8,128)(2,1)} %param.5) | data formatting | bytes 1572864 | tf_op jit(solution)/shard_map/reshape;squeeze | solution.py:273
  3.6 4.9 %collective-permute-start = (bf16[2,96,1024]{2,1,0:T(8,128)(2,1)}, bf16[2,96,1024]{2,1,0:T(8,128)(2,1)S(1)}, u32[]{:S(2)}, u32[]{:S(2)}) collective-permute-start(bf16[2,96,1024]{2,1,0:T(8,128)(2,1)} %get-tuple-element.42), channel_id=1, source_target_pairs={{0,4},{4,8},{8,12},{12,16},{16,20},{20,24},{24,28},{28,32},{32,36}... | collective-permute-start | bytes 1179656 | tf_op jit(solution)/shard_map/ppermute | solution.py:111
  8.6 1.9 %collective-permute-start.1 = (bf16[2,96,1024]{2,1,0:T(8,128)(2,1)}, bf16[2,96,1024]{2,1,0:T(8,128)(2,1)S(1)}, u32[]{:S(2)}, u32[]{:S(2)}) collective-permute-start(bf16[2,96,1024]{2,1,0:T(8,128)(2,1)} %get-tuple-element.43), channel_id=1, source_target_pairs={{4,0},{8,4},{12,8},{16,12},{20,16},{24,20},{28,24},{32,28},{36,32}... | collective-permute-start | bytes 1179656 | tf_op jit(solution)/shard_map/ppermute | solution.py:112
  11.5 1.1 copy.39
  13.6 4.3 %collective-permute-done.1 = bf16[2,96,1024]{2,1,0:T(8,128)(2,1)S(1)} collective-permute-done((bf16[2,96,1024]{2,1,0:T(8,128)(2,1)}, bf16[2,96,1024]{2,1,0:T(8,128)(2,1)S(1)}, u32[]{:S(2)}, u32[]{:S(2)}) %collective-permute-start.1) | collective-permute-done | bytes 393248 | tf_op jit(solution)/shard_map/ppermute | solution.py:112
  17.9 1.3 %pad_maximum_fusion.wide_ref = bf16[8,96,1024]{2,1,0:T(8,128)(2,1)} fusion(bf16[2,96,1024]{2,1,0:T(8,128)(2,1)S(1)} %collective-permute-done.1, bf16[4,96,1024]{2,1,0:T(8,128)(2,1)S(1)} %bitcast.32, bf16[2,96,1024]{2,1,0:T(8,128)(2,1)S(1)} %collective-permute-done), kind=kLoop, calls=%fused_computation | loop fusion | flops 1572864 | bytes 3145728 | tf_op jit(solution)/shard_map/concatenate | solution.py:113
  20.1 1.3 %broadcast_in_dim.4.kxy_ref = f32[2,9,96,128]{3,2,1,0:T(8,128)} broadcast(f32[2,9,96]{2,1,0:T(8,128)S(1)} %bitcast.41), dimensions={0,1,2} | broadcast | bytes 891648 | tf_op jit(solution)/shard_map/broadcast_in_dim | solution.py:275
  21.3 15.8 %shard_map.84 = (bf16[4,96,1024]{2,1,0:T(8,128)(2,1)}, f32[6,96,1024]{2,1,0:T(8,128)}, bf16[6,96,1024]{2,1,0:T(8,128)(2,1)}, f32[6,96,1024]{2,1,0:T(8,128)}, f32...) custom-call(f32[6]{0:T(128)} %and_convert_fusion.mask_ref, ...), custom_call_target="tpu_custom_call" | custom-call | tf_op jit(solution)/shard_map/pallas_call | solution.py:258
  37.1 1.1 fusion.1
  38.3 1.9 %collective-permute-start.2 = (bf16[1,96,1024]{2,1,0:T(8,128)(2,1)S(1)}, bf16[1,96,1024]{2,1,0:T(8,128)(2,1)S(1)}, u32[]{:S(2)}, u32[]{:S(2)}) collective-permute-start(bf16[1,96,1024]{2,1,0:T(8,128)(2,1)S(1)} %get-tuple-element.40), channel_id=1, source_target_pairs={{0,4},{4,8},{8,12},{12,16},{16,20},{20,24},{24,28},{28,32},{32,36}... | collective-permute-start | bytes 589832 | tf_op jit(solution)/shard_map/ppermute | solution.py:111
  40.2 2.4 %collective-permute-start.3 = (bf16[1,96,1024]{2,1,0:T(8,128)(2,1)S(1)}, bf16[1,96,1024]{2,1,0:T(8,128)(2,1)S(1)}, u32[]{:S(2)}, u32[]{:S(2)}) collective-permute-start(bf16[1,96,1024]{2,1,0:T(8,128)(2,1)S(1)} %get-tuple-element.41), channel_id=1, source_target_pairs={{4,0},{8,4},{12,8},{16,12},{20,16},{24,20},{28,24},{32,28},{36,32}... | collective-permute-start | bytes 589832 | tf_op jit(solution)/shard_map/ppermute | solution.py:112
  42.8 4.7 %collective-permute-done.3 = bf16[1,96,1024]{2,1,0:T(8,128)(2,1)S(1)} collective-permute-done((bf16[1,96,1024]{2,1,0:T(8,128)(2,1)S(1)}, bf16[1,96,1024]{2,1,0:T(8,128)(2,1)S(1)}, u32[]{:S(2)}, u32[]{:S(2)}) %collective-permute-start.3) | collective-permute-done | bytes 196640 | tf_op jit(solution)/shard_map/ppermute | solution.py:112
  47.5 1.3 pad_maximum_fusion.1.gp2_ref
  48.7 12.5 %shard_map.85 = (bf16[4,96,1024]{2,1,0:T(8,128)(2,1)}, f32[2,96,96]{2,1,0:T(8,128)}, f32[2,3,96,128]{3,2,1,0:T(8,128)}, f32[2,9,96,128]{3,2,1,0:T(8,128)}) custom-call(bf16[6,96,1024]{2,1,0:T(8,128)(2,1)} %pad_maximum_fusion.1.gp2_ref, bf16[8,96,1024]{2,1,0:T(8,128)(2,1)} %pad_maximum_fusion.wide_ref, f32[6,96,1024]{2,1,0:T(8,128)} %get-tuple-element.16.pre1_ref, ...), custom_call_target="tpu_custom_call" | custom-call | tf_op jit(solution)/shard_map/pallas_call | solution.py:258
  62.2 1.1 reduce_sum.19
  63.4 1.6 %reduce_sum.18 = f32[2,9,96]{2,1,0:T(8,128)S(1)} reduce(f32[2,9,96,128]{3,2,1,0:T(8,128)} %get-tuple-element.24, f32[]{:T(128)} %constant.7.clone.1), dimensions={3}, to_apply=%region_0.0 | reduce | flops 219456 | bytes 891652 | tf_op jit(solution)/shard_map/reduce_sum | solution.py:307
  66.4 31.7 %shard_map.87 = f32[168,128]{1,0:T(8,128)} custom-call(f32[168,128]{1,0:T(8,128)} %pad_bitcast_fusion.x_ref), custom_call_target="tpu_custom_call" | custom-call | tf_op jit(solution)/shard_map/pallas_call | solution.py:76
  101.3 10.1 %collective-permute-start.4 = (bf16[1,96,1024]{2,1,0:T(8,128)(2,1)S(1)}, bf16[1,96,1024]{2,1,0:T(8,128)(2,1)S(1)}, u32[]{:S(2)}, u32[]{:S(2)}) collective-permute-start(bf16[1,96,1024]{2,1,0:T(8,128)(2,1)S(1)} %get-tuple-element.38), channel_id=1, source_target_pairs={{0,4},{4,8},{8,12},{12,16},{16,20},{20,24},{24,28},{28,32},{32,36}... | collective-permute-start | bytes 589832 | tf_op jit(solution)/shard_map/ppermute | solution.py:111
  111.5 1.9 %collective-permute-start.5 = (bf16[1,96,1024]{2,1,0:T(8,128)(2,1)S(1)}, bf16[1,96,1024]{2,1,0:T(8,128)(2,1)S(1)}, u32[]{:S(2)}, u32[]{:S(2)}) collective-permute-start(bf16[1,96,1024]{2,1,0:T(8,128)(2,1)S(1)} %get-tuple-element.39), channel_id=1, source_target_pairs={{4,0},{8,4},{12,8},{16,12},{20,16},{24,20},{28,24},{32,28},{36,32}... | collective-permute-start | bytes 589832 | tf_op jit(solution)/shard_map/ppermute | solution.py:112
  115.2 3.3 %collective-permute-done.5 = bf16[1,96,1024]{2,1,0:T(8,128)(2,1)S(1)} collective-permute-done((bf16[1,96,1024]{2,1,0:T(8,128)(2,1)S(1)}, bf16[1,96,1024]{2,1,0:T(8,128)(2,1)S(1)}, u32[]{:S(2)}, u32[]{:S(2)}) %collective-permute-start.5) | collective-permute-done | bytes 196640 | tf_op jit(solution)/shard_map/ppermute | solution.py:112
  118.5 1.2 pad_maximum_fusion.2.gp1_ref
  119.6 5.2 %shard_map.86 = bf16[4,96,1024]{2,1,0:T(8,128)(2,1)} custom-call(bf16[6,96,1024]{2,1,0:T(8,128)(2,1)} %pad_maximum_fusion.2.gp1_ref, f32[2,9,96,128]{3,2,1,0:T(8,128)} %broadcast_in_dim.4.kxy_ref), custom_call_target="tpu_custom_call" | custom-call | tf_op jit(solution)/shard_map/pallas_call | solution.py:258
  124.8 1.3 %copy.35 = bf16[48,8,8,128]{3,2,1,0:T(8,128)(2,1)S(1)} copy(bf16[48,8,8,128]{3,1,2,0:T(8,128)(2,1)} %bitcast.34) | data formatting | bytes 1572864
  126.1 1.0 copy.30
  (41 shorter events, 11.5 us)
Async XLA Ops:
  2.6 7.9 %copy-start.5 = (bf16[2,96,3]{1,0,2:T(2,128)(2,1)S(1)}, bf16[2,96,3]{1,0,2:T(2,128)(2,1)}, u32[]{:S(2)}) copy-start(bf16[2,96,3]{1,0,2:T(2,128)(2,1)} %param.8) | copy-start | bytes 3460
  2.6 7.9 %copy-start.4 = (bf16[2,96,3,3]{1,0,3,2:T(2,128)(2,1)S(1)}, bf16[2,96,3,3]{1,0,3,2:T(2,128)(2,1)}, u32[]{:S(2)}) copy-start(bf16[2,96,3,3]{1,0,3,2:T(2,128)(2,1)} %param.7) | copy-start | bytes 10372
  2.7 7.9 %copy-start.3 = (bf16[2,96,96]{2,1,0:T(8,128)(2,1)S(1)}, bf16[2,96,96]{2,1,0:T(8,128)(2,1)}, u32[]{:S(2)}) copy-start(bf16[2,96,96]{2,1,0:T(8,128)(2,1)} %w_ref.3) | copy-start | bytes 110596
  2.7 8.6 %copy-start.2 = (bf16[1,96,4,8,128]{4,3,2,1,0:T(8,128)(2,1)S(1)}, bf16[1,96,4,8,128]{4,3,2,1,0:T(8,128)(2,1)}, u32[]{:S(2)}) copy-start(bf16[1,96,4,8,128]{4,3,2,1,0:T(8,128)(2,1)} %param.6) | copy-start | bytes 2359300
  3.6 9.9 %collective-permute-start = (bf16[2,96,1024]{2,1,0:T(8,128)(2,1)}, bf16[2,96,1024]{2,1,0:T(8,128)(2,1)S(1)}, u32[]{:S(2)}, u32[]{:S(2)}) collective-permute-start(bf16[2,96,1024]{2,1,0:T(8,128)(2,1)} %get-tuple-element.42), channel_id=1, source_target_pairs={{0,4},{4,8},{8,12},{12,16},{16,20},{20,24},{24,28},{28,32},{32,36}... | collective-permute-start | bytes 1179656 | tf_op jit(solution)/shard_map/ppermute | solution.py:111
  8.6 9.3 %collective-permute-start.1 = (bf16[2,96,1024]{2,1,0:T(8,128)(2,1)}, bf16[2,96,1024]{2,1,0:T(8,128)(2,1)S(1)}, u32[]{:S(2)}, u32[]{:S(2)}) collective-permute-start(bf16[2,96,1024]{2,1,0:T(8,128)(2,1)} %get-tuple-element.43), channel_id=1, source_target_pairs={{4,0},{8,4},{12,8},{16,12},{20,16},{24,20},{28,24},{32,28},{36,32}... | collective-permute-start | bytes 1179656 | tf_op jit(solution)/shard_map/ppermute | solution.py:112
  37.1 10.3 %copy-start.1 = (bf16[4,96,1024]{2,1,0:T(8,128)(2,1)S(1)}, bf16[4,96,1024]{2,1,0:T(8,128)(2,1)}, u32[]{:S(2)}) copy-start(bf16[4,96,1024]{2,1,0:T(8,128)(2,1)} %get-tuple-element.15) | copy-start | bytes 2359300
  38.3 4.5 %collective-permute-start.2 = (bf16[1,96,1024]{2,1,0:T(8,128)(2,1)S(1)}, bf16[1,96,1024]{2,1,0:T(8,128)(2,1)S(1)}, u32[]{:S(2)}, u32[]{:S(2)}) collective-permute-start(bf16[1,96,1024]{2,1,0:T(8,128)(2,1)S(1)} %get-tuple-element.40), channel_id=1, source_target_pairs={{0,4},{4,8},{8,12},{12,16},{16,20},{20,24},{24,28},{28,32},{32,36}... | collective-permute-start | bytes 589832 | tf_op jit(solution)/shard_map/ppermute | solution.py:111
  40.2 7.3 %collective-permute-start.3 = (bf16[1,96,1024]{2,1,0:T(8,128)(2,1)S(1)}, bf16[1,96,1024]{2,1,0:T(8,128)(2,1)S(1)}, u32[]{:S(2)}, u32[]{:S(2)}) collective-permute-start(bf16[1,96,1024]{2,1,0:T(8,128)(2,1)S(1)} %get-tuple-element.41), channel_id=1, source_target_pairs={{4,0},{8,4},{12,8},{16,12},{20,16},{24,20},{28,24},{32,28},{36,32}... | collective-permute-start | bytes 589832 | tf_op jit(solution)/shard_map/ppermute | solution.py:112
  63.3 38.0 %copy-start = (bf16[4,96,1024]{2,1,0:T(8,128)(2,1)S(1)}, bf16[4,96,1024]{2,1,0:T(8,128)(2,1)}, u32[]{:S(2)}) copy-start(bf16[4,96,1024]{2,1,0:T(8,128)(2,1)} %get-tuple-element.22) | copy-start | bytes 2359300
  101.3 13.8 %collective-permute-start.4 = (bf16[1,96,1024]{2,1,0:T(8,128)(2,1)S(1)}, bf16[1,96,1024]{2,1,0:T(8,128)(2,1)S(1)}, u32[]{:S(2)}, u32[]{:S(2)}) collective-permute-start(bf16[1,96,1024]{2,1,0:T(8,128)(2,1)S(1)} %get-tuple-element.38), channel_id=1, source_target_pairs={{0,4},{4,8},{8,12},{12,16},{16,20},{20,24},{24,28},{28,32},{32,36}... | collective-permute-start | bytes 589832 | tf_op jit(solution)/shard_map/ppermute | solution.py:111
  111.5 7.0 %collective-permute-start.5 = (bf16[1,96,1024]{2,1,0:T(8,128)(2,1)S(1)}, bf16[1,96,1024]{2,1,0:T(8,128)(2,1)S(1)}, u32[]{:S(2)}, u32[]{:S(2)}) collective-permute-start(bf16[1,96,1024]{2,1,0:T(8,128)(2,1)S(1)} %get-tuple-element.39), channel_id=1, source_target_pairs={{4,0},{8,4},{12,8},{16,12},{20,16},{24,20},{28,24},{32,28},{36,32}... | collective-permute-start | bytes 589832 | tf_op jit(solution)/shard_map/ppermute | solution.py:112

commit v4 on v3

--- a/solution.py
+++ b/solution.py
@@ -9,6 +9,7 @@
 from jax.sharding import PartitionSpec as P
 
 MESH = pl.DeviceIdType.MESH
+VMEM_LIMIT = 56 * 1024 * 1024
 
 
 def exchange_groups(axes, radix_bits):
@@ -20,7 +21,7 @@
     return [bits[i : i + radix_bits] for i in range(0, len(bits), radix_bits)]
 
 
-def allreduce_kernel(axes, groups, x_ref, o_ref, recv, acc, send_sem, recv_sem):
+def allreduce_kernel(axes, groups, x_ref, gp1_ref, kxy_ref, o_ref, vg_ref, recv, acc, send_sem, recv_sem):
     here = {name: lax.axis_index(name) for name, _ in axes}
     steps = []
     for group in groups:
@@ -56,6 +57,10 @@
             )
             copy.start()
             here_copies.append(copy)
+        planes = vg_ref.shape[0]
+        for q in range(g * planes // len(steps), (g + 1) * planes // len(steps)):
+            y, _ = coords(vg_ref.shape[1:])
+            vg_ref[q] = plane_conv([gp1_ref[q + i] for i in range(3)], kxy_ref, 0, True, y).astype(vg_ref.dtype)
         for copy in here_copies:
             copy.wait_recv()
         copies += here_copies
@@ -70,38 +75,42 @@
         copy.wait_send()
 
 
-def all_sum(flat, axes, radix_bits=2):
+def all_sum(flat, gp1, kxy, axes, radix_bits=2):
     groups = exchange_groups(axes, radix_bits)
     slots = sum((1 << len(g)) - 1 for g in groups)
+    own = gp1.shape[0] - 2
     return pl.pallas_call(
         functools.partial(allreduce_kernel, axes, groups),
-        out_shape=jax.ShapeDtypeStruct(flat.shape, flat.dtype),
-        in_specs=[pl.BlockSpec(memory_space=pltpu.VMEM)],
-        out_specs=pl.BlockSpec(memory_space=pltpu.VMEM),
+        out_shape=(
+            jax.ShapeDtypeStruct(flat.shape, flat.dtype),
+            jax.ShapeDtypeStruct((own,) + gp1.shape[1:], gp1.dtype),
+        ),
+        in_specs=[pl.BlockSpec(memory_space=pltpu.VMEM)] * 3,
+        out_specs=[pl.BlockSpec(memory_space=pltpu.VMEM)] * 2,
         scratch_shapes=[
             pltpu.VMEM((slots,) + flat.shape, flat.dtype),
             pltpu.VMEM((len(groups),) + flat.shape, flat.dtype),
             pltpu.SemaphoreType.DMA((slots,)),
             pltpu.SemaphoreType.DMA((slots,)),
         ],
-        compiler_params=pltpu.CompilerParams(collective_id=0, has_side_effects=True),
-    )(flat)
-
-
-def settle_all(*parts):
+        compiler_params=pltpu.CompilerParams(
+            collective_id=0, has_side_effects=True, vmem_limit_bytes=VMEM_LIMIT
+        ),
+    )(flat, gp1, kxy)
+
+
+def settle_all(parts, gp1, kxy):
     flat = jnp.concatenate([p.reshape(-1) for p in parts])
     rows = -(-flat.shape[0] // 1024) * 8
     flat = jnp.pad(flat, (0, rows * 128 - flat.shape[0])).reshape(rows, 128)
     axes = (("sp", lax.axis_size("sp")), ("dp", lax.axis_size("dp")))
-    flat = all_sum(flat, axes).reshape(-1)
+    flat, grad_in = all_sum(flat, gp1, kxy, axes)
+    flat = flat.reshape(-1)
     summed, at = [], 0
     for p in parts:
         summed.append(flat[at : at + p.size].reshape(p.shape))
         at += p.size
-    return summed
-
-
-VMEM_LIMIT = 56 * 1024 * 1024
+    return summed, grad_in
 
 
 def halo(x, width):
@@ -241,16 +250,6 @@
         return carry
 
     lax.fori_loop(0, own, block1, 0)
-
-
-def input_kernel(gp1_ref, kxy_ref, out_ref):
-    y, _ = coords(out_ref.shape[1:])
-
-    def plane(q, carry):
-        out_ref[q] = plane_conv([gp1_ref[q + i] for i in range(3)], kxy_ref, 0, True, y).astype(out_ref.dtype)
-        return carry
-
-    lax.fori_loop(0, out_ref.shape[0], plane, 0)
 
 
 def vmem_call(kernel, args, outs, scratch=(), smem=0, aliases=None):
@@ -301,11 +300,10 @@
         (plane(own, bf16), jax.ShapeDtypeStruct((2, chans, chans), f32),
          jax.ShapeDtypeStruct((2, 3, chans, 128), f32), jax.ShapeDtypeStruct((2, 9, chans, 128), f32)),
     )
-    grad_in = vmem_call(input_kernel, (halo(gp1, 1), kxy), (plane(own, bf16),))[0]
-    grad_in = grad_in.transpose(1, 0, 2).reshape(1, chans, own, depth, across)
     kz_sum = kzg.sum(axis=3).transpose(0, 2, 1)
     kxy_sum = kxyg.sum(axis=3).transpose(0, 2, 1).reshape(2, chans, 3, 3)
-    summed = settle_all(mix, kxy_sum, kz_sum)
+    summed, grad_in = settle_all((mix, kxy_sum, kz_sum), halo(gp1, 1), kxy)
+    grad_in = grad_in.transpose(1, 0, 2).reshape(1, chans, own, depth, across)
     factor = 1.0 / math.sqrt(lax.axis_size("dp") * own * ranks * depth * across)
     return (grad_in, summed[0] * factor, summed[1] * factor, summed[2] * factor)
 

time: 128 us -> 120 us (0.938)
  the two profiles are of different devices: /device:TPU:1 before, /device:TPU:32 now
where the time goes in v4:
time: 120 us
  Pallas kernels  70 us (58%)
  starting transfers between devices  17.8 us (15%)
  local copies, waits for them, and re-layouts  16.7 us (14%)
  other arithmetic  8.2 us (7%)
  waiting for transfers between devices  6.12 us (5%)
    pallas_call x1, Pallas kernels, all_sum(): pl.pallas_call(functools.partial(allreduce_kernel, axes, groups), out_sha...  41.7 us
    pallas_call x2, Pallas kernels, vmem_call(): pl.pallas_call(kernel, out_shape=outs, in_specs=specs, out_specs=[pl.Bloc...  28.2 us
    ppermute x3, starting transfers between devices, halo(): before = lax.ppermute(x[x.shape[0] - width:], 'sp', up)  10.1 us
    ppermute x3, starting transfers between devices, halo(): after = lax.ppermute(x[:width], 'sp', down)  7.66 us
    unnamed x19, local copies, waits for them, and re-layouts  4.5 us
    ppermute x3, waiting for transfers between devices, halo(): after = lax.ppermute(x[:width], 'sp', down)  3.9 us
    concatenate x3, other arithmetic, halo(): return jnp.concatenate([before, x, after], axis=0)  3.79 us
    slice x3, local copies, waits for them, and re-layouts, halo(): before = lax.ppermute(x[x.shape[0] - width:], 'sp', up)  3.2 us
  transfers between devices with their start and end apart: 6, of which 4 were waited for; matrix products, arithmetic and copies ran while one was open for 5% of the time, Pallas kernels for 0%

profile of v4, /device:TPU:32, one launch (start us, length us, event | category | flops | bytes accessed | tf_op | source)
XLA Modules:
  0.0 119.7 jit_solution(1177381486754849735)
XLA Ops:
  0.6 1.8 %reshape.47 = bf16[96,4,1024]{2,1,0:T(4,128)(2,1)S(1)} reshape(bf16[1,96,4,8,128]{4,3,2,1,0:T(8,128)(2,1)} %param.5) | data formatting | bytes 1572864 | tf_op jit(solution)/shard_map/reshape;squeeze | solution.py:272
  3.6 1.9 %collective-permute-start = (bf16[2,96,1024]{2,1,0:T(8,128)(2,1)}, bf16[2,96,1024]{2,1,0:T(8,128)(2,1)S(1)}, u32[]{:S(2)}, u32[]{:S(2)}) collective-permute-start(bf16[2,96,1024]{2,1,0:T(8,128)(2,1)} %get-tuple-element.46), channel_id=1, source_target_pairs={{0,4},{4,8},{8,12},{12,16},{16,20},{20,24},{24,28},{28,32},{32,36}... | collective-permute-start | bytes 1179656 | tf_op jit(solution)/shard_map/ppermute | solution.py:120
  5.5 3.6 %collective-permute-start.1 = (bf16[2,96,1024]{2,1,0:T(8,128)(2,1)}, bf16[2,96,1024]{2,1,0:T(8,128)(2,1)S(1)}, u32[]{:S(2)}, u32[]{:S(2)}) collective-permute-start(bf16[2,96,1024]{2,1,0:T(8,128)(2,1)} %get-tuple-element.47), channel_id=1, source_target_pairs={{4,0},{8,4},{12,8},{16,12},{20,16},{24,20},{28,24},{32,28},{36,32}... | collective-permute-start | bytes 1179656 | tf_op jit(solution)/shard_map/ppermute | solution.py:121
  10.2 1.1 copy.39
  11.8 1.1 collective-permute-done
  12.9 1.9 %collective-permute-done.1 = bf16[2,96,1024]{2,1,0:T(8,128)(2,1)S(1)} collective-permute-done((bf16[2,96,1024]{2,1,0:T(8,128)(2,1)}, bf16[2,96,1024]{2,1,0:T(8,128)(2,1)S(1)}, u32[]{:S(2)}, u32[]{:S(2)}) %collective-permute-start.1) | collective-permute-done | bytes 393248 | tf_op jit(solution)/shard_map/ppermute | solution.py:121
  14.8 1.4 %pad_maximum_fusion.wide_ref = bf16[8,96,1024]{2,1,0:T(8,128)(2,1)} fusion(bf16[2,96,1024]{2,1,0:T(8,128)(2,1)S(1)} %collective-permute-done.1, bf16[4,96,1024]{2,1,0:T(8,128)(2,1)S(1)} %bitcast.32, bf16[2,96,1024]{2,1,0:T(8,128)(2,1)S(1)} %collective-permute-done), kind=kLoop, calls=%fused_computation | loop fusion | flops 1572864 | bytes 3145728 | tf_op jit(solution)/shard_map/concatenate | solution.py:122
  17.0 1.3 %broadcast_in_dim.4.kxy_ref = f32[2,9,96,128]{3,2,1,0:T(8,128)} broadcast(f32[2,9,96]{2,1,0:T(8,128)S(1)} %bitcast.41), dimensions={0,1,2} | broadcast | bytes 891648 | tf_op jit(solution)/shard_map/broadcast_in_dim | solution.py:274
  18.3 15.8 %shard_map.84 = (bf16[4,96,1024]{2,1,0:T(8,128)(2,1)}, f32[6,96,1024]{2,1,0:T(8,128)}, bf16[6,96,1024]{2,1,0:T(8,128)(2,1)}, f32[6,96,1024]{2,1,0:T(8,128)}, f32...) custom-call(f32[6]{0:T(128)} %and_convert_fusion.mask_ref, ...), custom_call_target="tpu_custom_call" | custom-call | tf_op jit(solution)/shard_map/pallas_call | solution.py:257
  34.1 1.1 fusion.1
  35.2 4.0 %collective-permute-start.2 = (bf16[1,96,1024]{2,1,0:T(8,128)(2,1)S(1)}, bf16[1,96,1024]{2,1,0:T(8,128)(2,1)S(1)}, u32[]{:S(2)}, u32[]{:S(2)}) collective-permute-start(bf16[1,96,1024]{2,1,0:T(8,128)(2,1)S(1)} %get-tuple-element.44), channel_id=1, source_target_pairs={{0,4},{4,8},{8,12},{12,16},{16,20},{20,24},{24,28},{28,32},{32,36}... | collective-permute-start | bytes 589832 | tf_op jit(solution)/shard_map/ppermute | solution.py:120
  39.2 1.9 %collective-permute-start.3 = (bf16[1,96,1024]{2,1,0:T(8,128)(2,1)S(1)}, bf16[1,96,1024]{2,1,0:T(8,128)(2,1)S(1)}, u32[]{:S(2)}, u32[]{:S(2)}) collective-permute-start(bf16[1,96,1024]{2,1,0:T(8,128)(2,1)S(1)} %get-tuple-element.45), channel_id=1, source_target_pairs={{4,0},{8,4},{12,8},{16,12},{20,16},{24,20},{28,24},{32,28},{36,32}... | collective-permute-start | bytes 589832 | tf_op jit(solution)/shard_map/ppermute | solution.py:121
  41.1 1.1 collective-permute-done.2
  42.2 2.0 %collective-permute-done.3 = bf16[1,96,1024]{2,1,0:T(8,128)(2,1)S(1)} collective-permute-done((bf16[1,96,1024]{2,1,0:T(8,128)(2,1)S(1)}, bf16[1,96,1024]{2,1,0:T(8,128)(2,1)S(1)}, u32[]{:S(2)}, u32[]{:S(2)}) %collective-permute-start.3) | collective-permute-done | bytes 196640 | tf_op jit(solution)/shard_map/ppermute | solution.py:121
  44.3 1.3 %pad_maximum_fusion.1.gp2_ref = bf16[6,96,1024]{2,1,0:T(8,128)(2,1)} fusion(bf16[1,96,1024]{2,1,0:T(8,128)(2,1)S(1)} %collective-permute-done.3, bf16[4,96,1024]{2,1,0:T(8,128)(2,1)S(1)} %copy-done.1, bf16[1,96,1024]{2,1,0:T(8,128)(2,1)S(1)} %collective-permute-done.2), kind=kLoop, calls=%fused_computation.1 | loop fusion | flops 1179648 | bytes 2359296 | tf_op jit(solution)/shard_map/concatenate | solution.py:122
  45.5 12.5 %shard_map.85 = (bf16[4,96,1024]{2,1,0:T(8,128)(2,1)}, f32[2,96,96]{2,1,0:T(8,128)}, f32[2,3,96,128]{3,2,1,0:T(8,128)}, f32[2,9,96,128]{3,2,1,0:T(8,128)}) custom-call(bf16[6,96,1024]{2,1,0:T(8,128)(2,1)} %pad_maximum_fusion.1.gp2_ref, bf16[8,96,1024]{2,1,0:T(8,128)(2,1)} %pad_maximum_fusion.wide_ref, f32[6,96,1024]{2,1,0:T(8,128)} %get-tuple-element.18.pre1_ref, ...), custom_call_target="tpu_custom_call" | custom-call | tf_op jit(solution)/shard_map/pallas_call | solution.py:257
  58.0 1.1 fusion
  59.2 4.2 %collective-permute-start.4 = (bf16[1,96,1024]{2,1,0:T(8,128)(2,1)S(1)}, bf16[1,96,1024]{2,1,0:T(8,128)(2,1)S(1)}, u32[]{:S(2)}, u32[]{:S(2)}) collective-permute-start(bf16[1,96,1024]{2,1,0:T(8,128)(2,1)S(1)} %get-tuple-element.42), channel_id=1, source_target_pairs={{0,4},{4,8},{8,12},{12,16},{16,20},{20,24},{24,28},{28,32},{32,36}... | collective-permute-start | bytes 589832 | tf_op jit(solution)/shard_map/ppermute | solution.py:120
  63.4 2.1 %collective-permute-start.5 = (bf16[1,96,1024]{2,1,0:T(8,128)(2,1)S(1)}, bf16[1,96,1024]{2,1,0:T(8,128)(2,1)S(1)}, u32[]{:S(2)}, u32[]{:S(2)}) collective-permute-start(bf16[1,96,1024]{2,1,0:T(8,128)(2,1)S(1)} %get-tuple-element.43), channel_id=1, source_target_pairs={{4,0},{8,4},{12,8},{16,12},{20,16},{24,20},{28,24},{32,28},{36,32}... | collective-permute-start | bytes 589832 | tf_op jit(solution)/shard_map/ppermute | solution.py:121
  66.5 1.1 reduce_sum.19
  69.4 1.2 pad_maximum_fusion.2.gp1_ref
  70.6 41.7 %shard_map.86 = (f32[168,128]{1,0:T(8,128)}, bf16[4,96,1024]{2,1,0:T(8,128)(2,1)}) custom-call(f32[168,128]{1,0:T(8,128)} %pad_bitcast_fusion.x_ref, bf16[6,96,1024]{2,1,0:T(8,128)(2,1)} %pad_maximum_fusion.2.gp1_ref, f32[2,9,96,128]{3,2,1,0:T(8,128)} %broadcast_in_dim.4.kxy_ref), custom_call_target="tpu_custom_call" | custom-call | tf_op jit(solution)/shard_map/pallas_call | solution.py:82
  114.7 1.3 %copy.35 = bf16[48,8,8,128]{3,2,1,0:T(8,128)(2,1)S(1)} copy(bf16[48,8,8,128]{3,1,2,0:T(8,128)(2,1)} %bitcast.35) | data formatting | bytes 1572864
  116.0 1.0 copy.30
  (42 shorter events, 11.2 us)
Async XLA Ops:
  2.6 6.6 %copy-start.6 = (bf16[2,96,3]{1,0,2:T(2,128)(2,1)S(1)}, bf16[2,96,3]{1,0,2:T(2,128)(2,1)}, u32[]{:S(2)}) copy-start(bf16[2,96,3]{1,0,2:T(2,128)(2,1)} %param.8) | copy-start | bytes 3460
  2.6 6.6 %copy-start.5 = (bf16[2,96,3,3]{1,0,3,2:T(2,128)(2,1)S(1)}, bf16[2,96,3,3]{1,0,3,2:T(2,128)(2,1)}, u32[]{:S(2)}) copy-start(bf16[2,96,3,3]{1,0,3,2:T(2,128)(2,1)} %param.7) | copy-start | bytes 10372
  2.7 6.6 %copy-start.4 = (bf16[2,96,96]{2,1,0:T(8,128)(2,1)S(1)}, bf16[2,96,96]{2,1,0:T(8,128)(2,1)}, u32[]{:S(2)}) copy-start(bf16[2,96,96]{2,1,0:T(8,128)(2,1)} %w_ref.3) | copy-start | bytes 110596
  2.7 7.3 %copy-start.3 = (bf16[1,96,4,8,128]{4,3,2,1,0:T(8,128)(2,1)S(1)}, bf16[1,96,4,8,128]{4,3,2,1,0:T(8,128)(2,1)}, u32[]{:S(2)}) copy-start(bf16[1,96,4,8,128]{4,3,2,1,0:T(8,128)(2,1)} %param.6) | copy-start | bytes 2359300
  3.6 9.3 %collective-permute-start = (bf16[2,96,1024]{2,1,0:T(8,128)(2,1)}, bf16[2,96,1024]{2,1,0:T(8,128)(2,1)S(1)}, u32[]{:S(2)}, u32[]{:S(2)}) collective-permute-start(bf16[2,96,1024]{2,1,0:T(8,128)(2,1)} %get-tuple-element.46), channel_id=1, source_target_pairs={{0,4},{4,8},{8,12},{12,16},{16,20},{20,24},{24,28},{28,32},{32,36}... | collective-permute-start | bytes 1179656 | tf_op jit(solution)/shard_map/ppermute | solution.py:120
  5.5 9.2 %collective-permute-start.1 = (bf16[2,96,1024]{2,1,0:T(8,128)(2,1)}, bf16[2,96,1024]{2,1,0:T(8,128)(2,1)S(1)}, u32[]{:S(2)}, u32[]{:S(2)}) collective-permute-start(bf16[2,96,1024]{2,1,0:T(8,128)(2,1)} %get-tuple-element.47), channel_id=1, source_target_pairs={{4,0},{8,4},{12,8},{16,12},{20,16},{24,20},{28,24},{32,28},{36,32}... | collective-permute-start | bytes 1179656 | tf_op jit(solution)/shard_map/ppermute | solution.py:121
  34.1 10.2 %copy-start.1 = (bf16[4,96,1024]{2,1,0:T(8,128)(2,1)S(1)}, bf16[4,96,1024]{2,1,0:T(8,128)(2,1)}, u32[]{:S(2)}) copy-start(bf16[4,96,1024]{2,1,0:T(8,128)(2,1)} %get-tuple-element.17) | copy-start | bytes 2359300
  35.2 7.1 %collective-permute-start.2 = (bf16[1,96,1024]{2,1,0:T(8,128)(2,1)S(1)}, bf16[1,96,1024]{2,1,0:T(8,128)(2,1)S(1)}, u32[]{:S(2)}, u32[]{:S(2)}) collective-permute-start(bf16[1,96,1024]{2,1,0:T(8,128)(2,1)S(1)} %get-tuple-element.44), channel_id=1, source_target_pairs={{0,4},{4,8},{8,12},{12,16},{16,20},{20,24},{24,28},{28,32},{32,36}... | collective-permute-start | bytes 589832 | tf_op jit(solution)/shard_map/ppermute | solution.py:120
  39.2 5.1 %collective-permute-start.3 = (bf16[1,96,1024]{2,1,0:T(8,128)(2,1)S(1)}, bf16[1,96,1024]{2,1,0:T(8,128)(2,1)S(1)}, u32[]{:S(2)}, u32[]{:S(2)}) collective-permute-start(bf16[1,96,1024]{2,1,0:T(8,128)(2,1)S(1)} %get-tuple-element.45), channel_id=1, source_target_pairs={{4,0},{8,4},{12,8},{16,12},{20,16},{24,20},{28,24},{32,28},{36,32}... | collective-permute-start | bytes 589832 | tf_op jit(solution)/shard_map/ppermute | solution.py:121
  58.0 9.7 %copy-start.2 = (f32[2,9,96,128]{3,2,1,0:T(8,128)S(1)}, f32[2,9,96,128]{3,2,1,0:T(8,128)}, u32[]{:S(2)}) copy-start(f32[2,9,96,128]{3,2,1,0:T(8,128)} %get-tuple-element.25) | copy-start | bytes 2654212
  59.1 10.3 %copy-start = (bf16[4,96,1024]{2,1,0:T(8,128)(2,1)S(1)}, bf16[4,96,1024]{2,1,0:T(8,128)(2,1)}, u32[]{:S(2)}) copy-start(bf16[4,96,1024]{2,1,0:T(8,128)(2,1)} %get-tuple-element.27) | copy-start | bytes 2359300
  59.2 10.3 %collective-permute-start.4 = (bf16[1,96,1024]{2,1,0:T(8,128)(2,1)S(1)}, bf16[1,96,1024]{2,1,0:T(8,128)(2,1)S(1)}, u32[]{:S(2)}, u32[]{:S(2)}) collective-permute-start(bf16[1,96,1024]{2,1,0:T(8,128)(2,1)S(1)} %get-tuple-element.42), channel_id=1, source_target_pairs={{0,4},{4,8},{8,12},{12,16},{16,20},{20,24},{24,28},{28,32},{32,36}... | collective-permute-start | bytes 589832 | tf_op jit(solution)/shard_map/ppermute | solution.py:120
  63.4 6.0 %collective-permute-start.5 = (bf16[1,96,1024]{2,1,0:T(8,128)(2,1)S(1)}, bf16[1,96,1024]{2,1,0:T(8,128)(2,1)S(1)}, u32[]{:S(2)}, u32[]{:S(2)}) collective-permute-start(bf16[1,96,1024]{2,1,0:T(8,128)(2,1)S(1)} %get-tuple-element.43), channel_id=1, source_target_pairs={{4,0},{8,4},{12,8},{16,12},{20,16},{24,20},{28,24},{32,28},{36,32}... | collective-permute-start | bytes 589832 | tf_op jit(solution)/shard_map/ppermute | solution.py:121

commit v5 on v4

--- a/solution.py
+++ b/solution.py
@@ -21,7 +21,7 @@
     return [bits[i : i + radix_bits] for i in range(0, len(bits), radix_bits)]
 
 
-def allreduce_kernel(axes, groups, x_ref, gp1_ref, kxy_ref, o_ref, vg_ref, recv, acc, send_sem, recv_sem):
+def allreduce_kernel(axes, groups, x_ref, gp1_ref, kxy_ref, o_ref, vg_ref, recv, acc, edge, send_sem, recv_sem, edge_send, edge_recv):
     here = {name: lax.axis_index(name) for name, _ in axes}
     steps = []
     for group in groups:
@@ -34,13 +34,54 @@
                     where[name] = where[name] + stride * (1 - 2 * bit)
             partners.append(tuple(where[n] for n, _ in axes))
         steps.append(partners)
+    sp, last = here["sp"], axes[0][1] - 1
+    left = tuple(sp - 1 if n == "sp" else here[n] for n, _ in axes)
+    right = tuple(sp + 1 if n == "sp" else here[n] for n, _ in axes)
+    span = 1 << len(groups[0])
+    extra_left = (sp > 0) & (sp % span == 0)
+    extra_right = (sp < last) & (sp % span == span - 1)
     barrier = pltpu.get_barrier_semaphore()
     count = 0
     for partners in steps:
         for partner in partners:
             pl.semaphore_signal(barrier, inc=1, device_id=partner, device_id_type=MESH)
             count += 1
-    pl.semaphore_wait(barrier, count)
+
+    @pl.when(extra_left)
+    def _():
+        pl.semaphore_signal(barrier, inc=1, device_id=left, device_id_type=MESH)
+
+    @pl.when(extra_right)
+    def _():
+        pl.semaphore_signal(barrier, inc=1, device_id=right, device_id_type=MESH)
+
+    pl.semaphore_wait(barrier, count + extra_left.astype(jnp.int32) + extra_right.astype(jnp.int32))
+
+    own = vg_ref.shape[0]
+    to_left = pltpu.make_async_remote_copy(
+        src_ref=gp1_ref.at[0], dst_ref=edge.at[1], send_sem=edge_send.at[0], recv_sem=edge_recv.at[1],
+        device_id=left, device_id_type=MESH,
+    )
+    to_right = pltpu.make_async_remote_copy(
+        src_ref=gp1_ref.at[own - 1], dst_ref=edge.at[0], send_sem=edge_send.at[1], recv_sem=edge_recv.at[0],
+        device_id=right, device_id_type=MESH,
+    )
+
+    @pl.when(sp > 0)
+    def _():
+        to_left.start()
+
+    @pl.when(sp < last)
+    def _():
+        to_right.start()
+
+    y, _ = coords(vg_ref.shape[1:])
+
+    def conv_plane(q):
+        planes = [edge.at[0] if q == 0 else gp1_ref.at[q - 1], gp1_ref.at[q], edge.at[1] if q == own - 1 else gp1_ref.at[q + 1]]
+        vg_ref[q] = plane_conv([p[...] for p in planes], kxy_ref, 0, True, y).astype(vg_ref.dtype)
+
+    order = list(range(1, own - 1)) + [0, own - 1]
     src = x_ref
     copies = []
     slot = 0
@@ -57,10 +98,27 @@
             )
             copy.start()
             here_copies.append(copy)
-        planes = vg_ref.shape[0]
-        for q in range(g * planes // len(steps), (g + 1) * planes // len(steps)):
-            y, _ = coords(vg_ref.shape[1:])
-            vg_ref[q] = plane_conv([gp1_ref[q + i] for i in range(3)], kxy_ref, 0, True, y).astype(vg_ref.dtype)
+        todo = order[g * own // len(steps) : (g + 1) * own // len(steps)]
+        if 0 in todo:
+            @pl.when(sp > 0)
+            def _():
+                to_right.wait_recv()
+
+            @pl.when(sp == 0)
+            def _():
+                edge[0] = jnp.zeros(edge.shape[1:], edge.dtype)
+
+        if own - 1 in todo:
+            @pl.when(sp < last)
+            def _():
+                to_left.wait_recv()
+
+            @pl.when(sp == last)
+            def _():
+                edge[1] = jnp.zeros(edge.shape[1:], edge.dtype)
+
+        for q in todo:
+            conv_plane(q)
         for copy in here_copies:
             copy.wait_recv()
         copies += here_copies
@@ -74,11 +132,20 @@
     for copy in copies:
         copy.wait_send()
 
+    @pl.when(sp > 0)
+    def _():
+        to_left.wait_send()
+
+    @pl.when(sp < last)
+    def _():
+        to_right.wait_send()
+
 
 def all_sum(flat, gp1, kxy, axes, radix_bits=2):
     groups = exchange_groups(axes, radix_bits)
     slots = sum((1 << len(g)) - 1 for g in groups)
-    own = gp1.shape[0] - 2
+    own = gp1.shape[0]
+    assert own >= 2 and own % len(groups) == 0
     return pl.pallas_call(
         functools.partial(allreduce_kernel, axes, groups),
         out_shape=(
@@ -90,8 +157,11 @@
         scratch_shapes=[
             pltpu.VMEM((slots,) + flat.shape, flat.dtype),
             pltpu.VMEM((len(groups),) + flat.shape, flat.dtype),
+            pltpu.VMEM((2,) + gp1.shape[1:], gp1.dtype),
             pltpu.SemaphoreType.DMA((slots,)),
             pltpu.SemaphoreType.DMA((slots,)),
+            pltpu.SemaphoreType.DMA((2,)),
+            pltpu.SemaphoreType.DMA((2,)),
         ],
         compiler_params=pltpu.CompilerParams(
             collective_id=0, has_side_effects=True, vmem_limit_bytes=VMEM_LIMIT
@@ -302,7 +372,7 @@
     )
     kz_sum = kzg.sum(axis=3).transpose(0, 2, 1)
     kxy_sum = kxyg.sum(axis=3).transpose(0, 2, 1).reshape(2, chans, 3, 3)
-    summed, grad_in = settle_all((mix, kxy_sum, kz_sum), halo(gp1, 1), kxy)
+    summed, grad_in = settle_all((mix, kxy_sum, kz_sum), gp1, kxy)
     grad_in = grad_in.transpose(1, 0, 2).reshape(1, chans, own, depth, across)
     factor = 1.0 / math.sqrt(lax.axis_size("dp") * own * ranks * depth * across)
     return (grad_in, summed[0] * factor, summed[1] * factor, summed[2] * factor)

time: 120 us -> 114 us (0.950)
  the two profiles are of different devices: /device:TPU:32 before, /device:TPU:1 now
where the time goes in v5:
time: 114 us
  Pallas kernels  67.2 us (59%)
  local copies, waits for them, and re-layouts  15.4 us (14%)
  starting transfers between devices  11.2 us (10%)
  waiting for transfers between devices  9.62 us (8%)
  other arithmetic  9.3 us (8%)
    pallas_call x1, Pallas kernels, all_sum(): pl.pallas_call(functools.partial(allreduce_kernel, axes, groups), out_sha...  38.9 us
    pallas_call x2, Pallas kernels, vmem_call(): pl.pallas_call(kernel, out_shape=outs, in_specs=specs, out_specs=[pl.Bloc...  28.2 us
    ppermute x2, waiting for transfers between devices, halo(): after = lax.ppermute(x[:width], 'sp', down)  8.98 us
    ppermute x2, starting transfers between devices, halo(): before = lax.ppermute(x[x.shape[0] - width:], 'sp', up)  6.84 us
    unnamed x13, local copies, waits for them, and re-layouts  4.47 us
    ppermute x2, starting transfers between devices, halo(): after = lax.ppermute(x[:width], 'sp', down)  4.33 us
    concatenate x2, other arithmetic, halo(): return jnp.concatenate([before, x, after], axis=0)  3.73 us
    mul x3, other arithmetic, on_device(): return (grad_in, summed[0] * factor, summed[1] * factor, summed[2] * factor)  2.36 us
  transfers between devices with their start and end apart: 4, of which 4 were waited for; matrix products, arithmetic and copies ran while one was open for 2% of the time, Pallas kernels for 0%

profile of v5, /device:TPU:1, one launch (start us, length us, event | category | flops | bytes accessed | tf_op | source)
XLA Modules:
  0.0 113.6 jit_solution(3438414361819359819)
XLA Ops:
  0.6 1.8 %reshape.47 = bf16[96,4,1024]{2,1,0:T(4,128)(2,1)S(1)} reshape(bf16[1,96,4,8,128]{4,3,2,1,0:T(8,128)(2,1)} %param.5) | data formatting | bytes 1572864 | tf_op jit(solution)/shard_map/reshape;squeeze | solution.py:342
  2.7 0.9 fusion.1
  3.6 4.9 %collective-permute-start = (bf16[2,96,1024]{2,1,0:T(8,128)(2,1)}, bf16[2,96,1024]{2,1,0:T(8,128)(2,1)S(1)}, u32[]{:S(2)}, u32[]{:S(2)}) collective-permute-start(bf16[2,96,1024]{2,1,0:T(8,128)(2,1)} %get-tuple-element.44), channel_id=1, source_target_pairs={{0,4},{4,8},{8,12},{12,16},{16,20},{20,24},{24,28},{28,32},{32,36}... | collective-permute-start | bytes 1179656 | tf_op jit(solution)/shard_map/ppermute | solution.py:190
  8.5 1.9 %collective-permute-start.1 = (bf16[2,96,1024]{2,1,0:T(8,128)(2,1)}, bf16[2,96,1024]{2,1,0:T(8,128)(2,1)S(1)}, u32[]{:S(2)}, u32[]{:S(2)}) collective-permute-start(bf16[2,96,1024]{2,1,0:T(8,128)(2,1)} %get-tuple-element.45), channel_id=1, source_target_pairs={{4,0},{8,4},{12,8},{16,12},{20,16},{24,20},{28,24},{32,28},{36,32}... | collective-permute-start | bytes 1179656 | tf_op jit(solution)/shard_map/ppermute | solution.py:191
  11.5 1.1 copy.39
  13.6 4.3 %collective-permute-done.1 = bf16[2,96,1024]{2,1,0:T(8,128)(2,1)S(1)} collective-permute-done((bf16[2,96,1024]{2,1,0:T(8,128)(2,1)}, bf16[2,96,1024]{2,1,0:T(8,128)(2,1)S(1)}, u32[]{:S(2)}, u32[]{:S(2)}) %collective-permute-start.1) | collective-permute-done | bytes 393248 | tf_op jit(solution)/shard_map/ppermute | solution.py:191
  17.8 1.4 %pad_maximum_fusion.wide_ref = bf16[8,96,1024]{2,1,0:T(8,128)(2,1)} fusion(bf16[2,96,1024]{2,1,0:T(8,128)(2,1)S(1)} %collective-permute-done.1, bf16[4,96,1024]{2,1,0:T(8,128)(2,1)S(1)} %bitcast.32, bf16[2,96,1024]{2,1,0:T(8,128)(2,1)S(1)} %collective-permute-done), kind=kLoop, calls=%fused_computation | loop fusion | flops 1572864 | bytes 3145728 | tf_op jit(solution)/shard_map/concatenate | solution.py:192
  19.2 0.8 broadcast_in_dim.5.kz_ref
  20.0 1.3 %broadcast_in_dim.4.kxy_ref = f32[2,9,96,128]{3,2,1,0:T(8,128)} broadcast(f32[2,9,96]{2,1,0:T(8,128)S(1)} %bitcast.41), dimensions={0,1,2} | broadcast | bytes 891648 | tf_op jit(solution)/shard_map/broadcast_in_dim | solution.py:344
  21.4 15.8 %shard_map.84 = (bf16[4,96,1024]{2,1,0:T(8,128)(2,1)}, f32[6,96,1024]{2,1,0:T(8,128)}, bf16[6,96,1024]{2,1,0:T(8,128)(2,1)}, f32[6,96,1024]{2,1,0:T(8,128)}, f32...) custom-call(f32[6]{0:T(128)} %and_convert_fusion.mask_ref, ...), custom_call_target="tpu_custom_call" | custom-call | tf_op jit(solution)/shard_map/pallas_call | solution.py:327
  37.1 1.0 fusion
  38.2 1.9 %collective-permute-start.2 = (bf16[1,96,1024]{2,1,0:T(8,128)(2,1)S(1)}, bf16[1,96,1024]{2,1,0:T(8,128)(2,1)S(1)}, u32[]{:S(2)}, u32[]{:S(2)}) collective-permute-start(bf16[1,96,1024]{2,1,0:T(8,128)(2,1)S(1)} %get-tuple-element.42), channel_id=1, source_target_pairs={{0,4},{4,8},{8,12},{12,16},{16,20},{20,24},{24,28},{28,32},{32,36}... | collective-permute-start | bytes 589832 | tf_op jit(solution)/shard_map/ppermute | solution.py:190
  40.1 2.4 %collective-permute-start.3 = (bf16[1,96,1024]{2,1,0:T(8,128)(2,1)S(1)}, bf16[1,96,1024]{2,1,0:T(8,128)(2,1)S(1)}, u32[]{:S(2)}, u32[]{:S(2)}) collective-permute-start(bf16[1,96,1024]{2,1,0:T(8,128)(2,1)S(1)} %get-tuple-element.43), channel_id=1, source_target_pairs={{4,0},{8,4},{12,8},{16,12},{20,16},{24,20},{28,24},{32,28},{36,32}... | collective-permute-start | bytes 589832 | tf_op jit(solution)/shard_map/ppermute | solution.py:191
  42.7 4.7 %collective-permute-done.3 = bf16[1,96,1024]{2,1,0:T(8,128)(2,1)S(1)} collective-permute-done((bf16[1,96,1024]{2,1,0:T(8,128)(2,1)S(1)}, bf16[1,96,1024]{2,1,0:T(8,128)(2,1)S(1)}, u32[]{:S(2)}, u32[]{:S(2)}) %collective-permute-start.3) | collective-permute-done | bytes 196640 | tf_op jit(solution)/shard_map/ppermute | solution.py:191
  47.4 2.4 %pad_maximum_fusion.1.gp2_ref = bf16[6,96,1024]{2,1,0:T(8,128)(2,1)} fusion(bf16[1,96,1024]{2,1,0:T(8,128)(2,1)S(1)} %collective-permute-done.3, bf16[4,96,1024]{2,1,0:T(8,128)(2,1)} %get-tuple-element.17, bf16[1,96,1024]{2,1,0:T(8,128)(2,1)S(1)} %collective-permute-done.2), kind=kLoop, calls=%fused_computation.1 | loop fusion | flops 1179648 | bytes 2359296 | tf_op jit(solution)/shard_map/concatenate | solution.py:192
  49.8 12.5 %shard_map.85 = (bf16[4,96,1024]{2,1,0:T(8,128)(2,1)}, f32[2,96,96]{2,1,0:T(8,128)}, f32[2,3,96,128]{3,2,1,0:T(8,128)}, f32[2,9,96,128]{3,2,1,0:T(8,128)}) custom-call(bf16[6,96,1024]{2,1,0:T(8,128)(2,1)} %pad_maximum_fusion.1.gp2_ref, bf16[8,96,1024]{2,1,0:T(8,128)(2,1)} %pad_maximum_fusion.wide_ref, f32[6,96,1024]{2,1,0:T(8,128)} %get-tuple-element.18.pre1_ref, ...), custom_call_target="tpu_custom_call" | custom-call | tf_op jit(solution)/shard_map/pallas_call | solution.py:327
  62.2 1.0 reshape.41
  63.2 1.1 %reduce_sum.19 = f32[2,3,96]{2,1,0:T(4,128)S(1)} reduce(f32[2,3,96,128]{3,2,1,0:T(8,128)} %get-tuple-element.26, f32[]{:T(128)} %constant.7.clone.1), dimensions={3}, to_apply=%region_1.0 | reduce | flops 73152 | bytes 297220 | tf_op jit(solution)/shard_map/reduce_sum | solution.py:373
  64.4 1.5 %reduce_sum.18 = f32[2,9,96]{2,1,0:T(8,128)S(1)} reduce(f32[2,9,96,128]{3,2,1,0:T(8,128)} %get-tuple-element.25, f32[]{:T(128)} %constant.7.clone.1), dimensions={3}, to_apply=%region_0.0 | reduce | flops 219456 | bytes 891652 | tf_op jit(solution)/shard_map/reduce_sum | solution.py:374
  67.3 38.9 %shard_map.86 = (f32[168,128]{1,0:T(8,128)}, bf16[4,96,1024]{2,1,0:T(8,128)(2,1)}) custom-call(f32[168,128]{1,0:T(8,128)} %pad_bitcast_fusion.x_ref, bf16[4,96,1024]{2,1,0:T(8,128)(2,1)} %get-tuple-element.27.gp1_ref, f32[2,9,96,128]{3,2,1,0:T(8,128)} %broadcast_in_dim.4.kxy_ref), custom_call_target="tpu_custom_call" | custom-call | tf_op jit(solution)/shard_map/pallas_call | solution.py:149
  106.2 0.8 slice_multiply_fusion.2
  107.7 0.9 slice_multiply_fusion
  108.6 1.3 %copy.35 = bf16[48,8,8,128]{3,2,1,0:T(8,128)(2,1)S(1)} copy(bf16[48,8,8,128]{3,1,2,0:T(8,128)(2,1)} %bitcast.35) | data formatting | bytes 1572864
  109.9 1.0 copy.30
  (30 shorter events, 7.0 us)
Async XLA Ops:
  2.4 8.1 %copy-start.3 = (bf16[2,96,3]{1,0,2:T(2,128)(2,1)S(1)}, bf16[2,96,3]{1,0,2:T(2,128)(2,1)}, u32[]{:S(2)}) copy-start(bf16[2,96,3]{1,0,2:T(2,128)(2,1)} %param.8) | copy-start | bytes 3460
  2.4 8.1 %copy-start.2 = (bf16[2,96,3,3]{1,0,3,2:T(2,128)(2,1)S(1)}, bf16[2,96,3,3]{1,0,3,2:T(2,128)(2,1)}, u32[]{:S(2)}) copy-start(bf16[2,96,3,3]{1,0,3,2:T(2,128)(2,1)} %param.7) | copy-start | bytes 10372
  2.4 8.1 %copy-start.1 = (bf16[2,96,96]{2,1,0:T(8,128)(2,1)S(1)}, bf16[2,96,96]{2,1,0:T(8,128)(2,1)}, u32[]{:S(2)}) copy-start(bf16[2,96,96]{2,1,0:T(8,128)(2,1)} %w_ref.3) | copy-start | bytes 110596
  2.4 8.8 %copy-start = (bf16[1,96,4,8,128]{4,3,2,1,0:T(8,128)(2,1)S(1)}, bf16[1,96,4,8,128]{4,3,2,1,0:T(8,128)(2,1)}, u32[]{:S(2)}) copy-start(bf16[1,96,4,8,128]{4,3,2,1,0:T(8,128)(2,1)} %param.6) | copy-start | bytes 2359300
  3.6 9.9 %collective-permute-start = (bf16[2,96,1024]{2,1,0:T(8,128)(2,1)}, bf16[2,96,1024]{2,1,0:T(8,128)(2,1)S(1)}, u32[]{:S(2)}, u32[]{:S(2)}) collective-permute-start(bf16[2,96,1024]{2,1,0:T(8,128)(2,1)} %get-tuple-element.44), channel_id=1, source_target_pairs={{0,4},{4,8},{8,12},{12,16},{16,20},{20,24},{24,28},{28,32},{32,36}... | collective-permute-start | bytes 1179656 | tf_op jit(solution)/shard_map/ppermute | solution.py:190
  8.5 9.3 %collective-permute-start.1 = (bf16[2,96,1024]{2,1,0:T(8,128)(2,1)}, bf16[2,96,1024]{2,1,0:T(8,128)(2,1)S(1)}, u32[]{:S(2)}, u32[]{:S(2)}) collective-permute-start(bf16[2,96,1024]{2,1,0:T(8,128)(2,1)} %get-tuple-element.45), channel_id=1, source_target_pairs={{4,0},{8,4},{12,8},{16,12},{20,16},{24,20},{28,24},{32,28},{36,32}... | collective-permute-start | bytes 1179656 | tf_op jit(solution)/shard_map/ppermute | solution.py:191
  38.2 4.5 %collective-permute-start.2 = (bf16[1,96,1024]{2,1,0:T(8,128)(2,1)S(1)}, bf16[1,96,1024]{2,1,0:T(8,128)(2,1)S(1)}, u32[]{:S(2)}, u32[]{:S(2)}) collective-permute-start(bf16[1,96,1024]{2,1,0:T(8,128)(2,1)S(1)} %get-tuple-element.42), channel_id=1, source_target_pairs={{0,4},{4,8},{8,12},{12,16},{16,20},{20,24},{24,28},{28,32},{32,36}... | collective-permute-start | bytes 589832 | tf_op jit(solution)/shard_map/ppermute | solution.py:190
  40.1 7.3 %collective-permute-start.3 = (bf16[1,96,1024]{2,1,0:T(8,128)(2,1)S(1)}, bf16[1,96,1024]{2,1,0:T(8,128)(2,1)S(1)}, u32[]{:S(2)}, u32[]{:S(2)}) collective-permute-start(bf16[1,96,1024]{2,1,0:T(8,128)(2,1)S(1)} %get-tuple-element.43), channel_id=1, source_target_pairs={{4,0},{8,4},{12,8},{16,12},{20,16},{24,20},{28,24},{32,28},{36,32}... | collective-permute-start | bytes 589832 | tf_op jit(solution)/shard_map/ppermute | solution.py:191

commit v6 on v5

--- a/solution.py
+++ b/solution.py
@@ -183,15 +183,6 @@
     return summed, grad_in
 
 
-def halo(x, width):
-    count = lax.axis_size("sp")
-    up = [(i, i + 1) for i in range(count - 1)]
-    down = [(j, i) for i, j in up]
-    before = lax.ppermute(x[x.shape[0] - width :], "sp", up)
-    after = lax.ppermute(x[:width], "sp", down)
-    return jnp.concatenate([before, x, after], axis=0)
-
-
 def coords(shape):
     lane = lax.broadcasted_iota(jnp.int32, shape, 1)
     return jnp.bitwise_and(lane, 127), jnp.right_shift(lane, 7)
@@ -266,73 +257,112 @@
             kxyg_ref[b, i * 3 + j] += fold(gplf * at_y(src, j - 1, y))
 
 
-def upper_kernel(mask_ref, wide_ref, cot_ref, kxy_ref, kz_ref, w_ref, wt_ref,
-                 gp2_ref, pre1_ref, ax1_ref, pl1_ref, mix_ref, kzg_ref, kxyg_ref, h2_ref):
+def fused_kernel(mask_ref, vol_ref, cot_ref, kxy_ref, kz_ref, w_ref, wt_ref,
+                 gp1_ref, mix_ref, kzg_ref, kxyg_ref,
+                 wide, h2, pl1, ax1, pre1, gp2, in_send, in_recv, g_send, g_recv):
     own = cot_ref.shape[0]
     y, z = coords(cot_ref.shape[1:])
+    sp, last, dp = lax.axis_index("sp"), lax.axis_size("sp") - 1, lax.axis_index("dp")
+    left, right = (sp - 1, dp), (sp + 1, dp)
+    has_left, has_right = sp > 0, sp < last
+
+    barrier = pltpu.get_barrier_semaphore()
+
+    @pl.when(has_left)
+    def _():
+        pl.semaphore_signal(barrier, inc=1, device_id=left, device_id_type=MESH)
+
+    @pl.when(has_right)
+    def _():
+        pl.semaphore_signal(barrier, inc=1, device_id=right, device_id_type=MESH)
+
+    pl.semaphore_wait(barrier, has_left.astype(jnp.int32) + has_right.astype(jnp.int32))
+
+    def exchange(buf, first, count, send, recv, src, src_first):
+        to_left = pltpu.make_async_remote_copy(
+            src_ref=src.at[pl.ds(src_first, count)], dst_ref=buf.at[pl.ds(first + own, count)],
+            send_sem=send.at[0], recv_sem=recv.at[1], device_id=left, device_id_type=MESH,
+        )
+        to_right = pltpu.make_async_remote_copy(
+            src_ref=src.at[pl.ds(src_first + own - count, count)], dst_ref=buf.at[pl.ds(first - count, count)],
+            send_sem=send.at[1], recv_sem=recv.at[0], device_id=right, device_id_type=MESH,
+        )
+        pl.when(has_left)(to_left.start)
+        pl.when(has_right)(to_right.start)
+
+        def finish():
+            pl.when(has_left)(to_right.wait_recv)
+            pl.when(has_right)(to_left.wait_recv)
+            zeros = jnp.zeros((count,) + buf.shape[1:], buf.dtype)
+
+            @pl.when(sp == 0)
+            def _():
+                buf[pl.ds(first - count, count)] = zeros
+
+            @pl.when(sp == last)
+            def _():
+                buf[pl.ds(first + own, count)] = zeros
+
+        def drain():
+            pl.when(has_left)(to_left.wait_send)
+            pl.when(has_right)(to_right.wait_send)
+
+        return finish, drain
+
     mix_ref[...] = jnp.zeros_like(mix_ref)
     kzg_ref[...] = jnp.zeros_like(kzg_ref)
     kxyg_ref[...] = jnp.zeros_like(kxyg_ref)
 
-    def forward1(p, carry):
-        planar = plane_conv([wide_ref[p + i] for i in range(3)], kxy_ref, 0, False, y)
+    finish_in, drain_in = exchange(wide, 2, 2, in_send, in_recv, vol_ref, 0)
+    wide[pl.ds(2, own)] = vol_ref[...]
+
+    def forward1(p):
+        planar = plane_conv([wide[p + i] for i in range(3)], kxy_ref, 0, False, y)
         axial = depth_conv(planar, kz_ref, 0, False, z).astype(jnp.bfloat16)
         pre = jnp.dot(w_ref[0], axial, preferred_element_type=jnp.float32)
-        pl1_ref[p] = planar
-        ax1_ref[p] = axial
-        pre1_ref[p] = pre
-        h2_ref[p] = (pre * sigmoid(pre) * mask_ref[p]).astype(jnp.bfloat16)
-        return carry
-
-    lax.fori_loop(0, own + 2, forward1, 0)
-
-    def block2(q, carry):
-        around = [h2_ref[q + i] for i in range(3)]
+        pl1[p] = planar
+        ax1[p] = axial
+        pre1[p] = pre
+        h2[p] = (pre * sigmoid(pre) * mask_ref[p]).astype(jnp.bfloat16)
+
+    def block2(q):
+        around = [h2[q + i] for i in range(3)]
         planar = plane_conv(around, kxy_ref, 1, False, y)
         axial = depth_conv(planar, kz_ref, 1, False, z).astype(jnp.bfloat16)
         pre = jnp.dot(w_ref[1], axial, preferred_element_type=jnp.float32)
         gpre = silu_grad(cot_ref[q].astype(jnp.float32), pre)
         gax = jnp.dot(wt_ref[1], gpre, preferred_element_type=jnp.float32)
         gpl = depth_conv(gax, kz_ref, 1, True, z).astype(jnp.bfloat16)
-        gp2_ref[q] = gpl
+        gp2[q + 1] = gpl
         weight_grads(1, gpre, axial, gax, planar, gpl, around, mix_ref, kzg_ref, kxyg_ref, y, z)
-        return carry
-
-    lax.fori_loop(0, own, block2, 0)
-
-
-def lower_kernel(gp2_ref, wide_ref, pre1_ref, ax1_ref, pl1_ref, kxy_ref, kz_ref, w_ref, wt_ref, mix_in, kzg_in, kxyg_in,
-                 gp1_ref, mix_ref, kzg_ref, kxyg_ref):
-    own = gp1_ref.shape[0]
-    y, z = coords(gp1_ref.shape[1:])
-    mix_ref[...] = mix_in[...]
-    kzg_ref[...] = kzg_in[...]
-    kxyg_ref[...] = kxyg_in[...]
-
-    def block1(q, carry):
-        g1 = plane_conv([gp2_ref[q + i] for i in range(3)], kxy_ref, 1, True, y).astype(jnp.bfloat16)
-        gpre = silu_grad(g1.astype(jnp.float32), pre1_ref[q + 1])
+
+    def block1(q):
+        g1 = plane_conv([gp2[q + i] for i in range(3)], kxy_ref, 1, True, y).astype(jnp.bfloat16)
+        gpre = silu_grad(g1.astype(jnp.float32), pre1[q + 1])
         gax = jnp.dot(wt_ref[0], gpre, preferred_element_type=jnp.float32)
         gpl = depth_conv(gax, kz_ref, 0, True, z).astype(jnp.bfloat16)
         gp1_ref[q] = gpl
-        around = [wide_ref[q + 1 + i] for i in range(3)]
-        weight_grads(0, gpre, ax1_ref[q + 1], gax, pl1_ref[q + 1], gpl, around, mix_ref, kzg_ref, kxyg_ref, y, z)
-        return carry
-
-    lax.fori_loop(0, own, block1, 0)
-
-
-def vmem_call(kernel, args, outs, scratch=(), smem=0, aliases=None):
-    specs = [pl.BlockSpec(memory_space=pltpu.SMEM)] * smem + [pl.BlockSpec(memory_space=pltpu.VMEM)] * (len(args) - smem)
-    return pl.pallas_call(
-        kernel,
-        out_shape=outs,
-        in_specs=specs,
-        out_specs=[pl.BlockSpec(memory_space=pltpu.VMEM)] * len(outs),
-        scratch_shapes=list(scratch),
-        input_output_aliases=aliases or {},
-        compiler_params=pltpu.CompilerParams(vmem_limit_bytes=VMEM_LIMIT),
-    )(*args)
+        around = [wide[q + 1 + i] for i in range(3)]
+        weight_grads(0, gpre, ax1[q + 1], gax, pl1[q + 1], gpl, around, mix_ref, kzg_ref, kxyg_ref, y, z)
+
+    def run(body, lo, hi, place=lambda i: i):
+        def step(i, carry):
+            body(place(i))
+            return carry
+
+        lax.fori_loop(lo, hi, step, 0)
+
+    run(forward1, 2, own)
+    finish_in()
+    run(forward1, 0, 4, lambda i: i + (i // 2) * (own - 2))
+    run(block2, 0, 2, lambda i: i * (own - 1))
+    finish_g, drain_g = exchange(gp2, 1, 1, g_send, g_recv, gp2, 1)
+    run(block2, 1, own - 1)
+    run(block1, 1, own - 1)
+    finish_g()
+    run(block1, 0, 2, lambda i: i * (own - 1))
+    drain_in()
+    drain_g()
 
 
 def on_device(volume, cotangent, kernels_xy, kernels_z, mixing):
@@ -350,26 +380,29 @@
     place = lax.axis_index("sp")
     spots = place * own - 1 + jnp.arange(own + 2, dtype=jnp.int32)
     mask = ((spots >= 0) & (spots < own * ranks)).astype(f32)
-    wide = halo(vol, 2)
     plane = lambda n, t: jax.ShapeDtypeStruct((n, chans, lanes), t)
-    gp2, pre1, ax1, pl1, mix, kzg, kxyg = vmem_call(
-        upper_kernel,
-        (mask, wide, cot, kxy, kz, mixing, wt),
-        (
-            plane(own, bf16), plane(own + 2, f32), plane(own + 2, bf16), plane(own + 2, f32),
+    gp1, mix, kzg, kxyg = pl.pallas_call(
+        fused_kernel,
+        out_shape=(
+            plane(own, bf16),
             jax.ShapeDtypeStruct((2, chans, chans), f32),
             jax.ShapeDtypeStruct((2, 3, chans, 128), f32),
             jax.ShapeDtypeStruct((2, 9, chans, 128), f32),
         ),
-        scratch=[pltpu.VMEM((own + 2, chans, lanes), bf16)],
-        smem=1,
-    )
-    gp1, mix, kzg, kxyg = vmem_call(
-        lower_kernel,
-        (halo(gp2, 1), wide, pre1, ax1, pl1, kxy, kz, mixing, wt, mix, kzg, kxyg),
-        (plane(own, bf16), jax.ShapeDtypeStruct((2, chans, chans), f32),
-         jax.ShapeDtypeStruct((2, 3, chans, 128), f32), jax.ShapeDtypeStruct((2, 9, chans, 128), f32)),
-    )
+        in_specs=[pl.BlockSpec(memory_space=pltpu.SMEM)] + [pl.BlockSpec(memory_space=pltpu.VMEM)] * 6,
+        out_specs=[pl.BlockSpec(memory_space=pltpu.VMEM)] * 4,
+        scratch_shapes=[
+            pltpu.VMEM((own + 4, chans, lanes), bf16),
+            pltpu.VMEM((own + 2, chans, lanes), bf16),
+            pltpu.VMEM((own + 2, chans, lanes), f32),
+            pltpu.VMEM((own + 2, chans, lanes), bf16),
+            pltpu.VMEM((own + 2, chans, lanes), f32),
+            pltpu.VMEM((own + 2, chans, lanes), bf16),
+        ] + [pltpu.SemaphoreType.DMA((2,))] * 4,
+        compiler_params=pltpu.CompilerParams(
+            collective_id=1, has_side_effects=True, vmem_limit_bytes=VMEM_LIMIT
+        ),
+    )(mask, vol, cot, kxy, kz, mixing, wt)
     kz_sum = kzg.sum(axis=3).transpose(0, 2, 1)
     kxy_sum = kxyg.sum(axis=3).transpose(0, 2, 1).reshape(2, chans, 3, 3)
     summed, grad_in = settle_all((mix, kxy_sum, kz_sum), gp1, kxy)

time: 114 us -> 90.1 us (0.79)
  starting transfers between devices: 11.2 us -> 0 us
  waiting for transfers between devices: 9.62 us -> 0 us
  other arithmetic: 9.3 us -> 4.66 us
  Pallas kernels: 67.2 us -> 70.6 us
  local copies, waits for them, and re-layouts: 15.4 us -> 13.7 us
    ppermute x4 -> x0, starting transfers between devices: 11.2 us -> none  [the longest x2 6.84 us: halo(): before = lax.ppermute(x[x.shape[0] - width:], 'sp', up)]
    ppermute x4 -> x0, waiting for transfers between devices: 9.62 us -> none  [the longest x2 8.98 us: halo(): after = lax.ppermute(x[:width], 'sp', down)]
    concatenate x2 -> x0, other arithmetic: 3.73 us -> none  [halo(): return jnp.concatenate([before, x, after], axis=0)]
    pallas_call x1, Pallas kernels: 38.9 us -> 41.8 us  [all_sum(): pl.pallas_call(functools.partial(allreduce_kernel, axes, groups), out_sha...]
    mul x3, other arithmetic: 2.36 us -> 0.08 us  [on_device(): return (grad_in, summed[0] * factor, summed[1] * factor, summed[2] * factor)]
    slice x2 -> x0, local copies, waits for them, and re-layouts: 1.98 us -> none  [halo(): before = lax.ppermute(x[x.shape[0] - width:], 'sp', up)]
    transpose x0 -> x1, local copies, waits for them, and re-layouts: none -> 1.61 us  [on_device(): cot = cotangent[0].reshape(chans, own, lanes).transpose(1, 0, 2)]
    pallas_call x2 -> x1, Pallas kernels: 28.2 us -> 28.8 us  [on_device(): pl.pallas_call(fused_kernel, out_shape=(plane(own, bf16), jax.ShapeDtypeS...]
  transfers between devices with their start and end apart: 4 -> 0, of which waited for: 4 -> 0; matrix products, arithmetic and copies ran while one was open for 2% -> 0% of each run, Pallas kernels for 0% -> 0%
where the time goes in v6:
time: 90.1 us; the launch traced here: 89.7 us
  Pallas kernels  70.6 us (78%)
  local copies, waits for them, and re-layouts  13.7 us (15%)
  other arithmetic  4.66 us (5%)
    pallas_call x1, Pallas kernels, all_sum(): pl.pallas_call(functools.partial(allreduce_kernel, axes, groups), out_sha...  41.8 us
    pallas_call x1, Pallas kernels, on_device(): pl.pallas_call(fused_kernel, out_shape=(plane(own, bf16), jax.ShapeDtypeS...  28.8 us
    unnamed x11, local copies, waits for them, and re-layouts  4.46 us
    another operation x1, local copies, waits for them, and re-layouts, on_device(): vol = volume[0].reshape(chans, own, lanes).transpose(1, 0, 2)  1.82 us

profile of v6, /device:TPU:1, one launch (start us, length us, event | category | flops | bytes accessed | tf_op | source)
XLA Modules:
  0.0 89.7 jit_solution(260167413107478628)
XLA Ops:
  0.6 0.5 and_convert_fusion.mask_ref
  1.2 0.7 convert_bitcast_fusion
  1.9 0.7 bitcast_convert_fusion
  2.6 0.7 copy.27
  3.3 0.8 broadcast_in_dim.5.kz_ref
  4.1 1.8 %reshape.47 = bf16[96,4,1024]{2,1,0:T(4,128)(2,1)S(1)} reshape(bf16[1,96,4,8,128]{4,3,2,1,0:T(8,128)(2,1)} %param.5) | data formatting | bytes 1572864 | tf_op jit(solution)/shard_map/reshape;squeeze | solution.py:372
  6.0 0.2 reshape.48
  6.1 1.6 %copy_bitcast_fusion = (bf16[4,96,1024]{2,1,0:T(8,128)(2,1)}, bf16[4,96,1024]{2,1,0:T(8,128)(2,1)}) fusion(bf16[96,4,1024]{2,1,0:T(4,128)(2,1)S(1)} %reshape.48, bf16[96,4,1024]{2,1,0:T(4,128)(2,1)S(1)} %reshape.47), kind=kLoop, calls=%fused_computation | loop fusion | bytes 3145728 | tf_op jit(solution)/shard_map/transpose | solution.py:373
  7.8 1.2 %broadcast_in_dim.4.kxy_ref = f32[2,9,96,128]{3,2,1,0:T(8,128)} broadcast(f32[2,9,96]{2,1,0:T(8,128)S(1)} %bitcast.35), dimensions={0,1,2} | broadcast | bytes 891648 | tf_op jit(solution)/shard_map/broadcast_in_dim | solution.py:374
  9.0 28.8 %shard_map.84 = (bf16[4,96,1024]{2,1,0:T(8,128)(2,1)}, f32[2,96,96]{2,1,0:T(8,128)}, f32[2,3,96,128]{3,2,1,0:T(8,128)}, f32[2,9,96,128]{3,2,1,0:T(8,128)}) custom-call(f32[6]{0:T(128)} %and_convert_fusion.mask_ref, bf16[4,96,1024]{2,1,0:T(8,128)(2,1)} %get-tuple-element.29.vol_ref, bf16[4,96,1024]{2,1,0:T(8,128)(2,1)} %get-tuple-element.28.cot_ref, ...), custom_call_target="tpu_custom_call" | custom-call | tf_op jit(solution)/shard_map/pallas_call | solution.py:384
  37.8 1.0 %reshape.41 = f32[18432]{0:T(1024)S(1)} reshape(f32[2,96,96]{2,1,0:T(8,128)} %get-tuple-element.10) | data formatting | bytes 147456 | tf_op jit(solution)/shard_map/reshape | solution.py:173
  38.8 1.1 %reduce_sum.19 = f32[2,3,96]{2,1,0:T(4,128)S(1)} reduce(f32[2,3,96,128]{3,2,1,0:T(8,128)} %get-tuple-element.12, f32[]{:T(128)} %constant.7.clone.1), dimensions={3}, to_apply=%region_1.0 | reduce | flops 73152 | bytes 297220 | tf_op jit(solution)/shard_map/reduce_sum | solution.py:406
  39.9 1.5 %reduce_sum.18 = f32[2,9,96]{2,1,0:T(8,128)S(1)} reduce(f32[2,9,96,128]{3,2,1,0:T(8,128)} %get-tuple-element.11, f32[]{:T(128)} %constant.7.clone.1), dimensions={3}, to_apply=%region_0.0 | reduce | flops 219456 | bytes 891652 | tf_op jit(solution)/shard_map/reduce_sum | solution.py:407
  41.6 0.2 reshape_reshape.3
  41.9 0.2 reshape.42
  42.2 0.6 pad_bitcast_fusion.x_ref
  42.9 41.8 %shard_map.85 = (f32[168,128]{1,0:T(8,128)}, bf16[4,96,1024]{2,1,0:T(8,128)(2,1)}) custom-call(f32[168,128]{1,0:T(8,128)} %pad_bitcast_fusion.x_ref, bf16[4,96,1024]{2,1,0:T(8,128)(2,1)} %get-tuple-element.13.gp1_ref, f32[2,9,96,128]{3,2,1,0:T(8,128)} %broadcast_in_dim.4.kxy_ref), custom_call_target="tpu_custom_call" | custom-call | tf_op jit(solution)/shard_map/pallas_call | solution.py:149
  84.7 1.3 %copy.35 = bf16[48,8,8,128]{3,2,1,0:T(8,128)(2,1)S(1)} copy(bf16[48,8,8,128]{3,1,2,0:T(8,128)(2,1)} %bitcast.30) | data formatting | bytes 1572864
  86.0 1.0 %copy.30 = bf16[1,96,4,8,128]{4,3,2,1,0:T(8,128)(2,1)} copy(bf16[1,96,4,8,128]{4,3,1,2,0:T(8,128)(2,1)S(1)} %bitcast.29) | data formatting | bytes 1572864
  87.1 0.7 mul.33
  87.8 0.2 mul.39
  88.0 0.7 copy.32
  88.7 0.3 mul.36
  89.0 0.7 copy.31
  (14 shorter events, 0.4 us)
Async XLA Ops:
  0.6 1.9 %copy-start.1 = (bf16[2,96,96]{2,1,0:T(8,128)(2,1)S(1)}, bf16[2,96,96]{2,1,0:T(8,128)(2,1)}, u32[]{:S(2)}) copy-start(bf16[2,96,96]{2,1,0:T(8,128)(2,1)} %w_ref.1) | copy-start | bytes 110596
  4.1 1.8 %copy-start = (bf16[1,96,4,8,128]{4,3,2,1,0:T(8,128)(2,1)S(1)}, bf16[1,96,4,8,128]{4,3,2,1,0:T(8,128)(2,1)}, u32[]{:S(2)}) copy-start(bf16[1,96,4,8,128]{4,3,2,1,0:T(8,128)(2,1)} %param.6) | copy-start | bytes 2359300
  86.0 1.0 %copy-start.2 = (f32[168,128]{1,0:T(8,128)S(1)}, f32[168,128]{1,0:T(8,128)}, u32[]{:S(2)}) copy-start(f32[168,128]{1,0:T(8,128)} %get-tuple-element.15) | copy-start | bytes 258052

commit v7 on v6

v7 whole, which is shorter than its diff:
```python
import functools
import math

import jax
import jax.numpy as jnp
from jax import lax
from jax.experimental import pallas as pl
from jax.experimental.pallas import tpu as pltpu
from jax.sharding import PartitionSpec as P

MESH = pl.DeviceIdType.MESH
VMEM_LIMIT = 56 * 1024 * 1024


def exchange_groups(axes, radix_bits):
    bits = []
    for name, size in axes:
        assert size & (size - 1) == 0
        for b in range(size.bit_length() - 1):
            bits.append((name, 1 << b))
    return [bits[i : i + radix_bits] for i in range(0, len(bits), radix_bits)]


def coords(shape):
    lane = lax.broadcasted_iota(jnp.int32, shape, 1)
    return jnp.bitwise_and(lane, 127), jnp.right_shift(lane, 7)


def at_y(a, d, y):
    if d == 0:
        return a
    rolled = pltpu.roll(a, (-d) % a.shape[1], 1)
    return jnp.where((y + d >= 0) & (y + d < 128), rolled, 0.0)


def at_z(a, d, z):
    if d == 0:
        return a
    rolled = pltpu.roll(a, (-128 * d) % a.shape[1], 1)
    return jnp.where((z + d >= 0) & (z + d < a.shape[1] // 128), rolled, 0.0)


def widen(k, lanes):
    return jnp.concatenate([k] * (lanes // k.shape[1]), axis=1)


def fold(a):
    total = a[:, :128]
    for g in range(1, a.shape[1] // 128):
        total = total + a[:, g * 128 : (g + 1) * 128]
    return total


def sigmoid(u):
    return 1.0 / (1.0 + jnp.exp(-u))


def plane_conv(planes, k_ref, b, flip, y):
    lanes = planes[0].shape[1]
    total = None
    for i in range(3):
        src = planes[i].astype(jnp.float32)
        for j in range(3):
            tap = (2 - i) * 3 + (2 - j) if flip else i * 3 + j
            term = widen(k_ref[b, tap], lanes) * at_y(src, j - 1, y)
            total = term if total is None else total + term
    return total


def depth_conv(a, kz_ref, b, flip, z):
    lanes = a.shape[1]
    total = None
    for t in range(3):
        tap = 2 - t if flip else t
        term = widen(kz_ref[b, tap], lanes) * at_z(a, t - 1, z)
        total = term if total is None else total + term
    return total


def silu_grad(g, pre):
    s = sigmoid(pre)
    return (g * (s * (1.0 + pre * (1.0 - s)))).astype(jnp.bfloat16)


def weight_grads(b, gpre, ax, gax, pl, gpl, around, mix_ref, kzg_ref, kxyg_ref, y, z):
    mix_ref[b] += lax.dot_general(
        gpre, ax, (((1,), (1,)), ((), ())), preferred_element_type=jnp.float32
    )
    for t in range(3):
        kzg_ref[b, t] += fold(gax * at_z(pl, t - 1, z))
    gplf = gpl.astype(jnp.float32)
    for i in range(3):
        src = around[i].astype(jnp.float32)
        for j in range(3):
            kxyg_ref[b, i * 3 + j] += fold(gplf * at_y(src, j - 1, y))


def whole_kernel(axes, groups, factor, mask_ref, vol_ref, cot_ref, kxy_ref, kz_ref, w_ref, wt_ref,
                 vg_ref, sums_ref,
                 wide, h2, pl1, ax1, pre1, gp2, gp1, pay, mix_ref, kzg_ref, kxyg_ref, recv, acc,
                 in_send, in_recv, g_send, g_recv, e_send, e_recv, send_sem, recv_sem):
    own = cot_ref.shape[0]
    y, z = coords(cot_ref.shape[1:])
    here = {name: lax.axis_index(name) for name, _ in axes}
    steps = []
    for group in groups:
        partners = []
        for offset in range(1, 1 << len(group)):
            where = dict(here)
            for k, (name, stride) in enumerate(group):
                if (offset >> k) & 1:
                    bit = (where[name] // stride) % 2
                    where[name] = where[name] + stride * (1 - 2 * bit)
            partners.append(tuple(where[n] for n, _ in axes))
        steps.append(partners)
    sp, last, dp = here["sp"], axes[0][1] - 1, here["dp"]
    left, right = (sp - 1, dp), (sp + 1, dp)
    has_left, has_right = sp > 0, sp < last
    span = 1 << len(groups[0])
    extra_left = has_left & (sp % span == 0)
    extra_right = has_right & (sp % span == span - 1)

    barrier = pltpu.get_barrier_semaphore()
    count = 0
    for partners in steps:
        for partner in partners:
            pl.semaphore_signal(barrier, inc=1, device_id=partner, device_id_type=MESH)
            count += 1

    @pl.when(extra_left)
    def _():
        pl.semaphore_signal(barrier, inc=1, device_id=left, device_id_type=MESH)

    @pl.when(extra_right)
    def _():
        pl.semaphore_signal(barrier, inc=1, device_id=right, device_id_type=MESH)

    pl.semaphore_wait(barrier, count + extra_left.astype(jnp.int32) + extra_right.astype(jnp.int32))

    def exchange(buf, first, count, send, recv, src, src_first):
        to_left = pltpu.make_async_remote_copy(
            src_ref=src.at[pl.ds(src_first, count)], dst_ref=buf.at[pl.ds(first + own, count)],
            send_sem=send.at[0], recv_sem=recv.at[1], device_id=left, device_id_type=MESH,
        )
        to_right = pltpu.make_async_remote_copy(
            src_ref=src.at[pl.ds(src_first + own - count, count)], dst_ref=buf.at[pl.ds(first - count, count)],
            send_sem=send.at[1], recv_sem=recv.at[0], device_id=right, device_id_type=MESH,
        )
        pl.when(has_left)(to_left.start)
        pl.when(has_right)(to_right.start)

        def finish():
            pl.when(has_left)(to_right.wait_recv)
            pl.when(has_right)(to_left.wait_recv)
            zeros = jnp.zeros((count,) + buf.shape[1:], buf.dtype)

            @pl.when(sp == 0)
            def _():
                buf[pl.ds(first - count, count)] = zeros

            @pl.when(sp == last)
            def _():
                buf[pl.ds(first + own, count)] = zeros

        def drain():
            pl.when(has_left)(to_left.wait_send)
            pl.when(has_right)(to_right.wait_send)

        return finish, drain

    mix_ref[...] = jnp.zeros_like(mix_ref)
    kzg_ref[...] = jnp.zeros_like(kzg_ref)
    kxyg_ref[...] = jnp.zeros_like(kxyg_ref)

    finish_in, drain_in = exchange(wide, 2, 2, in_send, in_recv, vol_ref, 0)
    wide[pl.ds(2, own)] = vol_ref[...]

    def forward1(p):
        planar = plane_conv([wide[p + i] for i in range(3)], kxy_ref, 0, False, y)
        axial = depth_conv(planar, kz_ref, 0, False, z).astype(jnp.bfloat16)
        pre = jnp.dot(w_ref[0], axial, preferred_element_type=jnp.float32)
        pl1[p] = planar
        ax1[p] = axial
        pre1[p] = pre
        h2[p] = (pre * sigmoid(pre) * mask_ref[p]).astype(jnp.bfloat16)

    def block2(q):
        around = [h2[q + i] for i in range(3)]
        planar = plane_conv(around, kxy_ref, 1, False, y)
        axial = depth_conv(planar, kz_ref, 1, False, z).astype(jnp.bfloat16)
        pre = jnp.dot(w_ref[1], axial, preferred_element_type=jnp.float32)
        gpre = silu_grad(cot_ref[q].astype(jnp.float32), pre)
        gax = jnp.dot(wt_ref[1], gpre, preferred_element_type=jnp.float32)
        gpl = depth_conv(gax, kz_ref, 1, True, z).astype(jnp.bfloat16)
        gp2[q + 1] = gpl
        weight_grads(1, gpre, axial, gax, planar, gpl, around, mix_ref, kzg_ref, kxyg_ref, y, z)

    def block1(q):
        g1 = plane_conv([gp2[q + i] for i in range(3)], kxy_ref, 1, True, y).astype(jnp.bfloat16)
        gpre = silu_grad(g1.astype(jnp.float32), pre1[q + 1])
        gax = jnp.dot(wt_ref[0], gpre, preferred_element_type=jnp.float32)
        gpl = depth_conv(gax, kz_ref, 0, True, z).astype(jnp.bfloat16)
        gp1[q + 1] = gpl
        around = [wide[q + 1 + i] for i in range(3)]
        weight_grads(0, gpre, ax1[q + 1], gax, pl1[q + 1], gpl, around, mix_ref, kzg_ref, kxyg_ref, y, z)

    def run(body, lo, hi, place=lambda i: i):
        def step(i, carry):
            body(place(i))
            return carry

        lax.fori_loop(lo, hi, step, 0)

    run(forward1, 2, own)
    finish_in()
    run(forward1, 0, 4, lambda i: i + (i // 2) * (own - 2))
    run(block2, 0, 2, lambda i: i * (own - 1))
    finish_g, drain_g = exchange(gp2, 1, 1, g_send, g_recv, gp2, 1)
    run(block2, 1, own - 1)
    run(block1, 1, own - 1)
    finish_g()
    run(block1, 0, 2, lambda i: i * (own - 1))
    finish_e, drain_e = exchange(gp1, 1, 1, e_send, e_recv, gp1, 1)
    drain_in()
    drain_g()

    lane = lax.broadcasted_iota(jnp.int32, pay.shape[1:], 1)
    chans = pay.shape[1]
    for b in range(2):
        packed = jnp.zeros(pay.shape[1:], jnp.float32)
        packed = jnp.where(lane < chans, jnp.concatenate(
            [mix_ref[b], jnp.zeros((chans, pay.shape[2] - chans), jnp.float32)], axis=1), packed)
        for t in range(3):
            packed = jnp.where(lane == chans + t, jnp.sum(kzg_ref[b, t], axis=1, keepdims=True), packed)
        for t in range(9):
            packed = jnp.where(lane == chans + 3 + t, jnp.sum(kxyg_ref[b, t], axis=1, keepdims=True), packed)
        pay[b] = packed

    def conv_plane(q):
        vg_ref[q] = plane_conv([gp1[q + i] for i in range(3)], kxy_ref, 0, True, y).astype(vg_ref.dtype)

    order = list(range(1, own - 1)) + [0, own - 1]
    halo_done = False
    src = pay
    copies = []
    slot = 0
    for g, partners in enumerate(steps):
        here_copies = []
        for k, partner in enumerate(partners):
            copy = pltpu.make_async_remote_copy(
                src_ref=src,
                dst_ref=recv.at[slot + k],
                send_sem=send_sem.at[slot + k],
                recv_sem=recv_sem.at[slot + k],
                device_id=partner,
                device_id_type=MESH,
            )
            copy.start()
            here_copies.append(copy)
        todo = order[g * own // len(steps) : (g + 1) * own // len(steps)]
        if (0 in todo or own - 1 in todo) and not halo_done:
            finish_e()
            halo_done = True
        for q in todo:
            conv_plane(q)
        for copy in here_copies:
            copy.wait_recv()
        copies += here_copies
        vals = [src[...]] + [recv[slot + k] for k in range(len(partners))]
        while len(vals) > 1:
            vals = [vals[i] + vals[i + 1] for i in range(0, len(vals), 2)]
        if g == len(steps) - 1:
            sums_ref[...] = vals[0] * factor
        else:
            acc[g] = vals[0]
            src = acc.at[g]
        slot += len(partners)
    for copy in copies:
        copy.wait_send()
    drain_e()


def on_device(volume, cotangent, kernels_xy, kernels_z, mixing):
    _, chans, own, depth, across = volume.shape
    lanes = depth * across
    f32, bf16 = jnp.float32, jnp.bfloat16
    vol = volume[0].reshape(chans, own, lanes).transpose(1, 0, 2)
    cot = cotangent[0].reshape(chans, own, lanes).transpose(1, 0, 2)
    kxy = jnp.broadcast_to(
        kernels_xy.astype(f32).reshape(2, chans, 9).transpose(0, 2, 1)[..., None], (2, 9, chans, 128)
    )
    kz = jnp.broadcast_to(kernels_z.astype(f32).transpose(0, 2, 1)[..., None], (2, 3, chans, 128))
    wt = mixing.transpose(0, 2, 1)
    ranks = lax.axis_size("sp")
    place = lax.axis_index("sp")
    spots = place * own - 1 + jnp.arange(own + 2, dtype=jnp.int32)
    mask = ((spots >= 0) & (spots < own * ranks)).astype(f32)
    axes = (("sp", ranks), ("dp", lax.axis_size("dp")))
    groups = exchange_groups(axes, 2)
    slots = sum((1 << len(g)) - 1 for g in groups)
    assert own >= 2 and own % len(groups) == 0 and chans + 12 <= 128
    factor = 1.0 / math.sqrt(lax.axis_size("dp") * own * ranks * depth * across)
    planes = lambda n, t: pltpu.VMEM((n, chans, lanes), t)
    grad_in, sums = pl.pallas_call(
        functools.partial(whole_kernel, axes, groups, factor),
        out_shape=(
            jax.ShapeDtypeStruct((own, chans, lanes), bf16),
            jax.ShapeDtypeStruct((2, chans, 128), f32),
        ),
        in_specs=[pl.BlockSpec(memory_space=pltpu.SMEM)] + [pl.BlockSpec(memory_space=pltpu.VMEM)] * 6,
        out_specs=[pl.BlockSpec(memory_space=pltpu.VMEM)] * 2,
        scratch_shapes=[
            planes(own + 4, bf16),
            planes(own + 2, bf16),
            planes(own + 2, f32),
            planes(own + 2, bf16),
            planes(own + 2, f32),
            planes(own + 2, bf16),
            planes(own + 2, bf16),
            pltpu.VMEM((2, chans, 128), f32),
            pltpu.VMEM((2, chans, chans), f32),
            pltpu.VMEM((2, 3, chans, 128), f32),
            pltpu.VMEM((2, 9, chans, 128), f32),
            pltpu.VMEM((slots, 2, chans, 128), f32),
            pltpu.VMEM((len(groups), 2, chans, 128), f32),
        ] + [pltpu.SemaphoreType.DMA((2,))] * 6 + [pltpu.SemaphoreType.DMA((slots,))] * 2,
        compiler_params=pltpu.CompilerParams(
            collective_id=0, has_side_effects=True, vmem_limit_bytes=VMEM_LIMIT
        ),
    )(mask, vol, cot, kxy, kz, mixing, wt)
    grad_in = grad_in.transpose(1, 0, 2).reshape(1, chans, own, depth, across)
    mixing_grad = sums[:, :, :chans]
    z_grad = sums[:, :, chans : chans + 3]
    xy_grad = sums[:, :, chans + 3 : chans + 12].reshape(2, chans, 3, 3)
    return (grad_in, mixing_grad, xy_grad, z_grad)


def solution(mesh):
    return jax.shard_map(
        on_device,
        mesh=mesh,
        in_specs=(P("dp", None, "sp", None, None), P("dp", None, "sp", None, None), P(), P(), P()),
        out_specs=(P("dp", None, "sp", None, None), P(), P(), P()),
        check_vma=False,
    )
```

time: 90.1 us -> 81.8 us (0.908)
  local copies, waits for them, and re-layouts: 13.7 us -> 10.9 us
  other arithmetic: 4.66 us -> 1.89 us
  Pallas kernels: 70.6 us -> 68.1 us
    reduce_sum x2 -> x0, other arithmetic: 2.69 us -> none  [the longest x1 1.54 us: on_device(): kxy_sum = kxyg.sum(axis=3).transpose(0, 2, 1).reshape(2, chans, 3, 3)]
    pallas_call x2 -> x1, Pallas kernels: 70.6 us -> 68.1 us  [on_device(): pl.pallas_call(functools.partial(whole_kernel, axes, groups, factor), out...]
    reshape x3 -> x0, local copies, waits for them, and re-layouts: 1.85 us -> none  [the longest x2 1.2 us: settle_all(): flat = jnp.concatenate([p.reshape(-1) for p in parts])]
    mul x3 -> x0, local copies, waits for them, and re-layouts: 1.21 us -> none  [on_device(): return (grad_in, summed[0] * factor, summed[1] * factor, summed[2] * factor)]
where the time goes in v7:
time: 81.8 us; the launch traced here: 81.6 us
  Pallas kernels  68.1 us (83%)
  local copies, waits for them, and re-layouts  10.9 us (13%)
  other arithmetic  1.89 us (2%)
    pallas_call x1, Pallas kernels, on_device(): pl.pallas_call(functools.partial(whole_kernel, axes, groups, factor), out...  68.1 us
    unnamed x11, local copies, waits for them, and re-layouts  4.36 us
    another operation x1, local copies, waits for them, and re-layouts, on_device(): vol = volume[0].reshape(chans, own, lanes).transpose(1, 0, 2)  1.82 us
    transpose x1, local copies, waits for them, and re-layouts, on_device(): cot = cotangent[0].reshape(chans, own, lanes).transpose(1, 0, 2)  1.64 us

profile of v7, /device:TPU:1, one launch (start us, length us, event | category | flops | bytes accessed | tf_op | source)
XLA Modules:
  0.0 81.6 jit_solution(14439011882657216031)
XLA Ops:
  0.6 0.0 copy-start.2
  0.6 0.5 and_convert_fusion.mask_ref
  1.2 0.7 convert_bitcast_fusion
  1.9 0.7 bitcast_convert_fusion
  2.5 0.0 copy-done.2
  2.6 0.7 copy.21
  3.3 0.9 %broadcast_in_dim.5.kz_ref = f32[2,3,96,128]{3,2,1,0:T(8,128)} broadcast(f32[2,3,96]{2,1,0:T(4,128)S(1)} %copy.20), dimensions={0,1,2} | broadcast | bytes 297216 | tf_op jit(solution)/shard_map/broadcast_in_dim | solution.py:292
  4.1 0.0 copy-start.1
  4.1 1.8 %reshape.24 = bf16[96,4,1024]{2,1,0:T(4,128)(2,1)S(1)} reshape(bf16[1,96,4,8,128]{4,3,2,1,0:T(8,128)(2,1)} %param.5) | data formatting | bytes 1572864 | tf_op jit(solution)/shard_map/reshape;squeeze | solution.py:287
  6.0 0.0 copy-done.1
  6.0 0.2 reshape.25
  6.2 1.6 %copy_bitcast_fusion = (bf16[4,96,1024]{2,1,0:T(8,128)(2,1)}, bf16[4,96,1024]{2,1,0:T(8,128)(2,1)}) fusion(bf16[96,4,1024]{2,1,0:T(4,128)(2,1)S(1)} %reshape.25, bf16[96,4,1024]{2,1,0:T(4,128)(2,1)S(1)} %reshape.24), kind=kLoop, calls=%fused_computation | loop fusion | bytes 3145728 | tf_op jit(solution)/shard_map/transpose | solution.py:288
  7.8 1.2 %broadcast_in_dim.4.kxy_ref = f32[2,9,96,128]{3,2,1,0:T(8,128)} broadcast(f32[2,9,96]{2,1,0:T(8,128)S(1)} %bitcast.30), dimensions={0,1,2} | broadcast | bytes 891648 | tf_op jit(solution)/shard_map/broadcast_in_dim | solution.py:289
  9.0 68.1 %shard_map.84 = (bf16[4,96,1024]{2,1,0:T(8,128)(2,1)}, f32[2,96,128]{2,1,0:T(8,128)}) custom-call(f32[6]{0:T(128)} %and_convert_fusion.mask_ref, bf16[4,96,1024]{2,1,0:T(8,128)(2,1)} %get-tuple-element.17.vol_ref, bf16[4,96,1024]{2,1,0:T(8,128)(2,1)} %get-tuple-element.16.cot_ref, f32[2,9,96,128]{3,2,1,0:T(8,128)} %broadcast_in_dim.4.kxy_ref, ...), custom_call_target="tpu_custom_call" | custom-call | tf_op jit(solution)/shard_map/pallas_call | solution.py:304
  77.1 1.3 %copy.27 = bf16[48,8,8,128]{3,2,1,0:T(8,128)(2,1)S(1)} copy(bf16[48,8,8,128]{3,1,2,0:T(8,128)(2,1)} %bitcast.28) | data formatting | bytes 1572864
  78.4 0.0 copy-start
  78.4 1.0 %copy.23 = bf16[1,96,4,8,128]{4,3,2,1,0:T(8,128)(2,1)} copy(bf16[1,96,4,8,128]{4,3,1,2,0:T(8,128)(2,1)S(1)} %bitcast.26) | data formatting | bytes 1572864
  79.4 0.0 copy-done
  79.4 0.1 slice.11
  79.5 0.7 copy.24
  80.2 0.1 slice.10
  80.3 0.7 copy.22
  80.9 0.6 copy.33
  (2 shorter events, 0.0 us)
Async XLA Ops:
  0.6 1.9 %copy-start.2 = (bf16[2,96,96]{2,1,0:T(8,128)(2,1)S(1)}, bf16[2,96,96]{2,1,0:T(8,128)(2,1)}, u32[]{:S(2)}) copy-start(bf16[2,96,96]{2,1,0:T(8,128)(2,1)} %w_ref.1) | copy-start | bytes 110596
  4.1 1.8 %copy-start.1 = (bf16[1,96,4,8,128]{4,3,2,1,0:T(8,128)(2,1)S(1)}, bf16[1,96,4,8,128]{4,3,2,1,0:T(8,128)(2,1)}, u32[]{:S(2)}) copy-start(bf16[1,96,4,8,128]{4,3,2,1,0:T(8,128)(2,1)} %param.6) | copy-start | bytes 2359300
  78.4 1.0 %copy-start = (f32[2,96,128]{2,1,0:T(8,128)S(1)}, f32[2,96,128]{2,1,0:T(8,128)}, u32[]{:S(2)}) copy-start(f32[2,96,128]{2,1,0:T(8,128)} %get-tuple-element.7) | copy-start | bytes 294916

commit v8 on v7

--- a/solution.py
+++ b/solution.py
@@ -95,12 +95,19 @@
             kxyg_ref[b, i * 3 + j] += fold(gplf * at_y(src, j - 1, y))
 
 
-def whole_kernel(axes, groups, factor, mask_ref, vol_ref, cot_ref, kxy_ref, kz_ref, w_ref, wt_ref,
-                 vg_ref, sums_ref,
-                 wide, h2, pl1, ax1, pre1, gp2, gp1, pay, mix_ref, kzg_ref, kxyg_ref, recv, acc,
+def whole_kernel(axes, groups, factor, vol_hbm, cot_hbm, kxy_ref, kz_ref, w_ref, wt_ref,
+                 vg_hbm, sums_ref,
+                 wide, cot_ref, vg_ref, h2, pl1, ax1, pre1, gp2, gp1, pay, mix_ref, kzg_ref, kxyg_ref, recv, acc,
                  in_send, in_recv, g_send, g_recv, e_send, e_recv, send_sem, recv_sem):
     own = cot_ref.shape[0]
+    depth = vol_hbm.shape[2]
     y, z = coords(cot_ref.shape[1:])
+
+    def to_planes(raw, buf, first):
+        for x in range(own):
+            v = pltpu.einshape("czy->zcy", raw[:, x].astype(jnp.float32))
+            buf[first + x] = jnp.concatenate([v[k] for k in range(depth)], axis=1).astype(buf.dtype)
+
     here = {name: lax.axis_index(name) for name, _ in axes}
     steps = []
     for group in groups:
@@ -135,6 +142,8 @@
     def _():
         pl.semaphore_signal(barrier, inc=1, device_id=right, device_id_type=MESH)
 
+    to_planes(vol_hbm, wide, 2)
+    to_planes(cot_hbm, cot_ref, 0)
     pl.semaphore_wait(barrier, count + extra_left.astype(jnp.int32) + extra_right.astype(jnp.int32))
 
     def exchange(buf, first, count, send, recv, src, src_first):
@@ -172,8 +181,7 @@
     kzg_ref[...] = jnp.zeros_like(kzg_ref)
     kxyg_ref[...] = jnp.zeros_like(kxyg_ref)
 
-    finish_in, drain_in = exchange(wide, 2, 2, in_send, in_recv, vol_ref, 0)
-    wide[pl.ds(2, own)] = vol_ref[...]
+    finish_in, drain_in = exchange(wide, 2, 2, in_send, in_recv, wide, 2)
 
     def forward1(p):
         planar = plane_conv([wide[p + i] for i in range(3)], kxy_ref, 0, False, y)
@@ -182,7 +190,9 @@
         pl1[p] = planar
         ax1[p] = axial
         pre1[p] = pre
-        h2[p] = (pre * sigmoid(pre) * mask_ref[p]).astype(jnp.bfloat16)
+        spot = sp * own - 1 + p
+        inside = ((spot >= 0) & (spot < own * (last + 1))).astype(jnp.float32)
+        h2[p] = (pre * sigmoid(pre) * inside).astype(jnp.bfloat16)
 
     def block2(q):
         around = [h2[q + i] for i in range(3)]
@@ -236,8 +246,12 @@
             packed = jnp.where(lane == chans + 3 + t, jnp.sum(kxyg_ref[b, t], axis=1, keepdims=True), packed)
         pay[b] = packed
 
+
     def conv_plane(q):
         vg_ref[q] = plane_conv([gp1[q + i] for i in range(3)], kxy_ref, 0, True, y).astype(vg_ref.dtype)
+        v = vg_ref[q].astype(jnp.float32)
+        v = jnp.stack([v[:, k * 128 : (k + 1) * 128] for k in range(depth)], axis=0)
+        vg_hbm[:, q] = pltpu.einshape("zcy->czy", v).astype(vg_hbm.dtype)
 
     order = list(range(1, own - 1)) + [0, own - 1]
     halo_done = False
@@ -284,17 +298,12 @@
     _, chans, own, depth, across = volume.shape
     lanes = depth * across
     f32, bf16 = jnp.float32, jnp.bfloat16
-    vol = volume[0].reshape(chans, own, lanes).transpose(1, 0, 2)
-    cot = cotangent[0].reshape(chans, own, lanes).transpose(1, 0, 2)
     kxy = jnp.broadcast_to(
         kernels_xy.astype(f32).reshape(2, chans, 9).transpose(0, 2, 1)[..., None], (2, 9, chans, 128)
     )
     kz = jnp.broadcast_to(kernels_z.astype(f32).transpose(0, 2, 1)[..., None], (2, 3, chans, 128))
     wt = mixing.transpose(0, 2, 1)
     ranks = lax.axis_size("sp")
-    place = lax.axis_index("sp")
-    spots = place * own - 1 + jnp.arange(own + 2, dtype=jnp.int32)
-    mask = ((spots >= 0) & (spots < own * ranks)).astype(f32)
     axes = (("sp", ranks), ("dp", lax.axis_size("dp")))
     groups = exchange_groups(axes, 2)
     slots = sum((1 << len(g)) - 1 for g in groups)
@@ -304,13 +313,15 @@
     grad_in, sums = pl.pallas_call(
         functools.partial(whole_kernel, axes, groups, factor),
         out_shape=(
-            jax.ShapeDtypeStruct((own, chans, lanes), bf16),
+            jax.ShapeDtypeStruct((chans, own, depth, across), bf16),
             jax.ShapeDtypeStruct((2, chans, 128), f32),
         ),
-        in_specs=[pl.BlockSpec(memory_space=pltpu.SMEM)] + [pl.BlockSpec(memory_space=pltpu.VMEM)] * 6,
+        in_specs=[pl.BlockSpec(memory_space=pltpu.VMEM)] * 6,
         out_specs=[pl.BlockSpec(memory_space=pltpu.VMEM)] * 2,
         scratch_shapes=[
             planes(own + 4, bf16),
+            planes(own, bf16),
+            planes(own, bf16),
             planes(own + 2, bf16),
             planes(own + 2, f32),
             planes(own + 2, bf16),
@@ -327,8 +338,8 @@
         compiler_params=pltpu.CompilerParams(
             collective_id=0, has_side_effects=True, vmem_limit_bytes=VMEM_LIMIT
         ),
-    )(mask, vol, cot, kxy, kz, mixing, wt)
-    grad_in = grad_in.transpose(1, 0, 2).reshape(1, chans, own, depth, across)
+    )(volume[0], cotangent[0], kxy, kz, mixing, wt)
+    grad_in = grad_in[None]
     mixing_grad = sums[:, :, :chans]
     z_grad = sums[:, :, chans : chans + 3]
     xy_grad = sums[:, :, chans + 3 : chans + 12].reshape(2, chans, 3, 3)

time: 81.8 us -> 78.5 us (0.960)
  local copies, waits for them, and re-layouts: 10.9 us -> 8.14 us
    another operation x2 -> x0, local copies, waits for them, and re-layouts: 2 us -> none  [the longest x1 1.82 us: on_device(): vol = volume[0].reshape(chans, own, lanes).transpose(1, 0, 2)]
    transpose x1 -> x0, local copies, waits for them, and re-layouts: 1.64 us -> none  [on_device(): cot = cotangent[0].reshape(chans, own, lanes).transpose(1, 0, 2)]
    slice x1, local copies, waits for them, and re-layouts: 0.08 us -> 0.97 us  [on_device(): z_grad = sums[:, :, chans:chans + 3]]
    unnamed x11 -> x8, local copies, waits for them, and re-layouts: 4.36 us -> 4.32 us
where the time goes in v8:
time: 78.5 us; the launch traced here: 78.2 us
  Pallas kernels  68 us (87%)
  local copies, waits for them, and re-layouts  8.14 us (10%)
  other arithmetic  1.39 us (2%)
    pallas_call x1, Pallas kernels, on_device(): pl.pallas_call(functools.partial(whole_kernel, axes, groups, factor), out...  68 us
    unnamed x8, local copies, waits for them, and re-layouts  4.32 us

profile of v8, /device:TPU:1, one launch (start us, length us, event | category | flops | bytes accessed | tf_op | source)
XLA Modules:
  0.0 78.2 jit_solution(4485773163850561672)
XLA Ops:
  0.6 0.0 copy-start.1
  0.6 0.7 convert_bitcast_fusion
  1.3 0.7 bitcast_convert_fusion
  2.0 0.0 copy-done.1
  2.0 0.7 copy.16
  2.8 0.9 %broadcast_in_dim.7.kz_ref = f32[2,3,96,128]{3,2,1,0:T(8,128)} broadcast(f32[2,3,96]{2,1,0:T(4,128)S(1)} %copy.15), dimensions={0,1,2} | broadcast | bytes 297216 | tf_op jit(solution)/shard_map/broadcast_in_dim | solution.py:304
  3.6 1.2 %broadcast_in_dim.6.kxy_ref = f32[2,9,96,128]{3,2,1,0:T(8,128)} broadcast(f32[2,9,96]{2,1,0:T(8,128)S(1)} %bitcast.19), dimensions={0,1,2} | broadcast | bytes 891648 | tf_op jit(solution)/shard_map/broadcast_in_dim | solution.py:301
  4.8 68.0 %shard_map.84 = (bf16[96,4,8,128]{3,2,1,0:T(8,128)(2,1)}, f32[2,96,128]{2,1,0:T(8,128)}) custom-call(bf16[96,4,8,128]{3,2,1,0:T(8,128)(2,1)} %bitcast.16, bf16[96,4,8,128]{3,2,1,0:T(8,128)(2,1)} %bitcast.17, f32[2,9,96,128]{3,2,1,0:T(8,128)} %broadcast_in_dim.6.kxy_ref, f32[2,3,96,128]{3,2,1,0:T(8,128)} %broadcast_in_dim.7.kz_ref, bf16[2,96,96]{2,1,0:T(8,128)(2,1)} %w_ref.1, ...), custom_call_target="tpu_custom_call" | custom-call | tf_op jit(solution)/shard_map/pallas_call | solution.py:313
  72.9 1.0 %slice.11 = f32[2,96,3]{2,1,0:T(8,128)S(1)} slice(f32[2,96,128]{2,1,0:T(8,128)} %get-tuple-element.7), slice={[0:2], [0:96], [96:99]} | slice | bytes 4608 | tf_op jit(solution)/shard_map/slice | solution.py:344
  73.9 0.0 copy-start
  73.9 0.7 copy.18
  74.5 0.2 copy-done
  74.8 0.1 slice.10
  74.8 0.7 copy.17
  75.5 2.1 %copy.23 = bf16[1,96,4,8,128]{4,3,2,1,0:T(8,128)(2,1)} copy(bf16[1,96,4,8,128]{4,3,2,1,0:T(8,128)(2,1)} %bitcast.15) | data formatting | bytes 1572864
  77.6 0.6 copy.24
  (2 shorter events, 0.0 us)
Async XLA Ops:
  0.6 1.4 %copy-start.1 = (bf16[2,96,96]{2,1,0:T(8,128)(2,1)S(1)}, bf16[2,96,96]{2,1,0:T(8,128)(2,1)}, u32[]{:S(2)}) copy-start(bf16[2,96,96]{2,1,0:T(8,128)(2,1)} %w_ref.1) | copy-start | bytes 110596
  73.9 0.9 %copy-start = (f32[2,96,128]{2,1,0:T(8,128)S(1)}, f32[2,96,128]{2,1,0:T(8,128)}, u32[]{:S(2)}) copy-start(f32[2,96,128]{2,1,0:T(8,128)} %get-tuple-element.7) | copy-start | bytes 294916

commit v9 on v8

--- a/solution.py
+++ b/solution.py
@@ -41,7 +41,7 @@
 
 
 def widen(k, lanes):
-    return jnp.concatenate([k] * (lanes // k.shape[1]), axis=1)
+    return jnp.broadcast_to(k, (k.shape[0], lanes))
 
 
 def fold(a):
@@ -62,7 +62,7 @@
         src = planes[i].astype(jnp.float32)
         for j in range(3):
             tap = (2 - i) * 3 + (2 - j) if flip else i * 3 + j
-            term = widen(k_ref[b, tap], lanes) * at_y(src, j - 1, y)
+            term = widen(k_ref[b, :, tap : tap + 1], lanes) * at_y(src, j - 1, y)
             total = term if total is None else total + term
     return total
 
@@ -72,7 +72,7 @@
     total = None
     for t in range(3):
         tap = 2 - t if flip else t
-        term = widen(kz_ref[b, tap], lanes) * at_z(a, t - 1, z)
+        term = widen(kz_ref[b, :, 9 + tap : 10 + tap], lanes) * at_z(a, t - 1, z)
         total = term if total is None else total + term
     return total
 
@@ -95,12 +95,13 @@
             kxyg_ref[b, i * 3 + j] += fold(gplf * at_y(src, j - 1, y))
 
 
-def whole_kernel(axes, groups, factor, vol_hbm, cot_hbm, kxy_ref, kz_ref, w_ref, wt_ref,
+def whole_kernel(axes, groups, factor, vol_hbm, cot_hbm, kxy_ref, w_ref,
                  vg_hbm, sums_ref,
                  wide, cot_ref, vg_ref, h2, pl1, ax1, pre1, gp2, gp1, pay, mix_ref, kzg_ref, kxyg_ref, recv, acc,
                  in_send, in_recv, g_send, g_recv, e_send, e_recv, send_sem, recv_sem):
     own = cot_ref.shape[0]
     depth = vol_hbm.shape[2]
+    kz_ref = kxy_ref
     y, z = coords(cot_ref.shape[1:])
 
     def to_planes(raw, buf, first):
@@ -200,7 +201,7 @@
         axial = depth_conv(planar, kz_ref, 1, False, z).astype(jnp.bfloat16)
         pre = jnp.dot(w_ref[1], axial, preferred_element_type=jnp.float32)
         gpre = silu_grad(cot_ref[q].astype(jnp.float32), pre)
-        gax = jnp.dot(wt_ref[1], gpre, preferred_element_type=jnp.float32)
+        gax = lax.dot_general(w_ref[1], gpre, (((0,), (0,)), ((), ())), preferred_element_type=jnp.float32)
         gpl = depth_conv(gax, kz_ref, 1, True, z).astype(jnp.bfloat16)
         gp2[q + 1] = gpl
         weight_grads(1, gpre, axial, gax, planar, gpl, around, mix_ref, kzg_ref, kxyg_ref, y, z)
@@ -208,7 +209,7 @@
     def block1(q):
         g1 = plane_conv([gp2[q + i] for i in range(3)], kxy_ref, 1, True, y).astype(jnp.bfloat16)
         gpre = silu_grad(g1.astype(jnp.float32), pre1[q + 1])
-        gax = jnp.dot(wt_ref[0], gpre, preferred_element_type=jnp.float32)
+        gax = lax.dot_general(w_ref[0], gpre, (((0,), (0,)), ((), ())), preferred_element_type=jnp.float32)
         gpl = depth_conv(gax, kz_ref, 0, True, z).astype(jnp.bfloat16)
         gp1[q + 1] = gpl
         around = [wide[q + 1 + i] for i in range(3)]
@@ -298,11 +299,9 @@
     _, chans, own, depth, across = volume.shape
     lanes = depth * across
     f32, bf16 = jnp.float32, jnp.bfloat16
-    kxy = jnp.broadcast_to(
-        kernels_xy.astype(f32).reshape(2, chans, 9).transpose(0, 2, 1)[..., None], (2, 9, chans, 128)
-    )
-    kz = jnp.broadcast_to(kernels_z.astype(f32).transpose(0, 2, 1)[..., None], (2, 3, chans, 128))
-    wt = mixing.transpose(0, 2, 1)
+    taps = jnp.concatenate(
+        [kernels_xy.reshape(2, chans, 9), kernels_z], axis=2
+    ).astype(f32)
     ranks = lax.axis_size("sp")
     axes = (("sp", ranks), ("dp", lax.axis_size("dp")))
     groups = exchange_groups(axes, 2)
@@ -316,7 +315,7 @@
             jax.ShapeDtypeStruct((chans, own, depth, across), bf16),
             jax.ShapeDtypeStruct((2, chans, 128), f32),
         ),
-        in_specs=[pl.BlockSpec(memory_space=pltpu.VMEM)] * 6,
+        in_specs=[pl.BlockSpec(memory_space=pltpu.VMEM)] * 4,
         out_specs=[pl.BlockSpec(memory_space=pltpu.VMEM)] * 2,
         scratch_shapes=[
             planes(own + 4, bf16),
@@ -338,7 +337,7 @@
         compiler_params=pltpu.CompilerParams(
             collective_id=0, has_side_effects=True, vmem_limit_bytes=VMEM_LIMIT
         ),
-    )(volume[0], cotangent[0], kxy, kz, mixing, wt)
+    )(volume[0], cotangent[0], taps, mixing)
     grad_in = grad_in[None]
     mixing_grad = sums[:, :, :chans]
     z_grad = sums[:, :, chans : chans + 3]

time: 78.5 us -> 76.5 us (0.975)
  local copies, waits for them, and re-layouts: 8.14 us -> 6.76 us
    broadcast_in_dim x2 -> x0, local copies, waits for them, and re-layouts: 2.06 us -> none  [the longest x1 1.21 us: on_device(): jnp.broadcast_to(kernels_xy.astype(f32).reshape(2, chans, 9).transpose(0,...]
    transpose x2 -> x0, other arithmetic: 1.39 us -> none  [the longest x1 0.7 us: on_device(): kernels_z.astype(f32).transpose(0, 2, 1)[..., None]]
    unnamed x8 -> x7, local copies, waits for them, and re-layouts: 4.32 us -> 4.27 us
where the time goes in v9:
time: 76.5 us; the launch traced here: 76.2 us
  Pallas kernels  68.1 us (89%)
  local copies, waits for them, and re-layouts  6.76 us (9%)
    pallas_call x1, Pallas kernels, on_device(): pl.pallas_call(functools.partial(whole_kernel, axes, groups, factor), out...  68.1 us
    unnamed x7, local copies, waits for them, and re-layouts  4.27 us

profile of v9, /device:TPU:1, one launch (start us, length us, event | category | flops | bytes accessed | tf_op | source)
XLA Modules:
  0.0 76.2 jit_solution(5823277487058110478)
XLA Ops:
  0.6 0.0 copy-start.1
  0.6 0.7 copy-done.1
  1.3 0.7 maximum_convert_fusion
  2.0 0.7 copy.20.kxy_ref
  2.8 68.1 %shard_map.84 = (bf16[96,4,8,128]{3,2,1,0:T(8,128)(2,1)}, f32[2,96,128]{2,1,0:T(8,128)}) custom-call(bf16[96,4,8,128]{3,2,1,0:T(8,128)(2,1)} %bitcast.8, bf16[96,4,8,128]{3,2,1,0:T(8,128)(2,1)} %bitcast.9, f32[2,96,12]{2,1,0:T(8,128)} %copy.20.kxy_ref, bf16[2,96,96]{2,1,0:T(8,128)(2,1)} %w_ref.1), custom_call_target="tpu_custom_call" | custom-call | tf_op jit(solution)/shard_map/pallas_call | solution.py:312
  70.9 1.0 %slice.11 = f32[2,96,3]{2,1,0:T(8,128)S(1)} slice(f32[2,96,128]{2,1,0:T(8,128)} %get-tuple-element.7), slice={[0:2], [0:96], [96:99]} | slice | bytes 4608 | tf_op jit(solution)/shard_map/slice | solution.py:343
  71.9 0.0 copy-start
  71.9 0.7 copy.22
  72.5 0.2 copy-done
  72.8 0.1 slice.10
  72.8 0.7 copy.21
  73.5 2.1 %copy.25 = bf16[1,96,4,8,128]{4,3,2,1,0:T(8,128)(2,1)} copy(bf16[1,96,4,8,128]{4,3,2,1,0:T(8,128)(2,1)} %bitcast.7) | data formatting | bytes 1572864
  75.6 0.6 copy.26
Async XLA Ops:
  0.6 0.7 copy-start.1
  71.9 0.9 %copy-start = (f32[2,96,128]{2,1,0:T(8,128)S(1)}, f32[2,96,128]{2,1,0:T(8,128)}, u32[]{:S(2)}) copy-start(f32[2,96,128]{2,1,0:T(8,128)} %get-tuple-element.7) | copy-start | bytes 294916

commit v10 on v9

--- a/solution.py
+++ b/solution.py
@@ -57,13 +57,16 @@
 
 def plane_conv(planes, k_ref, b, flip, y):
     lanes = planes[0].shape[1]
+    srcs = [p.astype(jnp.float32) for p in planes]
     total = None
-    for i in range(3):
-        src = planes[i].astype(jnp.float32)
-        for j in range(3):
+    for j in range(3):
+        column = None
+        for i in range(3):
             tap = (2 - i) * 3 + (2 - j) if flip else i * 3 + j
-            term = widen(k_ref[b, :, tap : tap + 1], lanes) * at_y(src, j - 1, y)
-            total = term if total is None else total + term
+            term = widen(k_ref[b, :, tap : tap + 1], lanes) * srcs[i]
+            column = term if column is None else column + term
+        column = at_y(column, j - 1, y)
+        total = column if total is None else total + column
     return total
 
 
@@ -89,10 +92,11 @@
     for t in range(3):
         kzg_ref[b, t] += fold(gax * at_z(pl, t - 1, z))
     gplf = gpl.astype(jnp.float32)
-    for i in range(3):
-        src = around[i].astype(jnp.float32)
-        for j in range(3):
-            kxyg_ref[b, i * 3 + j] += fold(gplf * at_y(src, j - 1, y))
+    srcs = [a.astype(jnp.float32) for a in around]
+    for j in range(3):
+        shifted = at_y(gplf, 1 - j, y)
+        for i in range(3):
+            kxyg_ref[b, i * 3 + j] += fold(shifted * srcs[i])
 
 
 def whole_kernel(axes, groups, factor, vol_hbm, cot_hbm, kxy_ref, w_ref,

time: 76.5 us -> 74.9 us (0.979)
  Pallas kernels: 68.1 us -> 66.5 us
    pallas_call x1, Pallas kernels: 68.1 us -> 66.5 us  [on_device(): pl.pallas_call(functools.partial(whole_kernel, axes, groups, factor), out...]
where the time goes in v10:
time: 74.9 us; the launch traced here: 74.6 us
  Pallas kernels  66.5 us (89%)
  local copies, waits for them, and re-layouts  6.76 us (9%)
    pallas_call x1, Pallas kernels, on_device(): pl.pallas_call(functools.partial(whole_kernel, axes, groups, factor), out...  66.5 us
    unnamed x7, local copies, waits for them, and re-layouts  4.27 us

profile of v10, /device:TPU:1, one launch (start us, length us, event | category | flops | bytes accessed | tf_op | source)
XLA Modules:
  0.0 74.6 jit_solution(5133356545013449606)
XLA Ops:
  0.6 0.0 copy-start.1
  0.6 0.7 copy-done.1
  1.3 0.7 maximum_convert_fusion
  2.0 0.7 %copy.20.kxy_ref = f32[2,96,12]{2,1,0:T(8,128)} copy(f32[2,96,12]{1,0,2:T(2,128)S(1)} %maximum_convert_fusion) | data formatting | bytes 18432 | tf_op jit(solution)/shard_map/convert_element_type | solution.py:308
  2.8 66.5 %shard_map.84 = (bf16[96,4,8,128]{3,2,1,0:T(8,128)(2,1)}, f32[2,96,128]{2,1,0:T(8,128)}) custom-call(bf16[96,4,8,128]{3,2,1,0:T(8,128)(2,1)} %bitcast.8, bf16[96,4,8,128]{3,2,1,0:T(8,128)(2,1)} %bitcast.9, f32[2,96,12]{2,1,0:T(8,128)} %copy.20.kxy_ref, bf16[2,96,96]{2,1,0:T(8,128)(2,1)} %w_ref.1), custom_call_target="tpu_custom_call" | custom-call | tf_op jit(solution)/shard_map/pallas_call | solution.py:316
  69.3 1.0 %slice.11 = f32[2,96,3]{2,1,0:T(8,128)S(1)} slice(f32[2,96,128]{2,1,0:T(8,128)} %get-tuple-element.7), slice={[0:2], [0:96], [96:99]} | slice | bytes 4608 | tf_op jit(solution)/shard_map/slice | solution.py:347
  70.3 0.0 copy-start
  70.3 0.7 copy.22
  70.9 0.2 copy-done
  71.2 0.1 slice.10
  71.2 0.7 copy.21
  71.9 2.1 %copy.25 = bf16[1,96,4,8,128]{4,3,2,1,0:T(8,128)(2,1)} copy(bf16[1,96,4,8,128]{4,3,2,1,0:T(8,128)(2,1)} %bitcast.7) | data formatting | bytes 1572864
  74.0 0.6 copy.26
Async XLA Ops:
  0.6 0.7 copy-start.1
  70.3 0.9 %copy-start = (f32[2,96,128]{2,1,0:T(8,128)S(1)}, f32[2,96,128]{2,1,0:T(8,128)}, u32[]{:S(2)}) copy-start(f32[2,96,128]{2,1,0:T(8,128)} %get-tuple-element.7) | copy-start | bytes 294916

commit v11 on v10

--- a/solution.py
+++ b/solution.py
@@ -102,7 +102,7 @@
 def whole_kernel(axes, groups, factor, vol_hbm, cot_hbm, kxy_ref, w_ref,
                  vg_hbm, sums_ref,
                  wide, cot_ref, vg_ref, h2, pl1, ax1, pre1, gp2, gp1, pay, mix_ref, kzg_ref, kxyg_ref, recv, acc,
-                 in_send, in_recv, g_send, g_recv, e_send, e_recv, send_sem, recv_sem):
+                 in_send, in_recv, g_send, g_recv, e_send, e_recv, h_send, h_recv, send_sem, recv_sem):
     own = cot_ref.shape[0]
     depth = vol_hbm.shape[2]
     kz_ref = kxy_ref
@@ -147,7 +147,7 @@
     def _():
         pl.semaphore_signal(barrier, inc=1, device_id=right, device_id_type=MESH)
 
-    to_planes(vol_hbm, wide, 2)
+    to_planes(vol_hbm, wide, 1)
     to_planes(cot_hbm, cot_ref, 0)
     pl.semaphore_wait(barrier, count + extra_left.astype(jnp.int32) + extra_right.astype(jnp.int32))
 
@@ -186,7 +186,7 @@
     kzg_ref[...] = jnp.zeros_like(kzg_ref)
     kxyg_ref[...] = jnp.zeros_like(kxyg_ref)
 
-    finish_in, drain_in = exchange(wide, 2, 2, in_send, in_recv, wide, 2)
+    finish_in, drain_in = exchange(wide, 1, 1, in_send, in_recv, wide, 1)
 
     def forward1(p):
         planar = plane_conv([wide[p + i] for i in range(3)], kxy_ref, 0, False, y)
@@ -195,9 +195,7 @@
         pl1[p] = planar
         ax1[p] = axial
         pre1[p] = pre
-        spot = sp * own - 1 + p
-        inside = ((spot >= 0) & (spot < own * (last + 1))).astype(jnp.float32)
-        h2[p] = (pre * sigmoid(pre) * inside).astype(jnp.bfloat16)
+        h2[p + 1] = (pre * sigmoid(pre)).astype(jnp.bfloat16)
 
     def block2(q):
         around = [h2[q + i] for i in range(3)]
@@ -212,12 +210,12 @@
 
     def block1(q):
         g1 = plane_conv([gp2[q + i] for i in range(3)], kxy_ref, 1, True, y).astype(jnp.bfloat16)
-        gpre = silu_grad(g1.astype(jnp.float32), pre1[q + 1])
+        gpre = silu_grad(g1.astype(jnp.float32), pre1[q])
         gax = lax.dot_general(w_ref[0], gpre, (((0,), (0,)), ((), ())), preferred_element_type=jnp.float32)
         gpl = depth_conv(gax, kz_ref, 0, True, z).astype(jnp.bfloat16)
         gp1[q + 1] = gpl
-        around = [wide[q + 1 + i] for i in range(3)]
-        weight_grads(0, gpre, ax1[q + 1], gax, pl1[q + 1], gpl, around, mix_ref, kzg_ref, kxyg_ref, y, z)
+        around = [wide[q + i] for i in range(3)]
+        weight_grads(0, gpre, ax1[q], gax, pl1[q], gpl, around, mix_ref, kzg_ref, kxyg_ref, y, z)
 
     def run(body, lo, hi, place=lambda i: i):
         def step(i, carry):
@@ -226,17 +224,20 @@
 
         lax.fori_loop(lo, hi, step, 0)
 
-    run(forward1, 2, own)
+    run(forward1, 1, own - 1)
     finish_in()
-    run(forward1, 0, 4, lambda i: i + (i // 2) * (own - 2))
+    run(forward1, 0, 2, lambda i: i * (own - 1))
+    finish_h, drain_h = exchange(h2, 1, 1, h_send, h_recv, h2, 1)
+    run(block2, 1, own - 1)
+    finish_h()
     run(block2, 0, 2, lambda i: i * (own - 1))
     finish_g, drain_g = exchange(gp2, 1, 1, g_send, g_recv, gp2, 1)
-    run(block2, 1, own - 1)
     run(block1, 1, own - 1)
     finish_g()
     run(block1, 0, 2, lambda i: i * (own - 1))
     finish_e, drain_e = exchange(gp1, 1, 1, e_send, e_recv, gp1, 1)
     drain_in()
+    drain_h()
     drain_g()
 
     lane = lax.broadcasted_iota(jnp.int32, pay.shape[1:], 1)
@@ -322,13 +323,13 @@
         in_specs=[pl.BlockSpec(memory_space=pltpu.VMEM)] * 4,
         out_specs=[pl.BlockSpec(memory_space=pltpu.VMEM)] * 2,
         scratch_shapes=[
-            planes(own + 4, bf16),
+            planes(own + 2, bf16),
             planes(own, bf16),
             planes(own, bf16),
             planes(own + 2, bf16),
-            planes(own + 2, f32),
-            planes(own + 2, bf16),
-            planes(own + 2, f32),
+            planes(own, f32),
+            planes(own, bf16),
+            planes(own, f32),
             planes(own + 2, bf16),
             planes(own + 2, bf16),
             pltpu.VMEM((2, chans, 128), f32),
@@ -337,7 +338,7 @@
             pltpu.VMEM((2, 9, chans, 128), f32),
             pltpu.VMEM((slots, 2, chans, 128), f32),
             pltpu.VMEM((len(groups), 2, chans, 128), f32),
-        ] + [pltpu.SemaphoreType.DMA((2,))] * 6 + [pltpu.SemaphoreType.DMA((slots,))] * 2,
+        ] + [pltpu.SemaphoreType.DMA((2,))] * 8 + [pltpu.SemaphoreType.DMA((slots,))] * 2,
         compiler_params=pltpu.CompilerParams(
             collective_id=0, has_side_effects=True, vmem_limit_bytes=VMEM_LIMIT
         ),

time: 74.9 us -> 73.6 us (0.983)
  Pallas kernels: 66.5 us -> 65.2 us
    pallas_call x1, Pallas kernels: 66.5 us -> 65.2 us  [on_device(): pl.pallas_call(functools.partial(whole_kernel, axes, groups, factor), out...]
where the time goes in v11:
time: 73.6 us; the launch traced here: 73.4 us
  Pallas kernels  65.2 us (89%)
  local copies, waits for them, and re-layouts  6.76 us (9%)
    pallas_call x1, Pallas kernels, on_device(): pl.pallas_call(functools.partial(whole_kernel, axes, groups, factor), out...  65.2 us
    unnamed x7, local copies, waits for them, and re-layouts  4.27 us

profile of v11, /device:TPU:1, one launch (start us, length us, event | category | flops | bytes accessed | tf_op | source)
XLA Modules:
  0.0 73.4 jit_solution(12006268080395586001)
XLA Ops:
  0.6 0.0 copy-start.1
  0.6 0.7 copy-done.1
  1.3 0.7 maximum_convert_fusion
  2.0 0.7 %copy.20.kxy_ref = f32[2,96,12]{2,1,0:T(8,128)} copy(f32[2,96,12]{1,0,2:T(2,128)S(1)} %maximum_convert_fusion) | data formatting | bytes 18432 | tf_op jit(solution)/shard_map/convert_element_type | solution.py:309
  2.8 65.2 %shard_map.84 = (bf16[96,4,8,128]{3,2,1,0:T(8,128)(2,1)}, f32[2,96,128]{2,1,0:T(8,128)}) custom-call(bf16[96,4,8,128]{3,2,1,0:T(8,128)(2,1)} %bitcast.8, bf16[96,4,8,128]{3,2,1,0:T(8,128)(2,1)} %bitcast.9, f32[2,96,12]{2,1,0:T(8,128)} %copy.20.kxy_ref, bf16[2,96,96]{2,1,0:T(8,128)(2,1)} %w_ref.1), custom_call_target="tpu_custom_call" | custom-call | tf_op jit(solution)/shard_map/pallas_call | solution.py:317
  68.0 1.0 %slice.11 = f32[2,96,3]{2,1,0:T(8,128)S(1)} slice(f32[2,96,128]{2,1,0:T(8,128)} %get-tuple-element.7), slice={[0:2], [0:96], [96:99]} | slice | bytes 4608 | tf_op jit(solution)/shard_map/slice | solution.py:348
  69.0 0.0 copy-start
  69.0 0.7 copy.22
  69.7 0.2 copy-done
  69.9 0.1 slice.10
  70.0 0.7 copy.21
  70.7 2.1 %copy.25 = bf16[1,96,4,8,128]{4,3,2,1,0:T(8,128)(2,1)} copy(bf16[1,96,4,8,128]{4,3,2,1,0:T(8,128)(2,1)} %bitcast.7) | data formatting | bytes 1572864
  72.7 0.6 copy.26
Async XLA Ops:
  0.6 0.7 copy-start.1
  69.0 0.9 %copy-start = (f32[2,96,128]{2,1,0:T(8,128)S(1)}, f32[2,96,128]{2,1,0:T(8,128)}, u32[]{:S(2)}) copy-start(f32[2,96,128]{2,1,0:T(8,128)} %get-tuple-element.7) | copy-start | bytes 294916

commit v12 on v11

--- a/solution.py
+++ b/solution.py
@@ -18,6 +18,7 @@
         assert size & (size - 1) == 0
         for b in range(size.bit_length() - 1):
             bits.append((name, 1 << b))
+    bits = bits[1:]
     return [bits[i : i + radix_bits] for i in range(0, len(bits), radix_bits)]
 
 
@@ -102,7 +103,8 @@
 def whole_kernel(axes, groups, factor, vol_hbm, cot_hbm, kxy_ref, w_ref,
                  vg_hbm, sums_ref,
                  wide, cot_ref, vg_ref, h2, pl1, ax1, pre1, gp2, gp1, pay, mix_ref, kzg_ref, kxyg_ref, recv, acc,
-                 in_send, in_recv, g_send, g_recv, e_send, e_recv, h_send, h_recv, send_sem, recv_sem):
+                 in_send, in_recv, g_send, g_recv, e_send, e_recv, h_send, h_recv, sw_send, sw_recv, send_sem, recv_sem,
+                 half_in, acc0, fin):
     own = cot_ref.shape[0]
     depth = vol_hbm.shape[2]
     kz_ref = kxy_ref
@@ -128,12 +130,14 @@
     sp, last, dp = here["sp"], axes[0][1] - 1, here["dp"]
     left, right = (sp - 1, dp), (sp + 1, dp)
     has_left, has_right = sp > 0, sp < last
-    span = 1 << len(groups[0])
-    extra_left = has_left & (sp % span == 0)
-    extra_right = has_right & (sp % span == span - 1)
+    core = sp % 2
+    mate = (sp + 1 - 2 * core, dp)
+    extra_left = has_left & (core == 0)
+    extra_right = has_right & (core == 1)
 
     barrier = pltpu.get_barrier_semaphore()
-    count = 0
+    pl.semaphore_signal(barrier, inc=1, device_id=mate, device_id_type=MESH)
+    count = 1
     for partners in steps:
         for partner in partners:
             pl.semaphore_signal(barrier, inc=1, device_id=partner, device_id_type=MESH)
@@ -261,7 +265,14 @@
 
     order = list(range(1, own - 1)) + [0, own - 1]
     halo_done = False
-    src = pay
+    swap = pltpu.make_async_remote_copy(
+        src_ref=pay.at[1 - core], dst_ref=half_in, send_sem=sw_send.at[0], recv_sem=sw_recv.at[0],
+        device_id=mate, device_id_type=MESH,
+    )
+    swap.start()
+    swap.wait_recv()
+    acc0[...] = pay[core] + half_in[...]
+    src = acc0
     copies = []
     slot = 0
     for g, partners in enumerate(steps):
@@ -289,14 +300,21 @@
         vals = [src[...]] + [recv[slot + k] for k in range(len(partners))]
         while len(vals) > 1:
             vals = [vals[i] + vals[i + 1] for i in range(0, len(vals), 2)]
-        if g == len(steps) - 1:
-            sums_ref[...] = vals[0] * factor
-        else:
-            acc[g] = vals[0]
-            src = acc.at[g]
+        acc[g] = vals[0]
+        src = acc.at[g]
         slot += len(partners)
+    fin[core] = src[...]
+    back = pltpu.make_async_remote_copy(
+        src_ref=fin.at[core], dst_ref=fin.at[core], send_sem=sw_send.at[1], recv_sem=sw_recv.at[1],
+        device_id=mate, device_id_type=MESH,
+    )
+    back.start()
+    back.wait_recv()
+    sums_ref[...] = fin[...] * factor
     for copy in copies:
         copy.wait_send()
+    swap.wait_send()
+    back.wait_send()
     drain_e()
 
 
@@ -336,9 +354,13 @@
             pltpu.VMEM((2, chans, chans), f32),
             pltpu.VMEM((2, 3, chans, 128), f32),
             pltpu.VMEM((2, 9, chans, 128), f32),
-            pltpu.VMEM((slots, 2, chans, 128), f32),
-            pltpu.VMEM((len(groups), 2, chans, 128), f32),
-        ] + [pltpu.SemaphoreType.DMA((2,))] * 8 + [pltpu.SemaphoreType.DMA((slots,))] * 2,
+            pltpu.VMEM((slots, chans, 128), f32),
+            pltpu.VMEM((len(groups), chans, 128), f32),
+        ] + [pltpu.SemaphoreType.DMA((2,))] * 10 + [pltpu.SemaphoreType.DMA((slots,))] * 2 + [
+            pltpu.VMEM((chans, 128), f32),
+            pltpu.VMEM((chans, 128), f32),
+            pltpu.VMEM((2, chans, 128), f32),
+        ],
         compiler_params=pltpu.CompilerParams(
             collective_id=0, has_side_effects=True, vmem_limit_bytes=VMEM_LIMIT
         ),

time: 73.6 us -> 68.6 us (0.932)
  Pallas kernels: 65.2 us -> 60.2 us
    pallas_call x1, Pallas kernels: 65.2 us -> 60.2 us  [on_device(): pl.pallas_call(functools.partial(whole_kernel, axes, groups, factor), out...]
where the time goes in v12:
time: 68.6 us; the launch traced here: 68.3 us
  Pallas kernels  60.2 us (88%)
  local copies, waits for them, and re-layouts  6.76 us (10%)
  other arithmetic  0.69 us (1%)
    pallas_call x1, Pallas kernels, on_device(): pl.pallas_call(functools.partial(whole_kernel, axes, groups, factor), out...  60.2 us
    unnamed x7, local copies, waits for them, and re-layouts  4.27 us

profile of v12, /device:TPU:1, one launch (start us, length us, event | category | flops | bytes accessed | tf_op | source)
XLA Modules:
  0.0 68.3 jit_solution(3353322919079061675)
XLA Ops:
  0.6 0.0 copy-start.1
  0.6 0.7 copy-done.1
  1.3 0.7 %maximum_convert_fusion = f32[2,96,12]{1,0,2:T(2,128)S(1)} fusion(bf16[2,96,3]{1,0,2:T(2,128)(2,1)} %param.8, bf16[2,96,9]{1,0,2:T(2,128)(2,1)S(1)} %bitcast.11), kind=kLoop, calls=%fused_computation | loop fusion | flops 4608 | bytes 13824 | tf_op jit(solution)/shard_map/convert_element_type | solution.py:327
  2.0 0.7 %copy.20.kxy_ref = f32[2,96,12]{2,1,0:T(8,128)} copy(f32[2,96,12]{1,0,2:T(2,128)S(1)} %maximum_convert_fusion) | data formatting | bytes 18432 | tf_op jit(solution)/shard_map/convert_element_type | solution.py:327
  2.8 60.2 %shard_map.84 = (bf16[96,4,8,128]{3,2,1,0:T(8,128)(2,1)}, f32[2,96,128]{2,1,0:T(8,128)}) custom-call(bf16[96,4,8,128]{3,2,1,0:T(8,128)(2,1)} %bitcast.8, bf16[96,4,8,128]{3,2,1,0:T(8,128)(2,1)} %bitcast.9, f32[2,96,12]{2,1,0:T(8,128)} %copy.20.kxy_ref, bf16[2,96,96]{2,1,0:T(8,128)(2,1)} %w_ref.1), custom_call_target="tpu_custom_call" | custom-call | tf_op jit(solution)/shard_map/pallas_call | solution.py:335
  62.9 1.0 %slice.11 = f32[2,96,3]{2,1,0:T(8,128)S(1)} slice(f32[2,96,128]{2,1,0:T(8,128)} %get-tuple-element.7), slice={[0:2], [0:96], [96:99]} | slice | bytes 4608 | tf_op jit(solution)/shard_map/slice | solution.py:370
  63.9 0.0 copy-start
  63.9 0.7 copy.22
  64.6 0.2 copy-done
  64.8 0.1 slice.10
  64.9 0.7 %copy.21 = f32[2,96,9]{1,0,2:T(2,128)} copy(f32[2,96,9]{2,1,0:T(8,128)S(1)} %slice.10) | data formatting | bytes 13824 | tf_op jit(solution)/shard_map/slice | solution.py:371
  65.6 2.1 %copy.25 = bf16[1,96,4,8,128]{4,3,2,1,0:T(8,128)(2,1)} copy(bf16[1,96,4,8,128]{4,3,2,1,0:T(8,128)(2,1)} %bitcast.7) | data formatting | bytes 1572864
  67.7 0.6 copy.26
Async XLA Ops:
  0.6 0.7 %copy-start.1 = (bf16[2,96,3,3]{1,0,3,2:T(2,128)(2,1)S(1)}, bf16[2,96,3,3]{1,0,3,2:T(2,128)(2,1)}, u32[]{:S(2)}) copy-start(bf16[2,96,3,3]{1,0,3,2:T(2,128)(2,1)} %param.7) | copy-start | bytes 10372
  63.9 0.9 %copy-start = (f32[2,96,128]{2,1,0:T(8,128)S(1)}, f32[2,96,128]{2,1,0:T(8,128)}, u32[]{:S(2)}) copy-start(f32[2,96,128]{2,1,0:T(8,128)} %get-tuple-element.7) | copy-start | bytes 294916

commit v13 on v12

--- a/solution.py
+++ b/solution.py
@@ -270,6 +270,8 @@
         device_id=mate, device_id_type=MESH,
     )
     swap.start()
+    conv_plane(order[0])
+    order = order[1:]
     swap.wait_recv()
     acc0[...] = pay[core] + half_in[...]
     src = acc0
@@ -288,7 +290,7 @@
             )
             copy.start()
             here_copies.append(copy)
-        todo = order[g * own // len(steps) : (g + 1) * own // len(steps)]
+        todo = order[g * len(order) // len(steps) : (g + 1) * len(order) // len(steps)]
         if (0 in todo or own - 1 in todo) and not halo_done:
             finish_e()
             halo_done = True
@@ -329,7 +331,7 @@
     axes = (("sp", ranks), ("dp", lax.axis_size("dp")))
     groups = exchange_groups(axes, 2)
     slots = sum((1 << len(g)) - 1 for g in groups)
-    assert own >= 2 and own % len(groups) == 0 and chans + 12 <= 128
+    assert own >= 3 and chans + 12 <= 128
     factor = 1.0 / math.sqrt(lax.axis_size("dp") * own * ranks * depth * across)
     planes = lambda n, t: pltpu.VMEM((n, chans, lanes), t)
     grad_in, sums = pl.pallas_call(

time: 68.6 us -> 70.6 us (1.029)
  Pallas kernels: 60.2 us -> 62.2 us
    pallas_call x1, Pallas kernels: 60.2 us -> 62.2 us  [on_device(): pl.pallas_call(functools.partial(whole_kernel, axes, groups, factor), out...]
where the time goes in v13:
time: 70.6 us; the launch traced here: 70.3 us
  Pallas kernels  62.2 us (88%)
  local copies, waits for them, and re-layouts  6.76 us (10%)
    pallas_call x1, Pallas kernels, on_device(): pl.pallas_call(functools.partial(whole_kernel, axes, groups, factor), out...  62.2 us
    unnamed x7, local copies, waits for them, and re-layouts  4.27 us

profile of v13, /device:TPU:1, one launch (start us, length us, event | category | flops | bytes accessed | tf_op | source)
XLA Modules:
  0.0 70.3 jit_solution(14944635732234561965)
XLA Ops:
  0.6 0.0 copy-start.1
  0.6 0.7 copy-done.1
  1.3 0.7 maximum_convert_fusion
  2.0 0.7 %copy.20.kxy_ref = f32[2,96,12]{2,1,0:T(8,128)} copy(f32[2,96,12]{1,0,2:T(2,128)S(1)} %maximum_convert_fusion) | data formatting | bytes 18432 | tf_op jit(solution)/shard_map/convert_element_type | solution.py:329
  2.8 62.2 %shard_map.84 = (bf16[96,4,8,128]{3,2,1,0:T(8,128)(2,1)}, f32[2,96,128]{2,1,0:T(8,128)}) custom-call(bf16[96,4,8,128]{3,2,1,0:T(8,128)(2,1)} %bitcast.8, bf16[96,4,8,128]{3,2,1,0:T(8,128)(2,1)} %bitcast.9, f32[2,96,12]{2,1,0:T(8,128)} %copy.20.kxy_ref, bf16[2,96,96]{2,1,0:T(8,128)(2,1)} %w_ref.1), custom_call_target="tpu_custom_call" | custom-call | tf_op jit(solution)/shard_map/pallas_call | solution.py:337
  65.0 1.0 %slice.11 = f32[2,96,3]{2,1,0:T(8,128)S(1)} slice(f32[2,96,128]{2,1,0:T(8,128)} %get-tuple-element.7), slice={[0:2], [0:96], [96:99]} | slice | bytes 4608 | tf_op jit(solution)/shard_map/slice | solution.py:372
  65.9 0.0 copy-start
  66.0 0.7 copy.22
  66.6 0.2 copy-done
  66.8 0.1 slice.10
  66.9 0.7 copy.21
  67.6 2.1 %copy.25 = bf16[1,96,4,8,128]{4,3,2,1,0:T(8,128)(2,1)} copy(bf16[1,96,4,8,128]{4,3,2,1,0:T(8,128)(2,1)} %bitcast.7) | data formatting | bytes 1572864
  69.7 0.6 copy.26
Async XLA Ops:
  0.6 0.7 copy-start.1
  65.9 0.9 %copy-start = (f32[2,96,128]{2,1,0:T(8,128)S(1)}, f32[2,96,128]{2,1,0:T(8,128)}, u32[]{:S(2)}) copy-start(f32[2,96,128]{2,1,0:T(8,128)} %get-tuple-element.7) | copy-start | bytes 294916

commit v14 on v12

--- a/solution.py
+++ b/solution.py
@@ -19,7 +19,13 @@
         for b in range(size.bit_length() - 1):
             bits.append((name, 1 << b))
     bits = bits[1:]
-    return [bits[i : i + radix_bits] for i in range(0, len(bits), radix_bits)]
+    sizes = [2, 1, 2, 2] if len(bits) == 7 else [radix_bits] * len(bits)
+    groups, at = [], 0
+    for size in sizes:
+        if at < len(bits):
+            groups.append(bits[at : at + size])
+            at += size
+    return groups
 
 
 def coords(shape):

time: 68.6 us -> 67.8 us (0.988)
  Pallas kernels: 60.2 us -> 59.4 us
    pallas_call x1, Pallas kernels: 60.2 us -> 59.4 us  [on_device(): pl.pallas_call(functools.partial(whole_kernel, axes, groups, factor), out...]
where the time goes in v14:
time: 67.8 us; the launch traced here: 67.6 us
  Pallas kernels  59.4 us (88%)
  local copies, waits for them, and re-layouts  6.76 us (10%)
  other arithmetic  0.69 us (1%)
  between operations  0.68 us (1%)
    pallas_call x1, Pallas kernels, on_device(): pl.pallas_call(functools.partial(whole_kernel, axes, groups, factor), out...  59.4 us
    unnamed x7, local copies, waits for them, and re-layouts  4.27 us

profile of v14, /device:TPU:1, one launch (start us, length us, event | category | flops | bytes accessed | tf_op | source)
XLA Modules:
  0.0 67.6 jit_solution(6078731150255350175)
XLA Ops:
  0.6 0.0 copy-start.1
  0.6 0.7 %copy-done.1 = bf16[2,96,3,3]{1,0,3,2:T(2,128)(2,1)S(1)} copy-done((bf16[2,96,3,3]{1,0,3,2:T(2,128)(2,1)S(1)}, bf16[2,96,3,3]{1,0,3,2:T(2,128)(2,1)}, u32[]{:S(2)}) %copy-start.1) | copy-done | bytes 3480
  1.3 0.7 %maximum_convert_fusion = f32[2,96,12]{1,0,2:T(2,128)S(1)} fusion(bf16[2,96,3]{1,0,2:T(2,128)(2,1)} %param.8, bf16[2,96,9]{1,0,2:T(2,128)(2,1)S(1)} %bitcast.11), kind=kLoop, calls=%fused_computation | loop fusion | flops 4608 | bytes 13824 | tf_op jit(solution)/shard_map/convert_element_type | solution.py:333
  2.0 0.7 %copy.20.kxy_ref = f32[2,96,12]{2,1,0:T(8,128)} copy(f32[2,96,12]{1,0,2:T(2,128)S(1)} %maximum_convert_fusion) | data formatting | bytes 18432 | tf_op jit(solution)/shard_map/convert_element_type | solution.py:333
  2.8 59.4 %shard_map.84 = (bf16[96,4,8,128]{3,2,1,0:T(8,128)(2,1)}, f32[2,96,128]{2,1,0:T(8,128)}) custom-call(bf16[96,4,8,128]{3,2,1,0:T(8,128)(2,1)} %bitcast.8, bf16[96,4,8,128]{3,2,1,0:T(8,128)(2,1)} %bitcast.9, f32[2,96,12]{2,1,0:T(8,128)} %copy.20.kxy_ref, bf16[2,96,96]{2,1,0:T(8,128)(2,1)} %w_ref.1), custom_call_target="tpu_custom_call" | custom-call | tf_op jit(solution)/shard_map/pallas_call | solution.py:341
  62.2 1.0 %slice.11 = f32[2,96,3]{2,1,0:T(8,128)S(1)} slice(f32[2,96,128]{2,1,0:T(8,128)} %get-tuple-element.7), slice={[0:2], [0:96], [96:99]} | slice | bytes 4608 | tf_op jit(solution)/shard_map/slice | solution.py:376
  63.2 0.0 copy-start
  63.2 0.7 copy.22
  63.8 0.2 copy-done
  64.1 0.1 slice.10
  64.2 0.7 %copy.21 = f32[2,96,9]{1,0,2:T(2,128)} copy(f32[2,96,9]{2,1,0:T(8,128)S(1)} %slice.10) | data formatting | bytes 13824 | tf_op jit(solution)/shard_map/slice | solution.py:377
  64.9 2.1 %copy.25 = bf16[1,96,4,8,128]{4,3,2,1,0:T(8,128)(2,1)} copy(bf16[1,96,4,8,128]{4,3,2,1,0:T(8,128)(2,1)} %bitcast.7) | data formatting | bytes 1572864
  66.9 0.6 copy.26
Async XLA Ops:
  0.6 0.7 %copy-start.1 = (bf16[2,96,3,3]{1,0,3,2:T(2,128)(2,1)S(1)}, bf16[2,96,3,3]{1,0,3,2:T(2,128)(2,1)}, u32[]{:S(2)}) copy-start(bf16[2,96,3,3]{1,0,3,2:T(2,128)(2,1)} %param.7) | copy-start | bytes 10372
  63.2 0.9 %copy-start = (f32[2,96,128]{2,1,0:T(8,128)S(1)}, f32[2,96,128]{2,1,0:T(8,128)}, u32[]{:S(2)}) copy-start(f32[2,96,128]{2,1,0:T(8,128)} %get-tuple-element.7) | copy-start | bytes 294916

commit v15 on v14

--- a/solution.py
+++ b/solution.py
@@ -19,7 +19,7 @@
         for b in range(size.bit_length() - 1):
             bits.append((name, 1 << b))
     bits = bits[1:]
-    sizes = [2, 1, 2, 2] if len(bits) == 7 else [radix_bits] * len(bits)
+    sizes = [1, 2, 2, 2] if len(bits) == 7 else [radix_bits] * len(bits)
     groups, at = [], 0
     for size in sizes:
         if at < len(bits):

time: 67.8 us -> 65.9 us (0.972)
  Pallas kernels: 59.4 us -> 57.5 us
    pallas_call x1, Pallas kernels: 59.4 us -> 57.5 us  [on_device(): pl.pallas_call(functools.partial(whole_kernel, axes, groups, factor), out...]
where the time goes in v15:
time: 65.9 us; the launch traced here: 65.6 us
  Pallas kernels  57.5 us (87%)
  local copies, waits for them, and re-layouts  6.76 us (10%)
  other arithmetic  0.69 us (1%)
  between operations  0.68 us (1%)
    pallas_call x1, Pallas kernels, on_device(): pl.pallas_call(functools.partial(whole_kernel, axes, groups, factor), out...  57.5 us
    unnamed x7, local copies, waits for them, and re-layouts  4.27 us

profile of v15, /device:TPU:1, one launch (start us, length us, event | category | flops | bytes accessed | tf_op | source)
XLA Modules:
  0.0 65.6 jit_solution(13896855485445488890)
XLA Ops:
  0.6 0.0 copy-start.1
  0.6 0.7 %copy-done.1 = bf16[2,96,3,3]{1,0,3,2:T(2,128)(2,1)S(1)} copy-done((bf16[2,96,3,3]{1,0,3,2:T(2,128)(2,1)S(1)}, bf16[2,96,3,3]{1,0,3,2:T(2,128)(2,1)}, u32[]{:S(2)}) %copy-start.1) | copy-done | bytes 3480
  1.3 0.7 %maximum_convert_fusion = f32[2,96,12]{1,0,2:T(2,128)S(1)} fusion(bf16[2,96,3]{1,0,2:T(2,128)(2,1)} %param.8, bf16[2,96,9]{1,0,2:T(2,128)(2,1)S(1)} %bitcast.11), kind=kLoop, calls=%fused_computation | loop fusion | flops 4608 | bytes 13824 | tf_op jit(solution)/shard_map/convert_element_type | solution.py:333
  2.0 0.7 %copy.20.kxy_ref = f32[2,96,12]{2,1,0:T(8,128)} copy(f32[2,96,12]{1,0,2:T(2,128)S(1)} %maximum_convert_fusion) | data formatting | bytes 18432 | tf_op jit(solution)/shard_map/convert_element_type | solution.py:333
  2.8 57.5 %shard_map.84 = (bf16[96,4,8,128]{3,2,1,0:T(8,128)(2,1)}, f32[2,96,128]{2,1,0:T(8,128)}) custom-call(bf16[96,4,8,128]{3,2,1,0:T(8,128)(2,1)} %bitcast.8, bf16[96,4,8,128]{3,2,1,0:T(8,128)(2,1)} %bitcast.9, f32[2,96,12]{2,1,0:T(8,128)} %copy.20.kxy_ref, bf16[2,96,96]{2,1,0:T(8,128)(2,1)} %w_ref.1), custom_call_target="tpu_custom_call" | custom-call | tf_op jit(solution)/shard_map/pallas_call | solution.py:341
  60.2 1.0 %slice.11 = f32[2,96,3]{2,1,0:T(8,128)S(1)} slice(f32[2,96,128]{2,1,0:T(8,128)} %get-tuple-element.7), slice={[0:2], [0:96], [96:99]} | slice | bytes 4608 | tf_op jit(solution)/shard_map/slice | solution.py:376
  61.2 0.0 copy-start
  61.2 0.7 %copy.22 = f32[2,96,3]{1,0,2:T(2,128)} copy(f32[2,96,3]{2,1,0:T(8,128)S(1)} %slice.11) | data formatting | bytes 4608
  61.9 0.2 copy-done
  62.1 0.1 slice.10
  62.2 0.7 %copy.21 = f32[2,96,9]{1,0,2:T(2,128)} copy(f32[2,96,9]{2,1,0:T(8,128)S(1)} %slice.10) | data formatting | bytes 13824 | tf_op jit(solution)/shard_map/slice | solution.py:377
  62.9 2.1 %copy.25 = bf16[1,96,4,8,128]{4,3,2,1,0:T(8,128)(2,1)} copy(bf16[1,96,4,8,128]{4,3,2,1,0:T(8,128)(2,1)} %bitcast.7) | data formatting | bytes 1572864
  65.0 0.6 copy.26
Async XLA Ops:
  0.6 0.7 %copy-start.1 = (bf16[2,96,3,3]{1,0,3,2:T(2,128)(2,1)S(1)}, bf16[2,96,3,3]{1,0,3,2:T(2,128)(2,1)}, u32[]{:S(2)}) copy-start(bf16[2,96,3,3]{1,0,3,2:T(2,128)(2,1)} %param.7) | copy-start | bytes 10372
  61.2 0.9 %copy-start = (f32[2,96,128]{2,1,0:T(8,128)S(1)}, f32[2,96,128]{2,1,0:T(8,128)}, u32[]{:S(2)}) copy-start(f32[2,96,128]{2,1,0:T(8,128)} %get-tuple-element.7) | copy-start | bytes 294916

commit v16 on v15

--- a/solution.py
+++ b/solution.py
@@ -87,8 +87,8 @@
     return total
 
 
-def silu_grad(g, pre):
-    s = sigmoid(pre)
+def silu_grad(g, pre, s=None):
+    s = sigmoid(pre) if s is None else s
     return (g * (s * (1.0 + pre * (1.0 - s)))).astype(jnp.bfloat16)
 
 
@@ -110,7 +110,7 @@
                  vg_hbm, sums_ref,
                  wide, cot_ref, vg_ref, h2, pl1, ax1, pre1, gp2, gp1, pay, mix_ref, kzg_ref, kxyg_ref, recv, acc,
                  in_send, in_recv, g_send, g_recv, e_send, e_recv, h_send, h_recv, sw_send, sw_recv, send_sem, recv_sem,
-                 half_in, acc0, fin):
+                 half_in, acc0, fin, sig1):
     own = cot_ref.shape[0]
     depth = vol_hbm.shape[2]
     kz_ref = kxy_ref
@@ -205,7 +205,9 @@
         pl1[p] = planar
         ax1[p] = axial
         pre1[p] = pre
-        h2[p + 1] = (pre * sigmoid(pre)).astype(jnp.bfloat16)
+        s = sigmoid(pre)
+        sig1[p] = s
+        h2[p + 1] = (pre * s).astype(jnp.bfloat16)
 
     def block2(q):
         around = [h2[q + i] for i in range(3)]
@@ -220,7 +222,7 @@
 
     def block1(q):
         g1 = plane_conv([gp2[q + i] for i in range(3)], kxy_ref, 1, True, y).astype(jnp.bfloat16)
-        gpre = silu_grad(g1.astype(jnp.float32), pre1[q])
+        gpre = silu_grad(g1.astype(jnp.float32), pre1[q], sig1[q])
         gax = lax.dot_general(w_ref[0], gpre, (((0,), (0,)), ((), ())), preferred_element_type=jnp.float32)
         gpl = depth_conv(gax, kz_ref, 0, True, z).astype(jnp.bfloat16)
         gp1[q + 1] = gpl
@@ -366,6 +368,7 @@
             pltpu.VMEM((chans, 128), f32),
             pltpu.VMEM((chans, 128), f32),
             pltpu.VMEM((2, chans, 128), f32),
+            planes(own, f32),
         ],
         compiler_params=pltpu.CompilerParams(
             collective_id=0, has_side_effects=True, vmem_limit_bytes=VMEM_LIMIT

time: 65.9 us -> 65.8 us (level)
  no operation moved by 1% of the time
where the time goes in v16:
time: 65.8 us; the launch traced here: 65.5 us
  Pallas kernels  57.4 us (87%)
  local copies, waits for them, and re-layouts  6.76 us (10%)
  other arithmetic  0.69 us (1%)
  between operations  0.68 us (1%)
    pallas_call x1, Pallas kernels, on_device(): pl.pallas_call(functools.partial(whole_kernel, axes, groups, factor), out...  57.4 us
    unnamed x7, local copies, waits for them, and re-layouts  4.27 us

profile of v16, /device:TPU:1, one launch (start us, length us, event | category | flops | bytes accessed | tf_op | source)
XLA Modules:
  0.0 65.5 jit_solution(7788807065430399925)
XLA Ops:
  0.6 0.0 copy-start.1
  0.6 0.7 %copy-done.1 = bf16[2,96,3,3]{1,0,3,2:T(2,128)(2,1)S(1)} copy-done((bf16[2,96,3,3]{1,0,3,2:T(2,128)(2,1)S(1)}, bf16[2,96,3,3]{1,0,3,2:T(2,128)(2,1)}, u32[]{:S(2)}) %copy-start.1) | copy-done | bytes 3480
  1.3 0.7 %maximum_convert_fusion = f32[2,96,12]{1,0,2:T(2,128)S(1)} fusion(bf16[2,96,3]{1,0,2:T(2,128)(2,1)} %param.8, bf16[2,96,9]{1,0,2:T(2,128)(2,1)S(1)} %bitcast.11), kind=kLoop, calls=%fused_computation | loop fusion | flops 4608 | bytes 13824 | tf_op jit(solution)/shard_map/convert_element_type | solution.py:335
  2.0 0.7 %copy.20.kxy_ref = f32[2,96,12]{2,1,0:T(8,128)} copy(f32[2,96,12]{1,0,2:T(2,128)S(1)} %maximum_convert_fusion) | data formatting | bytes 18432 | tf_op jit(solution)/shard_map/convert_element_type | solution.py:335
  2.8 57.4 %shard_map.84 = (bf16[96,4,8,128]{3,2,1,0:T(8,128)(2,1)}, f32[2,96,128]{2,1,0:T(8,128)}) custom-call(bf16[96,4,8,128]{3,2,1,0:T(8,128)(2,1)} %bitcast.8, bf16[96,4,8,128]{3,2,1,0:T(8,128)(2,1)} %bitcast.9, f32[2,96,12]{2,1,0:T(8,128)} %copy.20.kxy_ref, bf16[2,96,96]{2,1,0:T(8,128)(2,1)} %w_ref.1), custom_call_target="tpu_custom_call" | custom-call | tf_op jit(solution)/shard_map/pallas_call | solution.py:343
  60.2 1.0 %slice.11 = f32[2,96,3]{2,1,0:T(8,128)S(1)} slice(f32[2,96,128]{2,1,0:T(8,128)} %get-tuple-element.7), slice={[0:2], [0:96], [96:99]} | slice | bytes 4608 | tf_op jit(solution)/shard_map/slice | solution.py:379
  61.2 0.0 copy-start
  61.2 0.7 %copy.22 = f32[2,96,3]{1,0,2:T(2,128)} copy(f32[2,96,3]{2,1,0:T(8,128)S(1)} %slice.11) | data formatting | bytes 4608
  61.8 0.2 copy-done
  62.1 0.1 slice.10
  62.2 0.7 %copy.21 = f32[2,96,9]{1,0,2:T(2,128)} copy(f32[2,96,9]{2,1,0:T(8,128)S(1)} %slice.10) | data formatting | bytes 13824 | tf_op jit(solution)/shard_map/slice | solution.py:380
  62.8 2.1 %copy.25 = bf16[1,96,4,8,128]{4,3,2,1,0:T(8,128)(2,1)} copy(bf16[1,96,4,8,128]{4,3,2,1,0:T(8,128)(2,1)} %bitcast.7) | data formatting | bytes 1572864
  64.9 0.6 copy.26
Async XLA Ops:
  0.6 0.7 %copy-start.1 = (bf16[2,96,3,3]{1,0,3,2:T(2,128)(2,1)S(1)}, bf16[2,96,3,3]{1,0,3,2:T(2,128)(2,1)}, u32[]{:S(2)}) copy-start(bf16[2,96,3,3]{1,0,3,2:T(2,128)(2,1)} %param.7) | copy-start | bytes 10372
  61.2 0.9 %copy-start = (f32[2,96,128]{2,1,0:T(8,128)S(1)}, f32[2,96,128]{2,1,0:T(8,128)}, u32[]{:S(2)}) copy-start(f32[2,96,128]{2,1,0:T(8,128)} %get-tuple-element.7) | copy-start | bytes 294916

commit v17 on v16

--- a/solution.py
+++ b/solution.py
@@ -19,13 +19,9 @@
         for b in range(size.bit_length() - 1):
             bits.append((name, 1 << b))
     bits = bits[1:]
-    sizes = [1, 2, 2, 2] if len(bits) == 7 else [radix_bits] * len(bits)
-    groups, at = [], 0
-    for size in sizes:
-        if at < len(bits):
-            groups.append(bits[at : at + size])
-            at += size
-    return groups
+    if len(bits) == 7:
+        return [[bits[i] for i in group] for group in ((1, 2), (3, 4), (0, 5, 6))]
+    return [bits[i : i + radix_bits] for i in range(0, len(bits), radix_bits)]
 
 
 def coords(shape):
@@ -337,7 +333,7 @@
     axes = (("sp", ranks), ("dp", lax.axis_size("dp")))
     groups = exchange_groups(axes, 2)
     slots = sum((1 << len(g)) - 1 for g in groups)
-    assert own >= 2 and own % len(groups) == 0 and chans + 12 <= 128
+    assert own >= 2 and chans + 12 <= 128
     factor = 1.0 / math.sqrt(lax.axis_size("dp") * own * ranks * depth * across)
     planes = lambda n, t: pltpu.VMEM((n, chans, lanes), t)
     grad_in, sums = pl.pallas_call(

time: 65.8 us -> 65.9 us (level)
  no operation moved by 1% of the time
where the time goes in v17:
time: 65.9 us; the launch traced here: 65.7 us
  Pallas kernels  57.5 us (87%)
  local copies, waits for them, and re-layouts  6.76 us (10%)
  other arithmetic  0.69 us (1%)
  between operations  0.68 us (1%)
    pallas_call x1, Pallas kernels, on_device(): pl.pallas_call(functools.partial(whole_kernel, axes, groups, factor), out...  57.5 us
    unnamed x7, local copies, waits for them, and re-layouts  4.27 us

profile of v17, /device:TPU:1, one launch (start us, length us, event | category | flops | bytes accessed | tf_op | source)
XLA Modules:
  0.0 65.7 jit_solution(6961288144462137540)
XLA Ops:
  0.6 0.0 copy-start.1
  0.6 0.7 %copy-done.1 = bf16[2,96,3,3]{1,0,3,2:T(2,128)(2,1)S(1)} copy-done((bf16[2,96,3,3]{1,0,3,2:T(2,128)(2,1)S(1)}, bf16[2,96,3,3]{1,0,3,2:T(2,128)(2,1)}, u32[]{:S(2)}) %copy-start.1) | copy-done | bytes 3480
  1.3 0.7 %maximum_convert_fusion = f32[2,96,12]{1,0,2:T(2,128)S(1)} fusion(bf16[2,96,3]{1,0,2:T(2,128)(2,1)} %param.8, bf16[2,96,9]{1,0,2:T(2,128)(2,1)S(1)} %bitcast.11), kind=kLoop, calls=%fused_computation | loop fusion | flops 4608 | bytes 13824 | tf_op jit(solution)/shard_map/convert_element_type | solution.py:331
  2.0 0.7 %copy.20.kxy_ref = f32[2,96,12]{2,1,0:T(8,128)} copy(f32[2,96,12]{1,0,2:T(2,128)S(1)} %maximum_convert_fusion) | data formatting | bytes 18432 | tf_op jit(solution)/shard_map/convert_element_type | solution.py:331
  2.8 57.5 %shard_map.84 = (bf16[96,4,8,128]{3,2,1,0:T(8,128)(2,1)}, f32[2,96,128]{2,1,0:T(8,128)}) custom-call(bf16[96,4,8,128]{3,2,1,0:T(8,128)(2,1)} %bitcast.8, bf16[96,4,8,128]{3,2,1,0:T(8,128)(2,1)} %bitcast.9, f32[2,96,12]{2,1,0:T(8,128)} %copy.20.kxy_ref, bf16[2,96,96]{2,1,0:T(8,128)(2,1)} %w_ref.1), custom_call_target="tpu_custom_call" | custom-call | tf_op jit(solution)/shard_map/pallas_call | solution.py:339
  60.3 1.0 %slice.11 = f32[2,96,3]{2,1,0:T(8,128)S(1)} slice(f32[2,96,128]{2,1,0:T(8,128)} %get-tuple-element.7), slice={[0:2], [0:96], [96:99]} | slice | bytes 4608 | tf_op jit(solution)/shard_map/slice | solution.py:375
  61.3 0.0 copy-start
  61.3 0.7 %copy.22 = f32[2,96,3]{1,0,2:T(2,128)} copy(f32[2,96,3]{2,1,0:T(8,128)S(1)} %slice.11) | data formatting | bytes 4608
  62.0 0.2 copy-done
  62.2 0.1 slice.10
  62.3 0.7 %copy.21 = f32[2,96,9]{1,0,2:T(2,128)} copy(f32[2,96,9]{2,1,0:T(8,128)S(1)} %slice.10) | data formatting | bytes 13824 | tf_op jit(solution)/shard_map/slice | solution.py:376
  63.0 2.1 %copy.25 = bf16[1,96,4,8,128]{4,3,2,1,0:T(8,128)(2,1)} copy(bf16[1,96,4,8,128]{4,3,2,1,0:T(8,128)(2,1)} %bitcast.7) | data formatting | bytes 1572864
  65.0 0.6 copy.26
Async XLA Ops:
  0.6 0.7 %copy-start.1 = (bf16[2,96,3,3]{1,0,3,2:T(2,128)(2,1)S(1)}, bf16[2,96,3,3]{1,0,3,2:T(2,128)(2,1)}, u32[]{:S(2)}) copy-start(bf16[2,96,3,3]{1,0,3,2:T(2,128)(2,1)} %param.7) | copy-start | bytes 10372
  61.3 0.9 %copy-start = (f32[2,96,128]{2,1,0:T(8,128)S(1)}, f32[2,96,128]{2,1,0:T(8,128)}, u32[]{:S(2)}) copy-start(f32[2,96,128]{2,1,0:T(8,128)} %get-tuple-element.7) | copy-start | bytes 294916

commit v18 on v17

--- a/solution.py
+++ b/solution.py
@@ -155,6 +155,9 @@
 
     to_planes(vol_hbm, wide, 1)
     to_planes(cot_hbm, cot_ref, 0)
+    mix_ref[...] = jnp.zeros_like(mix_ref)
+    kzg_ref[...] = jnp.zeros_like(kzg_ref)
+    kxyg_ref[...] = jnp.zeros_like(kxyg_ref)
     pl.semaphore_wait(barrier, count + extra_left.astype(jnp.int32) + extra_right.astype(jnp.int32))
 
     def exchange(buf, first, count, send, recv, src, src_first):
@@ -188,9 +191,6 @@
 
         return finish, drain
 
-    mix_ref[...] = jnp.zeros_like(mix_ref)
-    kzg_ref[...] = jnp.zeros_like(kzg_ref)
-    kxyg_ref[...] = jnp.zeros_like(kxyg_ref)
 
     finish_in, drain_in = exchange(wide, 1, 1, in_send, in_recv, wide, 1)
 

time: 65.9 us -> 65.9 us (level)
  no operation moved by 1% of the time
where the time goes in v18:
time: 65.9 us; the launch traced here: 65.6 us
  Pallas kernels  57.5 us (87%)
  local copies, waits for them, and re-layouts  6.76 us (10%)
  other arithmetic  0.69 us (1%)
  between operations  0.68 us (1%)
    pallas_call x1, Pallas kernels, on_device(): pl.pallas_call(functools.partial(whole_kernel, axes, groups, factor), out...  57.5 us
    unnamed x7, local copies, waits for them, and re-layouts  4.27 us

profile of v18, /device:TPU:1, one launch (start us, length us, event | category | flops | bytes accessed | tf_op | source)
XLA Modules:
  0.0 65.6 jit_solution(18288562375798041450)
XLA Ops:
  0.6 0.0 copy-start.1
  0.6 0.7 %copy-done.1 = bf16[2,96,3,3]{1,0,3,2:T(2,128)(2,1)S(1)} copy-done((bf16[2,96,3,3]{1,0,3,2:T(2,128)(2,1)S(1)}, bf16[2,96,3,3]{1,0,3,2:T(2,128)(2,1)}, u32[]{:S(2)}) %copy-start.1) | copy-done | bytes 3480
  1.3 0.7 %maximum_convert_fusion = f32[2,96,12]{1,0,2:T(2,128)S(1)} fusion(bf16[2,96,3]{1,0,2:T(2,128)(2,1)} %param.8, bf16[2,96,9]{1,0,2:T(2,128)(2,1)S(1)} %bitcast.11), kind=kLoop, calls=%fused_computation | loop fusion | flops 4608 | bytes 13824 | tf_op jit(solution)/shard_map/convert_element_type | solution.py:331
  2.0 0.7 %copy.20.kxy_ref = f32[2,96,12]{2,1,0:T(8,128)} copy(f32[2,96,12]{1,0,2:T(2,128)S(1)} %maximum_convert_fusion) | data formatting | bytes 18432 | tf_op jit(solution)/shard_map/convert_element_type | solution.py:331
  2.8 57.5 %shard_map.84 = (bf16[96,4,8,128]{3,2,1,0:T(8,128)(2,1)}, f32[2,96,128]{2,1,0:T(8,128)}) custom-call(bf16[96,4,8,128]{3,2,1,0:T(8,128)(2,1)} %bitcast.8, bf16[96,4,8,128]{3,2,1,0:T(8,128)(2,1)} %bitcast.9, f32[2,96,12]{2,1,0:T(8,128)} %copy.20.kxy_ref, bf16[2,96,96]{2,1,0:T(8,128)(2,1)} %w_ref.1), custom_call_target="tpu_custom_call" | custom-call | tf_op jit(solution)/shard_map/pallas_call | solution.py:339
  60.2 1.0 %slice.11 = f32[2,96,3]{2,1,0:T(8,128)S(1)} slice(f32[2,96,128]{2,1,0:T(8,128)} %get-tuple-element.7), slice={[0:2], [0:96], [96:99]} | slice | bytes 4608 | tf_op jit(solution)/shard_map/slice | solution.py:375
  61.2 0.0 copy-start
  61.2 0.7 %copy.22 = f32[2,96,3]{1,0,2:T(2,128)} copy(f32[2,96,3]{2,1,0:T(8,128)S(1)} %slice.11) | data formatting | bytes 4608
  61.9 0.2 copy-done
  62.1 0.1 slice.10
  62.2 0.7 %copy.21 = f32[2,96,9]{1,0,2:T(2,128)} copy(f32[2,96,9]{2,1,0:T(8,128)S(1)} %slice.10) | data formatting | bytes 13824 | tf_op jit(solution)/shard_map/slice | solution.py:376
  62.9 2.1 %copy.25 = bf16[1,96,4,8,128]{4,3,2,1,0:T(8,128)(2,1)} copy(bf16[1,96,4,8,128]{4,3,2,1,0:T(8,128)(2,1)} %bitcast.7) | data formatting | bytes 1572864
  65.0 0.6 copy.26
Async XLA Ops:
  0.6 0.7 %copy-start.1 = (bf16[2,96,3,3]{1,0,3,2:T(2,128)(2,1)S(1)}, bf16[2,96,3,3]{1,0,3,2:T(2,128)(2,1)}, u32[]{:S(2)}) copy-start(bf16[2,96,3,3]{1,0,3,2:T(2,128)(2,1)} %param.7) | copy-start | bytes 10372
  61.2 0.9 %copy-start = (f32[2,96,128]{2,1,0:T(8,128)S(1)}, f32[2,96,128]{2,1,0:T(8,128)}, u32[]{:S(2)}) copy-start(f32[2,96,128]{2,1,0:T(8,128)} %get-tuple-element.7) | copy-start | bytes 294916
